TPU v7x, 512 devices: a whole 4x8x8 slice. The times are simulated.
512 devices in a mesh: lon: 16 (over x, z_lo), lat: 4 (over z_hi, core), age: 8 (over y).
Axes of the slice: x: 4, y: 8, z: 8 (z_hi: 2, z_lo: 4; z = z_hi * 4 + z_lo), core: 2. Of those that a mesh axis runs over, the one named last changes fastest.
Arguments:
- density: float32 [64, 256, 4096], P('age', 'lat', 'lon'), may hold values from 0.1 to 3
- adjoint_next: float32 [64, 256, 4096], P('age', 'lat', 'lon'), may hold values from -6 to 6
- current_east: float32 [256, 4096], P('lat', 'lon'), may hold values from -0.25 to 0.25
- current_north: float32 [256, 4096], P('lat', 'lon'), may hold values from -0.25 to 0.25
- swim_speed: float32 [64], P('age'), may hold values from 0.3 to 1
- diffusion: float32 [64], P('age'), may hold values from 0.05 to 0.12
- mortality: float32 [64], P('age'), may hold values from 0.1 to 0.6
- cohort_mass: float32 [64], P('age'), may hold values from 0.2 to 2
- selectivity: float32 [8, 64], P(None, 'age'), may hold values from 0 to 1
- effort: float32 [8, 256, 4096], P(None, 'lat', 'lon'), may hold values from 0.01 to 0.5
- catch_mask: int32 [8, 256, 4096], P(None, 'lat', 'lon'), may hold values 0 or 1
- region: int32 [256, 4096], P('lat', 'lon'), may hold values from 0 to 15
- sea_mask: int32 [256, 4096], P('lat', 'lon'), may hold values 0 or 1
- habitat: float32 [256, 4096], P('lat', 'lon'), may hold values from 0.5 to 1
- observed: float32 [8, 16], replicated, may hold values from 0.3 to 3
Outputs:
- grad_density: float32 [64, 256, 4096], P('age', 'lat', 'lon')
All inputs are finite; a program needn't handle non-finite values. No bound on the sum of `catch_mask` or of `sea_mask` on one device may be relied on, other than what follows from the above.
Results may differ from a plain program's by a relative error of at most 0.000096.
Values sent between devices are 32-bit elements; how exact they have to be, the bound alone decides.
No kernel may reach another device: no remote copies, remote signals or barrier semaphores. Data moves between devices by JAX's collectives and lax.ppermute only.
A program may use at most 64 MiB of HBM per device.

v0:
```python
import jax
import jax.numpy as jnp
from jax import lax
from jax.sharding import PartitionSpec as P


def with_halo(block, sides, width):
    for axis, dim in sides:
        count = lax.axis_size(axis)
        forward = [(i, i + 1) for i in range(count - 1)]
        forward.append((count - 1, 0))
        backward = [(target, source) for source, target in forward]
        low = lax.ppermute(
            lax.slice_in_dim(block, block.shape[dim] - width, None, axis=dim), axis, forward
        )
        high = lax.ppermute(lax.slice_in_dim(block, 0, width, axis=dim), axis, backward)
        block = jnp.concatenate([low, block, high], axis=dim)
    return block


def prefix(part, axis, combine, identity, reverse):
    count = lax.axis_size(axis)
    place = lax.axis_index(axis)
    ahead = count - 1 - place if reverse else place
    gathered = lax.all_gather(part, axis)
    state = jnp.zeros_like(part) + jnp.asarray(identity, part.dtype)

    def one(step, state):
        source = count - 1 - step if reverse else step
        return combine(state, lax.dynamic_index_in_dim(gathered, source, 0, False))

    return lax.fori_loop(0, ahead, one, state)


def shifted(x, axis, by):
    size = lax.axis_size(axis)
    pairs = [(i, i + by) for i in range(size) if 0 <= i + by < size]
    return lax.ppermute(x, axis, pairs)


def cropped(array, margin):
    return array[..., margin : array.shape[-2] - margin, margin : array.shape[-1] - margin]


def extended(field, margin):
    widened = with_halo(field, (("lon", 2), ("lat", 1)), margin)
    row_count = widened.shape[1]
    places = lax.broadcasted_iota(jnp.int32, (row_count, 1), 0)
    at_south = lax.axis_index("lat") == 0
    at_north = lax.axis_index("lat") == lax.axis_size("lat") - 1
    outside = at_south & (places < margin) | at_north & (places >= row_count - margin)
    return jnp.where(outside[None], jnp.float32(0.0), widened)


def coeffs(current_east, current_north, swim_speed, diffusion):
    flow_east = swim_speed[:, None, None] * current_east[None]
    flow_north = swim_speed[:, None, None] * current_north[None]
    spread = diffusion[:, None, None]
    to_east = spread + jnp.maximum(-flow_east, 0.0)
    to_west = spread + jnp.maximum(flow_east, 0.0)
    to_north = spread + jnp.maximum(-flow_north, 0.0)
    to_south = spread + jnp.maximum(flow_north, 0.0)
    centre = 1.0 - (to_east + to_west + to_north + to_south)
    return (centre, to_east, to_west, to_north, to_south)


def advance(padded, coefs, sea):
    centre, to_east, to_west, to_north, to_south = coefs
    inside = padded[:, 1:-1, 1:-1]
    result = (
        centre * inside
        + to_east * padded[:, 1:-1, 2:]
        + to_west * padded[:, 1:-1, :-2]
        + to_north * padded[:, 2:, 1:-1]
        + to_south * padded[:, :-2, 1:-1]
    )
    return sea * result


def retreat(padded, coefs):
    centre, to_east, to_west, to_north, to_south = coefs
    result = cropped(centre, 1) * padded[:, 1:-1, 1:-1]
    result = result + (to_east * padded)[:, 1:-1, :-2] + (to_west * padded)[:, 1:-1, 2:]
    result = result + (to_north * padded)[:, :-2, 1:-1] + (to_south * padded)[:, 2:, 1:-1]
    return result


def local(
    density,
    adjoint_next,
    current_east,
    current_north,
    swim_speed,
    diffusion,
    mortality,
    cohort_mass,
    selectivity,
    effort,
    catch_mask,
    region,
    sea_mask,
    habitat,
    observed,
):
    highest = lax.Precision.HIGHEST
    cohort_count = density.shape[0]
    sea_core = sea_mask.astype(jnp.float32)[None]
    stacked = jnp.concatenate([density, current_east[None], current_north[None], sea_core], axis=0)
    widened = extended(stacked, 1)
    coefs_wide = coeffs(widened[cohort_count], widened[cohort_count + 1], swim_speed, diffusion)
    coefs_core = tuple((cropped(part, 1) for part in coefs_wide))
    midway = advance(widened[:cohort_count], coefs_core, sea_core)
    settled = advance(extended(midway, 1), coefs_core, sea_core)

    def combine(earlier, later):
        return earlier + later

    weighted = cohort_mass[:, None, None] * settled
    running = jnp.cumsum(weighted, axis=0)
    local_total = running[-1]
    above = prefix(local_total, "age", combine, jnp.zeros_like(local_total), True)
    older = above[None] + (local_total[None] - running)
    fishing = jnp.einsum("fa,fxy->axy", selectivity, effort, precision=highest)
    total_mort = mortality[:, None, None] + fishing + 0.02 * older
    survive = jnp.exp(-total_mort)
    yield_frac = (1.0 - survive) / total_mort
    landed = cohort_mass[:, None, None] * yield_frac * settled
    reported = effort * catch_mask.astype(jnp.float32)
    by_fleet = jnp.einsum("fa,axy->fxy", selectivity, landed, precision=highest) * reported
    region_count = observed.shape[1]
    onehot = (region[None] == jnp.arange(region_count, dtype=jnp.int32)[:, None, None]).astype(
        jnp.float32
    )
    partial_catch = jnp.einsum("fxy,rxy->fr", by_fleet, onehot, precision=highest)
    cell_count = density.shape[1] * density.shape[2] * lax.axis_size("lat") * lax.axis_size("lon")
    unit = region_count / cell_count
    predicted = lax.psum(partial_catch, ("lon", "lat", "age")) * unit
    misfit = 1.0 - observed / (1.0 + predicted)
    spread_back = jnp.einsum("fr,rxy->fxy", misfit, onehot, precision=highest) * reported
    pull = cohort_mass[:, None, None] * jnp.einsum(
        "fa,fxy->axy", selectivity, spread_back, precision=highest
    )
    incoming = shifted(adjoint_next[0], "age", -1)
    last_shard = lax.axis_index("age") == lax.axis_size("age") - 1
    tail_row = jnp.where(last_shard, adjoint_next[-1], incoming)
    carried = jnp.concatenate([adjoint_next[1:], tail_row[None]], axis=0)
    kept_grad = carried * habitat[None] * survive
    pressure = -kept_grad * settled + pull * settled * (survive - yield_frac) / total_mort
    run_press = jnp.cumsum(pressure, axis=0)
    below = prefix(run_press[-1], "age", combine, jnp.zeros_like(run_press[-1]), False)
    younger = below[None] + run_press - pressure
    adjoint_settled = kept_grad + pull * yield_frac + 0.02 * cohort_mass[:, None, None] * younger
    adjoint_mid = retreat(extended(sea_core * adjoint_settled, 1), coefs_wide)
    grad_density = retreat(extended(sea_core * adjoint_mid, 1), coefs_wide)
    return grad_density


def solution(mesh):
    placed = (
        P("age", "lat", "lon"),
        P("age", "lat", "lon"),
        P("lat", "lon"),
        P("lat", "lon"),
        P("age"),
        P("age"),
        P("age"),
        P("age"),
        P(None, "age"),
        P(None, "lat", "lon"),
        P(None, "lat", "lon"),
        P("lat", "lon"),
        P("lat", "lon"),
        P("lat", "lon"),
        P(),
    )
    return jax.shard_map(
        local, mesh=mesh, in_specs=placed, out_specs=P("age", "lat", "lon"), check_vma=False
    )
```

profile of v0, /device:TPU:1, one launch (start us, length us, event | category | flops | bytes accessed | tf_op | source)
XLA Modules:
  0.0 324.2 jit_solution(18076854717604417773)
XLA Ops:
  4.5 10.6 %collective-permute-start.1 = (f32[11,64,1]{2,0,1:T(8,128)S(1)}, f32[11,64,1]{2,0,1:T(8,128)S(1)}, u32[]{:S(2)}, u32[]{:S(2)}) collective-permute-start(f32[11,64,1]{2,0,1:T(8,128)S(1)} %get-tuple-element.123), channel_id=1, source_target_pairs={{32,0},{64,32},{96,64},{128,96},{160,128},{192,160},{224,192},{256... | collective-permute-start | bytes 8456 | tf_op jit(solution)/shard_map/ppermute | solution.py:16
  19.8 6.0 %collective-permute-done.1 = f32[11,64,1]{2,0,1:T(8,128)S(1)} collective-permute-done((f32[11,64,1]{2,0,1:T(8,128)S(1)}, f32[11,64,1]{2,0,1:T(8,128)S(1)}, u32[]{:S(2)}, u32[]{:S(2)}) %collective-permute-start.1) | collective-permute-done | bytes 2848 | tf_op jit(solution)/shard_map/ppermute | solution.py:16
  25.8 12.2 %collective-permute-done = f32[11,64,1]{2,0,1:T(8,128)S(1)} collective-permute-done((f32[11,64,1]{2,0,1:T(8,128)S(1)}, f32[11,64,1]{2,0,1:T(8,128)S(1)}, u32[]{:S(2)}, u32[]{:S(2)}) %collective-permute-start) | collective-permute-done | bytes 2848 | tf_op jit(solution)/shard_map/ppermute | solution.py:13
  38.0 3.2 collective-permute-start.3
  41.2 8.1 %collective-permute-start.2 = (f32[11,1,258]{2,0,1:T(8,128)S(1)}, f32[11,1,258]{2,0,1:T(8,128)S(1)}, u32[]{:S(2)}, u32[]{:S(2)}) collective-permute-start(f32[11,1,258]{2,0,1:T(8,128)S(1)} %get-tuple-element.112), channel_id=1, source_target_pairs={{0,8},{8,16},{16,24},{24,0},{1,9},{9,17},{17,25},{25,1},{2,10},{10... | collective-permute-start | bytes 34064 | tf_op jit(solution)/shard_map/ppermute | solution.py:13
  53.4 5.2 %collective-permute-start.6 = (f32[8,64,1]{2,0,1:T(8,128)S(1)}, f32[8,64,1]{2,0,1:T(8,128)S(1)}, u32[]{:S(2)}, u32[]{:S(2)}) collective-permute-start(f32[8,64,1]{2,0,1:T(8,128)S(1)} %get-tuple-element.129), channel_id=1, source_target_pairs={{32,0},{64,32},{96,64},{128,96},{160,128},{192,160},{224,192},{256... | collective-permute-start | bytes 6152 | tf_op jit(solution)/shard_map/ppermute | solution.py:16
  61.9 10.2 %collective-permute-done.5 = f32[8,64,1]{2,0,1:T(8,128)S(1)} collective-permute-done((f32[8,64,1]{2,0,1:T(8,128)S(1)}, f32[8,64,1]{2,0,1:T(8,128)S(1)}, u32[]{:S(2)}, u32[]{:S(2)}) %collective-permute-start.5) | collective-permute-done | bytes 2080 | tf_op jit(solution)/shard_map/ppermute | solution.py:13
  72.7 7.1 %collective-permute-start.8 = (f32[8,1,258]{2,0,1:T(8,128)S(1)}, f32[8,1,258]{2,0,1:T(8,128)S(1)}, u32[]{:S(2)}, u32[]{:S(2)}) collective-permute-start(f32[8,1,258]{2,0,1:T(8,128)S(1)} %get-tuple-element.121), channel_id=1, source_target_pairs={{8,0},{16,8},{24,16},{0,24},{9,1},{17,9},{25,17},{1,25},{10,2},{18... | collective-permute-start | bytes 24776 | tf_op jit(solution)/shard_map/ppermute | solution.py:16
  79.8 2.9 collective-permute-start.7
  90.4 2.3 reduce_window_sum.17
  93.8 23.4 %all_gather.6 = f32[8,64,256]{2,1,0:T(8,128)} all-gather(f32[1,64,256]{2,1,0:T(8,128)S(1)} %copy.64), channel_id=1, replica_groups=mesh['lon'=16,'lat'=4,'age'=8] {'age'}, dimensions={0}, use_global_device_ids=true | all-gather | bytes 589824 | tf_op jit(solution)/shard_map/all_gather | solution.py:25
  117.2 6.2 %while.22 = (s32[]{:T(128)}, f32[64,256]{1,0:T(8,128)S(1)}, s32[]{:T(128)}, f32[8,64,256]{2,1,0:T(8,128)}, s32[]{:T(128)}, /*index=5*/s32[]{:T(128)}, s32[]{:T(128)}, s32[]{:T(128)}) while((s32[]{:T(128)}, f32[64,256]{1,0:T(8,128)S(1)}, s32[]{:T(128)}, f32[8,64,256]{2,1,0:T(8,128)}, s32[]{:T(128)}, /*index=5*/s32[]{:T(128)}, s32[]{:T(128)}, ...), condition=%wide.region_2.3_spmd, body=%wide.region_1.2_spmd.sunk | while | flops 16390 | bytes 196751 | solution.py:32
  128.7 99.4 %psum.7 = f32[8,16]{1,0:T(8,128)S(1)} all-reduce(f32[8,16]{1,0:T(8,128)S(1)} %convolution_bitcast_fusion), channel_id=1, replica_groups=mesh['lon'=16,'lat'=4,'age'=8] {'lon','lat','age'}, use_global_device_ids=true, to_apply=%region_3.4 | all-reduce | flops 128 | bytes 1024 | tf_op jit(solution)/shard_map/psum | solution.py:137
  234.3 2.3 reduce_window_sum.18
  237.7 21.4 %all_gather.7 = f32[8,64,256]{2,1,0:T(8,128)} all-gather(f32[1,64,256]{2,1,0:T(8,128)S(1)} %copy.32), channel_id=1, replica_groups=mesh['lon'=16,'lat'=4,'age'=8] {'age'}, dimensions={0}, use_global_device_ids=true | all-gather | bytes 589824 | tf_op jit(solution)/shard_map/all_gather | solution.py:25
  259.1 2.2 add_multiply_fusion
  261.4 5.0 %collective-permute-start.10 = (f32[8,64,1]{2,0,1:T(8,128)S(1)}, f32[8,64,1]{2,0,1:T(8,128)S(1)}, u32[]{:S(2)}, u32[]{:S(2)}) collective-permute-start(f32[8,64,1]{2,0,1:T(8,128)S(1)} %get-tuple-element.127), channel_id=1, source_target_pairs={{32,0},{64,32},{96,64},{128,96},{160,128},{192,160},{224,192},{256... | collective-permute-start | bytes 6152 | tf_op jit(solution)/shard_map/ppermute | solution.py:16
  269.8 9.9 %collective-permute-done.9 = f32[8,64,1]{2,0,1:T(8,128)S(1)} collective-permute-done((f32[8,64,1]{2,0,1:T(8,128)S(1)}, f32[8,64,1]{2,0,1:T(8,128)S(1)}, u32[]{:S(2)}, u32[]{:S(2)}) %collective-permute-start.9) | collective-permute-done | bytes 2080 | tf_op jit(solution)/shard_map/ppermute | solution.py:13
  279.8 7.5 %collective-permute-start.12 = (f32[8,1,258]{2,0,1:T(8,128)S(1)}, f32[8,1,258]{2,0,1:T(8,128)S(1)}, u32[]{:S(2)}, u32[]{:S(2)}) collective-permute-start(f32[8,1,258]{2,0,1:T(8,128)S(1)} %get-tuple-element.119), channel_id=1, source_target_pairs={{8,0},{16,8},{24,16},{0,24},{9,1},{17,9},{25,17},{1,25},{10,2},{18... | collective-permute-start | bytes 24776 | tf_op jit(solution)/shard_map/ppermute | solution.py:16
  287.3 6.0 %collective-permute-start.11 = (f32[8,1,258]{2,0,1:T(8,128)S(1)}, f32[8,1,258]{2,0,1:T(8,128)S(1)}, u32[]{:S(2)}, u32[]{:S(2)}) collective-permute-start(f32[8,1,258]{2,0,1:T(8,128)S(1)} %get-tuple-element.118), channel_id=1, source_target_pairs={{0,8},{8,16},{16,24},{24,0},{1,9},{9,17},{17,25},{25,1},{2,10},{10... | collective-permute-start | bytes 24776 | tf_op jit(solution)/shard_map/ppermute | solution.py:13
  298.2 3.4 %collective-permute-start.13 = (f32[8,64,1]{2,0,1:T(8,128)S(1)}, f32[8,64,1]{2,0,1:T(8,128)S(1)}, u32[]{:S(2)}, u32[]{:S(2)}) collective-permute-start(f32[8,64,1]{2,0,1:T(8,128)S(1)} %get-tuple-element.124), channel_id=1, source_target_pairs={{0,32},{32,64},{64,96},{96,128},{128,160},{160,192},{192,224},{224... | collective-permute-start | bytes 6152 | tf_op jit(solution)/shard_map/ppermute | solution.py:13
  301.6 8.3 %collective-permute-done.14 = f32[8,64,1]{2,0,1:T(8,128)S(1)} collective-permute-done((f32[8,64,1]{2,0,1:T(8,128)S(1)}, f32[8,64,1]{2,0,1:T(8,128)S(1)}, u32[]{:S(2)}, u32[]{:S(2)}) %collective-permute-start.14) | collective-permute-done | bytes 2080 | tf_op jit(solution)/shard_map/ppermute | solution.py:16
  310.0 4.8 %collective-permute-start.16 = (f32[8,1,258]{2,0,1:T(8,128)S(1)}, f32[8,1,258]{2,0,1:T(8,128)S(1)}, u32[]{:S(2)}, u32[]{:S(2)}) collective-permute-start(f32[8,1,258]{2,0,1:T(8,128)S(1)} %get-tuple-element.117), channel_id=1, source_target_pairs={{8,0},{16,8},{24,16},{0,24},{9,1},{17,9},{25,17},{1,25},{10,2},{18... | collective-permute-start | bytes 24776 | tf_op jit(solution)/shard_map/ppermute | solution.py:16
  314.7 5.8 %collective-permute-start.15 = (f32[8,1,258]{2,0,1:T(8,128)S(1)}, f32[8,1,258]{2,0,1:T(8,128)S(1)}, u32[]{:S(2)}, u32[]{:S(2)}) collective-permute-start(f32[8,1,258]{2,0,1:T(8,128)S(1)} %get-tuple-element.116), channel_id=1, source_target_pairs={{0,8},{8,16},{16,24},{24,0},{1,9},{9,17},{17,25},{25,1},{2,10},{10... | collective-permute-start | bytes 24776 | tf_op jit(solution)/shard_map/ppermute | solution.py:13
  (110 shorter events, 56.6 us)
Async XLA Ops:
  0.0 123.4 %copy-start = (f32[8,8]{1,0:T(8,128)S(1)}, f32[8,8]{1,0:T(8,128)}, u32[]{:S(2)}) copy-start(f32[8,8]{1,0:T(8,128)} %param.27) | copy-start | bytes 772
  4.5 21.3 %collective-permute-start.1 = (f32[11,64,1]{2,0,1:T(8,128)S(1)}, f32[11,64,1]{2,0,1:T(8,128)S(1)}, u32[]{:S(2)}, u32[]{:S(2)}) collective-permute-start(f32[11,64,1]{2,0,1:T(8,128)S(1)} %get-tuple-element.123), channel_id=1, source_target_pairs={{32,0},{64,32},{96,64},{128,96},{160,128},{192,160},{224,192},{256... | collective-permute-start | bytes 8456 | tf_op jit(solution)/shard_map/ppermute | solution.py:16
  15.1 22.8 %collective-permute-start = (f32[11,64,1]{2,0,1:T(8,128)S(1)}, f32[11,64,1]{2,0,1:T(8,128)S(1)}, u32[]{:S(2)}, u32[]{:S(2)}) collective-permute-start(f32[11,64,1]{2,0,1:T(8,128)S(1)} %get-tuple-element.122), channel_id=1, source_target_pairs={{0,32},{32,64},{64,96},{96,128},{128,160},{160,192},{192,224},{224... | collective-permute-start | bytes 8456 | tf_op jit(solution)/shard_map/ppermute | solution.py:13
  18.5 212.6 %collective-permute-start.4 = (f32[64,256]{1,0:T(8,128)}, f32[64,256]{1,0:T(8,128)}, u32[]{:S(2)}, u32[]{:S(2)}) collective-permute-start(f32[64,256]{1,0:T(8,128)} %slice_bitcast_fusion), channel_id=1, source_target_pairs={{1,0},{2,1},{3,2},{4,3},{5,4},{6,5},{7,6},{9,8},{10,9},{11,10},{12... | collective-permute-start | bytes 196616 | tf_op jit(solution)/shard_map/ppermute | solution.py:38
  38.0 11.3 %collective-permute-start.3 = (f32[11,1,258]{2,0,1:T(8,128)S(1)}, f32[11,1,258]{2,0,1:T(8,128)S(1)}, u32[]{:S(2)}, u32[]{:S(2)}) collective-permute-start(f32[11,1,258]{2,0,1:T(8,128)S(1)} %get-tuple-element.113), channel_id=1, source_target_pairs={{8,0},{16,8},{24,16},{0,24},{9,1},{17,9},{25,17},{1,25},{10,2},{18... | collective-permute-start | bytes 34064 | tf_op jit(solution)/shard_map/ppermute | solution.py:16
  41.2 9.0 %collective-permute-start.2 = (f32[11,1,258]{2,0,1:T(8,128)S(1)}, f32[11,1,258]{2,0,1:T(8,128)S(1)}, u32[]{:S(2)}, u32[]{:S(2)}) collective-permute-start(f32[11,1,258]{2,0,1:T(8,128)S(1)} %get-tuple-element.112), channel_id=1, source_target_pairs={{0,8},{8,16},{16,24},{24,0},{1,9},{9,17},{17,25},{25,1},{2,10},{10... | collective-permute-start | bytes 34064 | tf_op jit(solution)/shard_map/ppermute | solution.py:13
  53.2 18.8 %copy-start.1 = (f32[8,64,256]{2,0,1:T(8,128)}, f32[8,64,256]{2,0,1:T(8,128)S(1)}, u32[]{:S(2)}) copy-start(f32[8,64,256]{2,0,1:T(8,128)S(1)} %fusion.26) | copy-start | bytes 1572868
  53.2 29.5 %copy-start.18 = (f32[8]{0:T(128)S(1)}, f32[8]{0:T(128)}, u32[]{:S(2)}) copy-start(f32[8]{0:T(128)} %param.26) | copy-start | bytes 100
  53.4 8.5 %collective-permute-start.6 = (f32[8,64,1]{2,0,1:T(8,128)S(1)}, f32[8,64,1]{2,0,1:T(8,128)S(1)}, u32[]{:S(2)}, u32[]{:S(2)}) collective-permute-start(f32[8,64,1]{2,0,1:T(8,128)S(1)} %get-tuple-element.129), channel_id=1, source_target_pairs={{32,0},{64,32},{96,64},{128,96},{160,128},{192,160},{224,192},{256... | collective-permute-start | bytes 6152 | tf_op jit(solution)/shard_map/ppermute | solution.py:16
  58.5 13.5 %collective-permute-start.5 = (f32[8,64,1]{2,0,1:T(8,128)S(1)}, f32[8,64,1]{2,0,1:T(8,128)S(1)}, u32[]{:S(2)}, u32[]{:S(2)}) collective-permute-start(f32[8,64,1]{2,0,1:T(8,128)S(1)} %get-tuple-element.128), channel_id=1, source_target_pairs={{0,32},{32,64},{64,96},{96,128},{128,160},{160,192},{192,224},{224... | collective-permute-start | bytes 6152 | tf_op jit(solution)/shard_map/ppermute | solution.py:13
  61.9 10.2 %copy-start.10 = (f32[8,64,1]{2,0,1:T(8,128)}, f32[8,64,1]{2,0,1:T(8,128)S(1)}, u32[]{:S(2)}) copy-start(f32[8,64,1]{2,0,1:T(8,128)S(1)} %collective-permute-done.6) | copy-start | bytes 6148
  72.7 13.9 %collective-permute-start.8 = (f32[8,1,258]{2,0,1:T(8,128)S(1)}, f32[8,1,258]{2,0,1:T(8,128)S(1)}, u32[]{:S(2)}, u32[]{:S(2)}) collective-permute-start(f32[8,1,258]{2,0,1:T(8,128)S(1)} %get-tuple-element.121), channel_id=1, source_target_pairs={{8,0},{16,8},{24,16},{0,24},{9,1},{17,9},{25,17},{1,25},{10,2},{18... | collective-permute-start | bytes 24776 | tf_op jit(solution)/shard_map/ppermute | solution.py:16
  79.8 6.9 %collective-permute-start.7 = (f32[8,1,258]{2,0,1:T(8,128)S(1)}, f32[8,1,258]{2,0,1:T(8,128)S(1)}, u32[]{:S(2)}, u32[]{:S(2)}) collective-permute-start(f32[8,1,258]{2,0,1:T(8,128)S(1)} %get-tuple-element.120), channel_id=1, source_target_pairs={{0,8},{8,16},{16,24},{24,0},{1,9},{9,17},{17,25},{25,1},{2,10},{10... | collective-permute-start | bytes 24776 | tf_op jit(solution)/shard_map/ppermute | solution.py:13
  90.4 33.0 %copy-start.15 = (f32[8]{0:T(128)S(1)}, f32[8]{0:T(128)}, u32[]{:S(2)}) copy-start(f32[8]{0:T(128)} %param.25) | copy-start | bytes 100
  126.5 101.6 %copy-start.14 = (f32[8,16]{1,0:T(8,128)S(1)}, f32[8,16]{1,0:T(8,128)}, u32[]{:S(2)}) copy-start(f32[8,16]{1,0:T(8,128)} %param.33) | copy-start | bytes 1540
  128.7 103.4 %copy-start.13 = (f32[64,256]{1,0:T(8,128)S(1)}, f32[64,256]{1,0:T(8,128)}, u32[]{:S(2)}) copy-start(f32[64,256]{1,0:T(8,128)} %param.32) | copy-start | bytes 196612
  261.4 8.3 %collective-permute-start.10 = (f32[8,64,1]{2,0,1:T(8,128)S(1)}, f32[8,64,1]{2,0,1:T(8,128)S(1)}, u32[]{:S(2)}, u32[]{:S(2)}) collective-permute-start(f32[8,64,1]{2,0,1:T(8,128)S(1)} %get-tuple-element.127), channel_id=1, source_target_pairs={{32,0},{64,32},{96,64},{128,96},{160,128},{192,160},{224,192},{256... | collective-permute-start | bytes 6152 | tf_op jit(solution)/shard_map/ppermute | solution.py:16
  266.4 13.3 %collective-permute-start.9 = (f32[8,64,1]{2,0,1:T(8,128)S(1)}, f32[8,64,1]{2,0,1:T(8,128)S(1)}, u32[]{:S(2)}, u32[]{:S(2)}) collective-permute-start(f32[8,64,1]{2,0,1:T(8,128)S(1)} %get-tuple-element.126), channel_id=1, source_target_pairs={{0,32},{32,64},{64,96},{96,128},{128,160},{160,192},{192,224},{224... | collective-permute-start | bytes 6152 | tf_op jit(solution)/shard_map/ppermute | solution.py:13
  279.8 13.5 %collective-permute-start.12 = (f32[8,1,258]{2,0,1:T(8,128)S(1)}, f32[8,1,258]{2,0,1:T(8,128)S(1)}, u32[]{:S(2)}, u32[]{:S(2)}) collective-permute-start(f32[8,1,258]{2,0,1:T(8,128)S(1)} %get-tuple-element.119), channel_id=1, source_target_pairs={{8,0},{16,8},{24,16},{0,24},{9,1},{17,9},{25,17},{1,25},{10,2},{18... | collective-permute-start | bytes 24776 | tf_op jit(solution)/shard_map/ppermute | solution.py:16
  287.3 6.8 %collective-permute-start.11 = (f32[8,1,258]{2,0,1:T(8,128)S(1)}, f32[8,1,258]{2,0,1:T(8,128)S(1)}, u32[]{:S(2)}, u32[]{:S(2)}) collective-permute-start(f32[8,1,258]{2,0,1:T(8,128)S(1)} %get-tuple-element.118), channel_id=1, source_target_pairs={{0,8},{8,16},{16,24},{24,0},{1,9},{9,17},{17,25},{25,1},{2,10},{10... | collective-permute-start | bytes 24776 | tf_op jit(solution)/shard_map/ppermute | solution.py:13
  296.3 13.6 %collective-permute-start.14 = (f32[8,64,1]{2,0,1:T(8,128)S(1)}, f32[8,64,1]{2,0,1:T(8,128)S(1)}, u32[]{:S(2)}, u32[]{:S(2)}) collective-permute-start(f32[8,64,1]{2,0,1:T(8,128)S(1)} %get-tuple-element.125), channel_id=1, source_target_pairs={{32,0},{64,32},{96,64},{128,96},{160,128},{192,160},{224,192},{256... | collective-permute-start | bytes 6152 | tf_op jit(solution)/shard_map/ppermute | solution.py:16
  298.2 11.7 %collective-permute-start.13 = (f32[8,64,1]{2,0,1:T(8,128)S(1)}, f32[8,64,1]{2,0,1:T(8,128)S(1)}, u32[]{:S(2)}, u32[]{:S(2)}) collective-permute-start(f32[8,64,1]{2,0,1:T(8,128)S(1)} %get-tuple-element.124), channel_id=1, source_target_pairs={{0,32},{32,64},{64,96},{96,128},{128,160},{160,192},{192,224},{224... | collective-permute-start | bytes 6152 | tf_op jit(solution)/shard_map/ppermute | solution.py:13
  310.0 10.5 %collective-permute-start.16 = (f32[8,1,258]{2,0,1:T(8,128)S(1)}, f32[8,1,258]{2,0,1:T(8,128)S(1)}, u32[]{:S(2)}, u32[]{:S(2)}) collective-permute-start(f32[8,1,258]{2,0,1:T(8,128)S(1)} %get-tuple-element.117), channel_id=1, source_target_pairs={{8,0},{16,8},{24,16},{0,24},{9,1},{17,9},{25,17},{1,25},{10,2},{18... | collective-permute-start | bytes 24776 | tf_op jit(solution)/shard_map/ppermute | solution.py:16
  314.7 6.6 %collective-permute-start.15 = (f32[8,1,258]{2,0,1:T(8,128)S(1)}, f32[8,1,258]{2,0,1:T(8,128)S(1)}, u32[]{:S(2)}, u32[]{:S(2)}) collective-permute-start(f32[8,1,258]{2,0,1:T(8,128)S(1)} %get-tuple-element.116), channel_id=1, source_target_pairs={{0,8},{8,16},{16,24},{24,0},{1,9},{9,17},{17,25},{25,1},{2,10},{10... | collective-permute-start | bytes 24776 | tf_op jit(solution)/shard_map/ppermute | solution.py:13
  (12 other events, 36.0 us)
where the time goes:
time: 330 us; the launch traced here: 324 us
  blocking collectives  144 us (44%)
  starting transfers between devices  78.4 us (24%)
  waiting for transfers between devices  51 us (15%)
  other arithmetic  28.1 us (9%)
  local copies, waits for them, and re-layouts  13.9 us (4%)
  matrix products  7.91 us (2%)
    psum x1, blocking collectives, local(): predicted = lax.psum(partial_catch, ('lon', 'lat', 'age')) * unit  99.4 us
    ppermute x8, starting transfers between devices, with_halo(): lax.ppermute(lax.slice_in_dim(block, 0, width, axis=dim), axis, backward)  45.2 us
    all_gather x2, blocking collectives, prefix(): gathered = lax.all_gather(part, axis)  44.8 us
    ppermute x8, waiting for transfers between devices, with_halo(): lax.ppermute(lax.slice_in_dim(block, block.shape[dim] - width, None, axis...  34.7 us
    ppermute x8, starting transfers between devices, with_halo(): lax.ppermute(lax.slice_in_dim(block, block.shape[dim] - width, None, axis...  31.9 us
    ppermute x8, waiting for transfers between devices, with_halo(): lax.ppermute(lax.slice_in_dim(block, 0, width, axis=dim), axis, backward)  16.2 us
  transfers between devices with their start and end apart: 17, of which 10 were waited for; matrix products, arithmetic and copies ran while one was open for 9% of the time, Pallas kernels for 0%

commit v1 on v0

v1 whole, which is shorter than its diff:
```python
import functools

import jax
import jax.numpy as jnp
from jax import lax
from jax.experimental import pallas as pl
from jax.experimental.pallas import tpu as pltpu
from jax.sharding import PartitionSpec as P

ROWS, COLS = 64, 256
EROWS, ECOLS = ROWS + 8, COLS + 128
LANES = 128
N = 8
WIDE, NARROW = 4, 2
DENSITY, EAST, NORTH, SEA = 0, 32, 36, 40
ADJOINT, EFFORT, MASK, REGION, HABITAT = 44, 60, 76, 92, 94
STRIP = 96
PACKED = 2 * EROWS + 8
F32 = jnp.float32


def every_field(density, adjoint, effort, mask, east, north, region, sea, habitat):
    for c in range(N):
        yield density, c, DENSITY + WIDE * c, WIDE
    yield east, None, EAST, WIDE
    yield north, None, NORTH, WIDE
    yield sea, None, SEA, WIDE
    for c in range(N):
        yield adjoint, c, ADJOINT + NARROW * c, NARROW
    for f in range(N):
        yield effort, f, EFFORT + NARROW * f, NARROW
    for f in range(N):
        yield mask, f, MASK + NARROW * f, NARROW
    yield region, None, REGION, NARROW
    yield habitat, None, HABITAT, NARROW


def part(ref, index, rows, cols):
    block = ref[rows, cols] if index is None else ref[index, rows, cols]
    return block.astype(F32)


def lane_iota(rows):
    return lax.broadcasted_iota(jnp.int32, (rows, LANES), 1)


def turned(block, by):
    by = by % LANES
    return block if by == 0 else pltpu.roll(block, by, 1)


def pack_kernel(*refs):
    inputs, (to_east, to_west, to_north, to_south) = refs[:9], refs[9:]
    lane = lane_iota(ROWS)
    everything = slice(0, ROWS)
    right = jnp.zeros((ROWS, LANES), F32)
    left = jnp.zeros((ROWS, LANES), F32)
    for ref, index, place, width in every_field(*inputs):
        here = (lane >= place) & (lane < place + width)
        right = jnp.where(here, turned(part(ref, index, everything, slice(LANES, COLS)), place + width), right)
        left = jnp.where(here, turned(part(ref, index, everything, slice(0, LANES)), place), left)
        columns = slice(0, COLS)
        to_north[place : place + width, :] = part(ref, index, slice(ROWS - width, ROWS), columns)
        to_south[place : place + width, :] = part(ref, index, slice(0, width), columns)
    to_east[...] = right
    to_west[...] = left


def corner_kernel(north_in, south_in, west_low, west_high, east_low, east_high, to_north, to_south):
    del north_in, south_in
    to_north[...] = jnp.zeros((8, COLS), F32)
    to_south[...] = jnp.zeros((8, COLS), F32)
    to_north[0:4, 0:LANES] = west_high[4:8, :]
    to_north[0:4, LANES:COLS] = east_high[4:8, :]
    to_south[0:4, 0:LANES] = west_low[0:4, :]
    to_south[0:4, LANES:COLS] = east_low[0:4, :]


def spill(total, out, count):
    side_lane = lane_iota(8)
    packed = jnp.zeros((8, LANES), F32)
    for k in range(EROWS // 8):
        side = total[8 * k : 8 * k + 8, COLS:ECOLS]
        here = (side_lane >= 4 * k) & (side_lane < 4 * k + 4)
        packed = jnp.where(here, turned(side, 4 * k + 2), packed)
    first, second = total[:, 0:LANES], total[:, LANES:COLS]

    for slot in range(count):
        out[slot, 0:EROWS, :] = first
        out[slot, EROWS : 2 * EROWS, :] = second
        out[slot, 2 * EROWS : PACKED, :] = packed


def gathered(received, keep, out):
    total = jnp.zeros((PACKED, LANES), F32)
    for slot in range(received.shape[0]):
        total = total + jnp.where(keep(slot), received[slot], 0.0)
    out[:, 0:LANES] = total[0:EROWS]
    out[:, LANES:COLS] = total[EROWS : 2 * EROWS]
    packed = total[2 * EROWS : PACKED]
    side_lane = lane_iota(8)
    here = (side_lane < NARROW) | (side_lane >= LANES - NARROW)
    for k in range(EROWS // 8):
        out[8 * k : 8 * k + 8, COLS:ECOLS] = jnp.where(here, turned(packed, -(4 * k + 2)), 0.0)


def coeffs(east, north, swim, spread):
    flow_east = swim * east
    flow_north = swim * north
    to_east = spread + jnp.maximum(-flow_east, 0.0)
    to_west = spread + jnp.maximum(flow_east, 0.0)
    to_north = spread + jnp.maximum(-flow_north, 0.0)
    to_south = spread + jnp.maximum(flow_north, 0.0)
    centre = 1.0 - (to_east + to_west + to_north + to_south)
    return centre, to_east, to_west, to_north, to_south


def ahead(x, axis):
    return pltpu.roll(x, x.shape[axis] - 1, axis)


def behind(x, axis):
    return pltpu.roll(x, 1, axis)


def advance(u, coefs, sea):
    centre, to_east, to_west, to_north, to_south = coefs
    return sea * (
        centre * u + to_east * ahead(u, 1) + to_west * behind(u, 1) + to_north * ahead(u, 0) + to_south * behind(u, 0)
    )


def retreat(v, coefs):
    centre, to_east, to_west, to_north, to_south = coefs
    return (
        centre * v + behind(to_east * v, 1) + ahead(to_west * v, 1) + behind(to_north * v, 0) + ahead(to_south * v, 0)
    )


def settle_kernel(*refs):
    inputs = refs[:9]
    west_in, east_in, north_in, south_in, swim, spread, mass = refs[9:16]
    settled_out, total_out, tail_out, adjoint_out, effort_out, mask_out, fields_out = refs[16:23]
    density_ext, west, east, total = refs[23:]
    outs = {}
    for c in range(N):
        outs[DENSITY + WIDE * c] = density_ext.at[c]
        outs[ADJOINT + NARROW * c] = adjoint_out.at[c]
        outs[EFFORT + NARROW * c] = effort_out.at[c]
        outs[MASK + NARROW * c] = mask_out.at[c]
    for k, place in enumerate((EAST, NORTH, SEA, REGION, HABITAT)):
        outs[place] = fields_out.at[k]
    west[0:ROWS, :] = west_in[...]
    east[0:ROWS, :] = east_in[...]
    west[ROWS : ROWS + 4, :] = north_in[STRIP : STRIP + 4, 0:LANES]
    east[ROWS : ROWS + 4, :] = north_in[STRIP : STRIP + 4, LANES:COLS]
    west[ROWS + 4 : EROWS, :] = south_in[STRIP : STRIP + 4, 0:LANES]
    east[ROWS + 4 : EROWS, :] = south_in[STRIP : STRIP + 4, LANES:COLS]
    lane = lane_iota(EROWS)
    for ref, index, place, width in every_field(*inputs):
        out = outs[place]
        out[0:ROWS, 0:COLS] = part(ref, index, slice(0, ROWS), slice(0, COLS))
        if width < 4:
            out[ROWS:EROWS, 0:COLS] = jnp.zeros((8, COLS), F32)
        out[ROWS : ROWS + width, 0:COLS] = north_in[place : place + width, :]
        out[EROWS - width : EROWS, 0:COLS] = south_in[place : place + width, :]
        side = jnp.where(lane < width, turned(east[...], -place), 0.0)
        side = jnp.where(lane >= LANES - width, turned(west[...], LANES - width - place), side)
        out[:, COLS:ECOLS] = side
    tail_out[...] = adjoint_out[0]
    total[...] = jnp.zeros((EROWS, ECOLS), F32)

    def cohort(c, carry):
        sea = fields_out[2]
        coefs = coeffs(fields_out[0], fields_out[1], swim[c], spread[c])
        settled = advance(advance(density_ext[c], coefs, sea), coefs, sea)
        settled_out[c] = settled
        total[...] += mass[c] * settled
        return carry

    lax.fori_loop(0, N, cohort, 0)
    spill(total[...], total_out, total_out.shape[0])


def catch_kernel(
    age, received, settled, tail, adjoint, effort, mask, fields, mortality, mass, selectivity,
    kept_out, yield_out, slope_out, catch_out, older, fleets,
):
    shard = age[0]
    last = shard == age[1] - 1
    gathered(received, lambda slot: slot > shard, older)

    def strip(t, carry):
        rows = pl.ds(pl.multiple_of(t * 8, 8), 8)
        harvest = [effort[f, rows, :] for f in range(N)]
        habitat = fields[4, rows, :]
        run = older[rows, :]
        taken = [jnp.zeros((8, COLS), F32) for _ in range(N)]
        for c in reversed(range(N)):
            settled_c = settled[c, rows, :]
            total_mort = mortality[c] + 0.02 * run
            for f in range(N):
                total_mort = total_mort + selectivity[f, c] * harvest[f]
            survive = jnp.exp(-total_mort)
            inverse = 1.0 / total_mort
            yield_frac = (1.0 - survive) * inverse
            if c + 1 < N:
                carried = adjoint[c + 1, rows, :]
            else:
                carried = jnp.where(last, adjoint[c, rows, :], tail[rows, :])
            weighted = mass[c] * settled_c
            kept_out[c, rows, :] = carried * habitat * survive
            yield_out[c, rows, :] = mass[c] * yield_frac
            slope_out[c, rows, :] = weighted * (survive - yield_frac) * inverse
            landed = (weighted * yield_frac)[:, 0:COLS]
            for f in range(N):
                taken[f] = taken[f] + selectivity[f, c] * landed
            run = run + weighted
        for f in range(N):
            fleets[f, rows, :] = taken[f] * (harvest[f] * mask[f, rows, :])[:, 0:COLS]
        return carry

    lax.fori_loop(0, EROWS // 8, strip, 0)
    lane = lane_iota(N)
    fleet = lax.broadcasted_iota(jnp.int32, (N, LANES), 0)

    def one_region(r, table):
        sums = [jnp.zeros((8, LANES), F32) for _ in range(N)]
        for t in range(ROWS // 8):
            for half in range(2):
                rows, cols = slice(8 * t, 8 * t + 8), slice(LANES * half, LANES * half + LANES)
                here = fields[3, rows, cols] == r.astype(F32)
                for f in range(N):
                    sums[f] = sums[f] + jnp.where(here, fleets[f, rows, cols], 0.0)
        for f in range(N):
            column = jnp.sum(sums[f], axis=0, keepdims=True)
            column = jnp.sum(column, axis=1, keepdims=True)
            table = jnp.where((fleet == f) & (lane == r + 16 * f), column, table)
        return table

    table = lax.fori_loop(0, 16, one_region, jnp.zeros((N, LANES), F32))
    row = jnp.sum(table, axis=0, keepdims=True)
    catch_out[...] = jnp.broadcast_to(row, catch_out.shape)


def press_kernel(
    catches, observed, settled, effort, mask, fields, kept, yields, slope, selectivity,
    base_out, press_out, total_out, total, *, unit,
):
    predicted = jnp.sum(catches[...], axis=0, keepdims=True) * unit
    misfit = jnp.broadcast_to(1.0 - observed[...] / (1.0 + predicted), (8, LANES))

    def strip(t, carry):
        rows = pl.ds(pl.multiple_of(t * 8, 8), 8)
        region = fields[3, rows, :].astype(jnp.int32)
        spread_back = []
        for f in range(N):
            picked = [
                jnp.take_along_axis(misfit, region[:, LANES * k : LANES * k + LANES] + 16 * f, axis=1)
                for k in range(ECOLS // LANES)
            ]
            spread_back.append(jnp.concatenate(picked, axis=1) * effort[f, rows, :] * mask[f, rows, :])
        run = jnp.zeros((8, ECOLS), F32)
        for c in range(N):
            pull = selectivity[0, c] * spread_back[0]
            for f in range(1, N):
                pull = pull + selectivity[f, c] * spread_back[f]
            kept_c = kept[c, rows, :]
            pressure = slope[c, rows, :] * pull - kept_c * settled[c, rows, :]
            base_out[c, rows, :] = kept_c + yields[c, rows, :] * pull
            press_out[c, rows, :] = run
            run = run + pressure
        total[rows, :] = run
        return carry

    lax.fori_loop(0, EROWS // 8, strip, 0)
    spill(total[...], total_out, total_out.shape[0])


def retreat_kernel(age, received, base, press, fields, swim, spread, mass, grad_out, younger):
    shard = age[0]
    gathered(received, lambda slot: slot < shard, younger)

    def cohort(c, carry):
        sea = fields[2]
        coefs = coeffs(fields[0], fields[1], swim[c], spread[c])
        settled_bar = base[c] + (0.02 * mass[c]) * (younger[...] + press[c])
        middle_bar = retreat(sea * settled_bar, coefs)
        grad_out[c] = retreat(sea * middle_bar, coefs)[0:ROWS, 0:COLS]
        return carry

    lax.fori_loop(0, N, cohort, 0)


VMEM = pl.BlockSpec(memory_space=pltpu.VMEM)
SMEM = pl.BlockSpec(memory_space=pltpu.SMEM)


def shape(*dims):
    return jax.ShapeDtypeStruct(dims, F32)


def call(kernel, name, in_specs, outs, scratch=()):
    return pl.pallas_call(
        kernel,
        name=name,
        in_specs=in_specs,
        out_specs=[VMEM] * len(outs),
        out_shape=outs,
        scratch_shapes=[pltpu.VMEM(dims, F32) for dims in scratch],
    )


def local(
    density, adjoint_next, current_east, current_north, swim_speed, diffusion, mortality, cohort_mass,
    selectivity, effort, catch_mask, region, sea_mask, habitat, observed,
):
    lons, lats, ages = (lax.axis_size(axis) for axis in ("lon", "lat", "age"))
    devices = lons * lats * ages
    age = jnp.stack([lax.axis_index("age"), jnp.int32(ages)])
    inputs = (density, adjoint_next, effort, catch_mask, current_east, current_north, region, sea_mask, habitat)
    strip_rows = STRIP + 8

    to_east, to_west, to_north, to_south = call(
        pack_kernel,
        "pack",
        [VMEM] * 9,
        [shape(ROWS, LANES), shape(ROWS, LANES), shape(strip_rows, COLS), shape(strip_rows, COLS)],
    )(*inputs)
    from_west = lax.ppermute(to_east, "lon", [(i, (i + 1) % lons) for i in range(lons)])
    from_east = lax.ppermute(to_west, "lon", [((i + 1) % lons, i) for i in range(lons)])
    low = pl.BlockSpec((8, LANES), lambda i: (0, 0))
    high = pl.BlockSpec((8, LANES), lambda i: (ROWS // 8 - 1, 0))
    corner = pl.BlockSpec((8, COLS), lambda i: (STRIP // 8, 0))
    to_north, to_south = pl.pallas_call(
        corner_kernel,
        name="corner",
        grid=(1,),
        in_specs=[pl.BlockSpec(memory_space=pl.ANY)] * 2 + [low, high, low, high],
        out_specs=[corner, corner],
        out_shape=[shape(strip_rows, COLS)] * 2,
        input_output_aliases={0: 0, 1: 1},
    )(to_north, to_south, from_west, from_west, from_east, from_east)
    from_south = lax.ppermute(to_north, "lat", [(i, i + 1) for i in range(lats - 1)])
    from_north = lax.ppermute(to_south, "lat", [(i + 1, i) for i in range(lats - 1)])

    stack = shape(N, EROWS, ECOLS)
    summed = shape(ages, PACKED, LANES)
    extended = (EROWS, ECOLS)
    settled, totals, tail, adjoint_ext, effort_ext, mask_ext, fields = call(
        settle_kernel,
        "settle",
        [VMEM] * 13 + [SMEM] * 3,
        [stack, summed, shape(*extended), stack, stack, stack, shape(5, *extended)],
        [(N, *extended), (EROWS, LANES), (EROWS, LANES), extended],
    )(*inputs, from_west, from_east, from_north, from_south, swim_speed, diffusion, cohort_mass)
    tail = lax.ppermute(tail, "age", [(i + 1, i) for i in range(ages - 1)])
    totals = lax.all_to_all(totals, "age", 0, 0, tiled=True)

    kept, yields, slope, catches = call(
        catch_kernel,
        "catch",
        [SMEM] + [VMEM] * 7 + [SMEM] * 3,
        [stack, stack, stack, shape(devices, LANES)],
        [extended, (N, EROWS, COLS)],
    )(age, totals, settled, tail, adjoint_ext, effort_ext, mask_ext, fields, mortality, cohort_mass, selectivity)
    catches = lax.all_to_all(catches, ("lon", "lat", "age"), 0, 0, tiled=True)

    unit = observed.shape[1] / (ROWS * COLS * lons * lats)
    base, press, totals = call(
        functools.partial(press_kernel, unit=unit),
        "press",
        [VMEM] * 9 + [SMEM],
        [stack, stack, summed],
        [extended],
    )(catches, observed.reshape(1, LANES), settled, effort_ext, mask_ext, fields, kept, yields, slope, selectivity)
    totals = lax.all_to_all(totals, "age", 0, 0, tiled=True)

    (grad,) = call(
        retreat_kernel,
        "retreat",
        [SMEM] + [VMEM] * 4 + [SMEM] * 3,
        [shape(N, ROWS, COLS)],
        [extended],
    )(age, totals, base, press, fields, swim_speed, diffusion, cohort_mass)
    return grad


def solution(mesh):
    placed = (
        P("age", "lat", "lon"),
        P("age", "lat", "lon"),
        P("lat", "lon"),
        P("lat", "lon"),
        P("age"),
        P("age"),
        P("age"),
        P("age"),
        P(None, "age"),
        P(None, "lat", "lon"),
        P(None, "lat", "lon"),
        P("lat", "lon"),
        P("lat", "lon"),
        P("lat", "lon"),
        P(),
    )
    return jax.shard_map(
        local, mesh=mesh, in_specs=placed, out_specs=P("age", "lat", "lon"), check_vma=False
    )
```

time: 330 us -> 136 us (0.41); the launches traced: 324 us -> 135 us
  blocking collectives: 144 us -> 22.9 us
  starting transfers between devices: 78.4 us -> 48.2 us
  Pallas kernels: 0 us -> 29 us
  other arithmetic: 28.1 us -> 0.58 us
  waiting for transfers between devices: 51 us -> 31.3 us
  local copies, waits for them, and re-layouts: 13.9 us -> 3.4 us
  matrix products: 7.91 us -> 0 us
    psum x1 -> x0, blocking collectives: 99.4 us -> none  [local(): predicted = lax.psum(partial_catch, ('lon', 'lat', 'age')) * unit]
    ppermute x17 -> x5, starting transfers between devices: 78.4 us -> 25.5 us  [the longest x1 7.73 us: local(): lax.ppermute(to_west, 'lon', [((i + 1) % lons, i) for i in range(lons)])]
    all_gather x2 -> x0, blocking collectives: 44.8 us -> none  [prefix(): gathered = lax.all_gather(part, axis)]
    ppermute x17 -> x5, waiting for transfers between devices: 51 us -> 13.8 us  [the longest x1 10.5 us: local(): tail = lax.ppermute(tail, 'age', [(i + 1, i) for i in range(ages - 1)])]
    pallas_call x0 -> x6, Pallas kernels: none -> 29 us  [the longest x1 7.56 us: local(): call(catch_kernel, 'catch', [SMEM] + [VMEM] * 7 + [SMEM] * 3, [stack, sta...]
    all_to_all x0 -> x1, blocking collectives: none -> 22.9 us  [local(): totals = lax.all_to_all(totals, 'age', 0, 0, tiled=True)]
    all_to_all x0 -> x2, starting transfers between devices: none -> 22.7 us  [the longest x1 15.7 us: local(): catches = lax.all_to_all(catches, ('lon', 'lat', 'age'), 0, 0, tiled=True)]
    all_to_all x0 -> x2, waiting for transfers between devices: none -> 17.5 us  [the longest x1 16 us: local(): catches = lax.all_to_all(catches, ('lon', 'lat', 'age'), 0, 0, tiled=True)]
  transfers between devices with their start and end apart: 17 -> 7, of which waited for: 10 -> 6; matrix products, arithmetic and copies ran while one was open for 9% -> 1% of each run, Pallas kernels for 0% -> 0%
where the time goes in v1:
time: 136 us; the launch traced here: 135 us
  starting transfers between devices  48.2 us (35%)
  waiting for transfers between devices  31.3 us (23%)
  Pallas kernels  29 us (21%)
  blocking collectives  22.9 us (17%)
  local copies, waits for them, and re-layouts  3.4 us (2%)
    all_to_all x1, blocking collectives, local(): totals = lax.all_to_all(totals, 'age', 0, 0, tiled=True)  22.9 us
    all_to_all x1, waiting for transfers between devices, local(): catches = lax.all_to_all(catches, ('lon', 'lat', 'age'), 0, 0, tiled=True)  16 us
    all_to_all x1, starting transfers between devices, local(): catches = lax.all_to_all(catches, ('lon', 'lat', 'age'), 0, 0, tiled=True)  15.7 us
    ppermute x1, waiting for transfers between devices, local(): tail = lax.ppermute(tail, 'age', [(i + 1, i) for i in range(ages - 1)])  10.5 us
    ppermute x1, starting transfers between devices, local(): lax.ppermute(to_west, 'lon', [((i + 1) % lons, i) for i in range(lons)])  7.73 us
    pallas_call x1, Pallas kernels, local(): call(catch_kernel, 'catch', [SMEM] + [VMEM] * 7 + [SMEM] * 3, [stack, sta...  7.56 us
    all_to_all x1, starting transfers between devices, local(): totals = lax.all_to_all(totals, 'age', 0, 0, tiled=True)  6.96 us
    pallas_call x1, Pallas kernels, local(): call(settle_kernel, 'settle', [VMEM] * 13 + [SMEM] * 3, [stack, summed, s...  6.83 us
  transfers between devices with their start and end apart: 7, of which 6 were waited for; matrix products, arithmetic and copies ran while one was open for 1% of the time, Pallas kernels for 0%

profile of v1, /device:TPU:1, one launch (start us, length us, event | category | flops | bytes accessed | tf_op | source)
XLA Modules:
  0.0 135.5 jit_solution(9488286149587611377)
XLA Ops:
  0.0 2.9 %pack.1 = (f32[64,128]{1,0:T(8,128)}, f32[64,128]{1,0:T(8,128)}, f32[104,256]{1,0:T(8,128)}, f32[104,256]{1,0:T(8,128)}) custom-call(f32[8,64,256]{2,1,0:T(8,128)} %refs_0_.3, f32[8,64,256]{2,1,0:T(8,128)} %refs_1_.3, f32[8,64,256]{2,1,0:T(8,128)} %refs_2_.3, s32[8,64,256]{2,1,0:T(8,128)} %refs_3_.3, f32[64,256]{1,0:T(8,128)} %refs_4_.3, f32[64,256]{1,0:T(8,128)} %refs_5_.3, ...), custom_call_target="tpu_custom_call" | custom-call | tf_op jit(solution)/shard_map/pack/pallas_call | solution.py:324
  2.9 4.8 %collective-permute-start = (f32[64,128]{1,0:T(8,128)}, f32[64,128]{1,0:T(8,128)S(1)}, u32[]{:S(2)}, u32[]{:S(2)}) collective-permute-start(f32[64,128]{1,0:T(8,128)} %get-tuple-element.25), channel_id=1, source_target_pairs={{0,32},{32,64},{64,96},{96,128},{128,160},{160,192},{192,224},{224... | collective-permute-start | bytes 98312 | tf_op jit(solution)/shard_map/ppermute | solution.py:330
  7.8 7.7 %collective-permute-start.1 = (f32[64,128]{1,0:T(8,128)}, f32[64,128]{1,0:T(8,128)S(1)}, u32[]{:S(2)}, u32[]{:S(2)}) collective-permute-start(f32[64,128]{1,0:T(8,128)} %get-tuple-element.26), channel_id=1, source_target_pairs={{32,0},{64,32},{96,64},{128,96},{160,128},{192,160},{224,192},{256... | collective-permute-start | bytes 98312 | tf_op jit(solution)/shard_map/ppermute | solution.py:331
  15.5 1.3 collective-permute-done.1.east_low.east_high.refs_10_
  17.4 1.3 corner.1
  18.7 6.5 %collective-permute-start.2 = (f32[104,256]{1,0:T(8,128)}, f32[104,256]{1,0:T(8,128)S(1)}, u32[]{:S(2)}, u32[]{:S(2)}) collective-permute-start(f32[104,256]{1,0:T(8,128)} %get-tuple-element.29), channel_id=1, source_target_pairs={{8,0},{16,8},{24,16},{9,1},{17,9},{25,17},{10,2},{18,10},{26,18},{... | collective-permute-start | bytes 319496 | tf_op jit(solution)/shard_map/ppermute | solution.py:345
  25.3 5.2 %collective-permute-start.3 = (f32[104,256]{1,0:T(8,128)}, f32[104,256]{1,0:T(8,128)S(1)}, u32[]{:S(2)}, u32[]{:S(2)}) collective-permute-start(f32[104,256]{1,0:T(8,128)} %get-tuple-element.30), channel_id=1, source_target_pairs={{0,8},{8,16},{16,24},{1,9},{9,17},{17,25},{2,10},{10,18},{18,26},{... | collective-permute-start | bytes 319496 | tf_op jit(solution)/shard_map/ppermute | solution.py:344
  30.5 0.7 collective-permute-done.2.refs_11_
  31.1 1.4 collective-permute-done.3.refs_12_
  32.5 0.6 copy-done.6
  33.1 6.8 %settle.1 = (f32[8,72,384]{2,1,0:T(8,128)}, f32[8,152,128]{2,1,0:T(8,128)}, f32[72,384]{1,0:T(8,128)}, f32[8,72,384]{2,1,0:T(8,128)}, f32[8,72,384]{2,1,0:T(8,12...) custom-call(f32[8,64,256]{2,1,0:T(8,128)} %refs_0_.3, f32[8,64,256]{2,1,0:T(8,128)} %refs_1_.3, f32[8,64,256]{2,1,0:T(8,128)} %refs_2_.3, ...), custom_call_target="tpu_custom_call" | custom-call | tf_op jit(solution)/shard_map/settle/pallas_call | solution.py:350
  40.0 7.0 %all-to-all-start = ((f32[8,152,128]{2,1,0:T(8,128)}), f32[8,152,128]{2,1,0:T(8,128)S(1)}, u32[]{:S(2)}, u32[]{:S(2)}) async-start(f32[8,152,128]{2,1,0:T(8,128)} %get-tuple-element.31), calls=%async_computation | async-start | bytes 1245184 | tf_op jit(solution)/shard_map/all_to_all | solution.py:358
  46.9 1.3 collective-permute-start.4
  48.8 10.5 %collective-permute-done.4.tail = f32[72,384]{1,0:T(8,128)S(1)} collective-permute-done((f32[72,384]{1,0:T(8,128)S(1)}, f32[72,384]{1,0:T(8,128)S(1)}, u32[]{:S(2)}, u32[]{:S(2)}) %collective-permute-start.4) | collective-permute-done | bytes 110624 | tf_op jit(solution)/shard_map/ppermute | solution.py:357
  59.3 1.5 %all-to-all-done.received = f32[8,152,128]{2,1,0:T(8,128)S(1)} async-done(((f32[8,152,128]{2,1,0:T(8,128)}), f32[8,152,128]{2,1,0:T(8,128)S(1)}, u32[]{:S(2)}, u32[]{:S(2)}) %all-to-all-start) | async-done | bytes 622624 | tf_op jit(solution)/shard_map/all_to_all | solution.py:358
  60.8 0.8 copy-done
  61.6 7.6 %catch.1 = (f32[8,72,384]{2,1,0:T(8,128)}, f32[8,72,384]{2,1,0:T(8,128)}, f32[8,72,384]{2,1,0:T(8,128)}, f32[512,128]{1,0:T(8,128)}) custom-call(s32[2]{0:T(128)} %pad_add_fusion.age, f32[8,152,128]{2,1,0:T(8,128)} %copy-done, f32[8,72,384]{2,1,0:T(8,128)} %get-tuple-element.32.settled, f32[72,384]{1,0:T(8,128)} %copy-done.4, ...), custom_call_target="tpu_custom_call" | custom-call | tf_op jit(solution)/shard_map/catch/pallas_call | solution.py:360
  69.2 15.7 %all-to-all-start.1 = ((f32[512,1,128]{2,1,0:T(1,128)}), f32[512,1,128]{2,1,0:T(1,128)S(1)}, u32[]{:S(2)}, u32[]{:S(2)}) async-start(f32[512,1,128]{2,1,0:T(1,128)} %bitcast.6), calls=%async_computation.1 | async-start | bytes 524288 | tf_op jit(solution)/shard_map/all_to_all | solution.py:367
  84.9 0.6 reshape.5.observed
  85.5 16.0 %all-to-all-done.1 = f32[512,1,128]{2,1,0:T(1,128)S(1)} async-done(((f32[512,1,128]{2,1,0:T(1,128)}), f32[512,1,128]{2,1,0:T(1,128)S(1)}, u32[]{:S(2)}, u32[]{:S(2)}) %all-to-all-start.1) | async-done | bytes 262176 | tf_op jit(solution)/shard_map/all_to_all | solution.py:367
  101.5 0.7 copy-done.1
  102.2 5.7 %press.1 = (f32[8,72,384]{2,1,0:T(8,128)}, f32[8,72,384]{2,1,0:T(8,128)}, f32[8,152,128]{2,1,0:T(8,128)}) custom-call(f32[512,128]{1,0:T(8,128)} %bitcast.5, f32[1,128]{1,0:T(1,128)} %reshape.5.observed, f32[8,72,384]{2,1,0:T(8,128)} %get-tuple-element.32.settled, f32[8,72,384]{2,1,0:T(8,128)} %get-tuple-element.35.effort, ...), custom_call_target="tpu_custom_call" | custom-call | tf_op jit(solution)/shard_map/press/pallas_call | solution.py:370
  107.9 22.9 %all_to_all.21.received = f32[8,152,128]{2,1,0:T(8,128)} all-to-all(f32[8,152,128]{2,1,0:T(8,128)} %get-tuple-element.42), channel_id=1, replica_groups=mesh['lon'=16,'lat'=4,'age'=8] {'age'}, dimensions={0} | all-to-all | bytes 1245184 | tf_op jit(solution)/shard_map/all_to_all | solution.py:377
  130.8 4.7 %retreat.1 = f32[8,64,256]{2,1,0:T(8,128)} custom-call(s32[2]{0:T(128)} %pad_add_fusion.age, f32[8,152,128]{2,1,0:T(8,128)} %all_to_all.21.received, f32[8,72,384]{2,1,0:T(8,128)} %get-tuple-element.43.base, f32[8,72,384]{2,1,0:T(8,128)} %get-tuple-element.44.press, f32[5,72,384]{2,1,0:T(8,128)} %get-tuple-element.37.fields, f32[8]{0:T(128)} %swim.1, ...), custom_call_target="tpu_custom_call" | custom-call | tf_op jit(solution)/shard_map/retreat/pallas_call | solution.py:379
  (17 shorter events, 1.2 us)
Async XLA Ops:
  2.9 12.6 %collective-permute-start = (f32[64,128]{1,0:T(8,128)}, f32[64,128]{1,0:T(8,128)S(1)}, u32[]{:S(2)}, u32[]{:S(2)}) collective-permute-start(f32[64,128]{1,0:T(8,128)} %get-tuple-element.25), channel_id=1, source_target_pairs={{0,32},{32,64},{64,96},{96,128},{128,160},{160,192},{192,224},{224... | collective-permute-start | bytes 98312 | tf_op jit(solution)/shard_map/ppermute | solution.py:330
  7.8 9.1 %collective-permute-start.1 = (f32[64,128]{1,0:T(8,128)}, f32[64,128]{1,0:T(8,128)S(1)}, u32[]{:S(2)}, u32[]{:S(2)}) collective-permute-start(f32[64,128]{1,0:T(8,128)} %get-tuple-element.26), channel_id=1, source_target_pairs={{32,0},{64,32},{96,64},{128,96},{160,128},{192,160},{224,192},{256... | collective-permute-start | bytes 98312 | tf_op jit(solution)/shard_map/ppermute | solution.py:331
  15.5 1.3 copy-start.2
  16.8 0.6 copy-start.3
  18.7 12.4 %collective-permute-start.2 = (f32[104,256]{1,0:T(8,128)}, f32[104,256]{1,0:T(8,128)S(1)}, u32[]{:S(2)}, u32[]{:S(2)}) collective-permute-start(f32[104,256]{1,0:T(8,128)} %get-tuple-element.29), channel_id=1, source_target_pairs={{8,0},{16,8},{24,16},{9,1},{17,9},{25,17},{10,2},{18,10},{26,18},{... | collective-permute-start | bytes 319496 | tf_op jit(solution)/shard_map/ppermute | solution.py:345
  25.3 7.2 %collective-permute-start.3 = (f32[104,256]{1,0:T(8,128)}, f32[104,256]{1,0:T(8,128)S(1)}, u32[]{:S(2)}, u32[]{:S(2)}) collective-permute-start(f32[104,256]{1,0:T(8,128)} %get-tuple-element.30), channel_id=1, source_target_pairs={{0,8},{8,16},{16,24},{1,9},{9,17},{17,25},{2,10},{10,18},{18,26},{... | collective-permute-start | bytes 319496 | tf_op jit(solution)/shard_map/ppermute | solution.py:344
  31.1 1.4 %copy-start.5 = (f32[104,256]{1,0:T(8,128)}, f32[104,256]{1,0:T(8,128)S(1)}, u32[]{:S(2)}) copy-start(f32[104,256]{1,0:T(8,128)S(1)} %collective-permute-done.2.refs_11_) | copy-start | bytes 319492
  32.5 0.6 copy-start.6
  39.9 7.0 %copy-start.8 = (f32[72,384]{1,0:T(8,128)S(1)}, f32[72,384]{1,0:T(8,128)}, u32[]{:S(2)}) copy-start(f32[72,384]{1,0:T(8,128)} %get-tuple-element.33) | copy-start | bytes 331780
  40.0 20.9 %all-to-all-start = ((f32[8,152,128]{2,1,0:T(8,128)}), f32[8,152,128]{2,1,0:T(8,128)S(1)}, u32[]{:S(2)}, u32[]{:S(2)}) async-start(f32[8,152,128]{2,1,0:T(8,128)} %get-tuple-element.31), calls=%async_computation | async-start | bytes 1245184 | tf_op jit(solution)/shard_map/all_to_all | solution.py:358
  46.9 12.3 %collective-permute-start.4 = (f32[72,384]{1,0:T(8,128)S(1)}, f32[72,384]{1,0:T(8,128)S(1)}, u32[]{:S(2)}, u32[]{:S(2)}) collective-permute-start(f32[72,384]{1,0:T(8,128)S(1)} %copy-done.8), channel_id=1, source_target_pairs={{1,0},{2,1},{3,2},{4,3},{5,4},{6,5},{7,6},{9,8},{10,9},{11,10},{12... | collective-permute-start | bytes 331784 | tf_op jit(solution)/shard_map/ppermute | solution.py:357
  59.3 1.5 %copy-start.4 = (f32[72,384]{1,0:T(8,128)}, f32[72,384]{1,0:T(8,128)S(1)}, u32[]{:S(2)}) copy-start(f32[72,384]{1,0:T(8,128)S(1)} %collective-permute-done.4.tail) | copy-start | bytes 331780
  60.8 0.8 copy-start
  69.2 15.7 %copy-start.7 = (f32[8,16]{1,0:T(8,128)S(1)}, f32[8,16]{1,0:T(8,128)}, u32[]{:S(2)}) copy-start(f32[8,16]{1,0:T(8,128)} %param.29) | copy-start | bytes 1540
  69.2 32.3 %all-to-all-start.1 = ((f32[512,1,128]{2,1,0:T(1,128)}), f32[512,1,128]{2,1,0:T(1,128)S(1)}, u32[]{:S(2)}, u32[]{:S(2)}) async-start(f32[512,1,128]{2,1,0:T(1,128)} %bitcast.6), calls=%async_computation.1 | async-start | bytes 524288 | tf_op jit(solution)/shard_map/all_to_all | solution.py:367
  101.5 0.7 copy-start.1

commit v2 on v1

v2 whole, which is shorter than its diff:
```python
import functools

import jax
import jax.numpy as jnp
from jax import lax
from jax.experimental import pallas as pl
from jax.experimental.pallas import tpu as pltpu
from jax.sharding import PartitionSpec as P

ROWS, COLS = 64, 256
EROWS, ECOLS = ROWS + 8, COLS + 128
LANES = 128
N = 8
WIDE, NARROW = 4, 2
DENSITY, EAST, NORTH, SEA = 0, 32, 36, 40
ADJOINT, EFFORT, MASK, REGION, HABITAT = 44, 60, 76, 92, 94
STRIP = 96
PACKED = 2 * EROWS + 8
F32 = jnp.float32


def every_field(density, adjoint, effort, mask, east, north, region, sea, habitat):
    for c in range(N):
        yield density, c, DENSITY + WIDE * c, WIDE
    yield east, None, EAST, WIDE
    yield north, None, NORTH, WIDE
    yield sea, None, SEA, WIDE
    for c in range(N):
        yield adjoint, c, ADJOINT + NARROW * c, NARROW
    for f in range(N):
        yield effort, f, EFFORT + NARROW * f, NARROW
    for f in range(N):
        yield mask, f, MASK + NARROW * f, NARROW
    yield region, None, REGION, NARROW
    yield habitat, None, HABITAT, NARROW


def part(ref, index, rows, cols):
    block = ref[rows, cols] if index is None else ref[index, rows, cols]
    return block.astype(F32)


def lane_iota(rows):
    return lax.broadcasted_iota(jnp.int32, (rows, LANES), 1)


def turned(block, by):
    by = by % LANES
    return block if by == 0 else pltpu.roll(block, by, 1)


def pack_kernel(*refs):
    inputs, (to_east, to_west, to_north, to_south) = refs[:9], refs[9:]
    lane = lane_iota(ROWS)
    everything = slice(0, ROWS)
    right = jnp.zeros((ROWS, LANES), F32)
    left = jnp.zeros((ROWS, LANES), F32)
    for ref, index, place, width in every_field(*inputs):
        here = (lane >= place) & (lane < place + width)
        right = jnp.where(here, turned(part(ref, index, everything, slice(LANES, COLS)), place + width), right)
        left = jnp.where(here, turned(part(ref, index, everything, slice(0, LANES)), place), left)
        columns = slice(0, COLS)
        to_north[place : place + width, :] = part(ref, index, slice(ROWS - width, ROWS), columns)
        to_south[place : place + width, :] = part(ref, index, slice(0, width), columns)
    to_east[...] = right
    to_west[...] = left


def corner_kernel(north_in, south_in, west, east, to_north, to_south):
    if north_in is not to_north:
        to_north[0:STRIP, :] = north_in[0:STRIP, :]
        to_south[0:STRIP, :] = south_in[0:STRIP, :]
    to_north[STRIP : STRIP + 4, 0:LANES] = west[ROWS - 4 : ROWS, :]
    to_north[STRIP : STRIP + 4, LANES:COLS] = east[ROWS - 4 : ROWS, :]
    to_south[STRIP : STRIP + 4, 0:LANES] = west[0:4, :]
    to_south[STRIP : STRIP + 4, LANES:COLS] = east[0:4, :]
    to_north[STRIP + 4 :, :] = jnp.zeros((4, COLS), F32)
    to_south[STRIP + 4 :, :] = jnp.zeros((4, COLS), F32)


def at_all(out, slots, rows, value):
    for slot in range(slots):
        out[slot, rows, :] = value


def side_of(tile, k):
    return turned(tile, 4 * k + 2)


def packed_side(sides):
    lane = lane_iota(8)
    packed = jnp.zeros((8, LANES), F32)
    for k, side in enumerate(sides):
        packed = jnp.where((lane >= 4 * k) & (lane < 4 * k + 4), side_of(side, k), packed)
    return packed


def pack_into(out, index, x):
    out[index, 0:EROWS, :] = x[:, 0:LANES]
    out[index, EROWS : 2 * EROWS, :] = x[:, LANES:COLS]
    sides = [x[8 * k : 8 * k + 8, COLS:ECOLS] for k in range(EROWS // 8)]
    out[index, 2 * EROWS : PACKED, :] = packed_side(sides)


def unpack_into(out, packed):
    out[:, 0:LANES] = packed[0:EROWS]
    out[:, LANES:COLS] = packed[EROWS : 2 * EROWS]
    side = packed[2 * EROWS : PACKED]
    lane = lane_iota(8)
    here = (lane < NARROW) | (lane >= LANES - NARROW)
    for k in range(EROWS // 8):
        out[8 * k : 8 * k + 8, COLS:ECOLS] = jnp.where(here, turned(side, -(4 * k + 2)), 0.0)


def picked(received, keep):
    total = jnp.zeros((PACKED, LANES), F32)
    for slot in range(received.shape[0]):
        total = total + jnp.where(keep(slot), received[slot], 0.0)
    return total


def ahead(x, axis):
    return pltpu.roll(x, x.shape[axis] - 1, axis)


def behind(x, axis):
    return pltpu.roll(x, 1, axis)


def rates(flow):
    east, north = flow[0], flow[1]
    return jnp.maximum(-east, 0.0), jnp.maximum(east, 0.0), jnp.maximum(-north, 0.0), jnp.maximum(north, 0.0)


def moves(u):
    return ahead(u, 1), behind(u, 1), ahead(u, 0), behind(u, 0)


def spreading(u):
    e, w, n, s = moves(u)
    return ((e + w) + (n + s)) - 4.0 * u


def drifting(u, rate, out_rate):
    e, w, n, s = moves(u)
    return (rate[0] * e + rate[1] * w + rate[2] * n + rate[3] * s) - out_rate * u


def drifting_back(w, rate, out_rate):
    return (
        behind(rate[0] * w, 1) + ahead(rate[1] * w, 1) + behind(rate[2] * w, 0) + ahead(rate[3] * w, 0)
    ) - out_rate * w


def coeffs(flow, swim, spread):
    rate = rates(flow)
    to = [spread + swim * one for one in rate]
    return 1.0 - (to[0] + to[1] + to[2] + to[3]), *to


def advance(u, coefs, sea):
    centre, to_east, to_west, to_north, to_south = coefs
    e, w, n, s = moves(u)
    return sea * (centre * u + to_east * e + to_west * w + to_north * n + to_south * s)


def retreat(v, coefs):
    centre, to_east, to_west, to_north, to_south = coefs
    return (
        centre * v + behind(to_east * v, 1) + ahead(to_west * v, 1) + behind(to_north * v, 0) + ahead(to_south * v, 0)
    )


def strips(west_in, east_in, north_in, south_in, west, east):
    west[0:ROWS, :] = west_in[...]
    east[0:ROWS, :] = east_in[...]
    west[ROWS : ROWS + 4, :] = north_in[STRIP : STRIP + 4, 0:LANES]
    east[ROWS : ROWS + 4, :] = north_in[STRIP : STRIP + 4, LANES:COLS]
    west[ROWS + 4 : EROWS, :] = south_in[STRIP : STRIP + 4, 0:LANES]
    east[ROWS + 4 : EROWS, :] = south_in[STRIP : STRIP + 4, LANES:COLS]


def narrow_field(ref, index, place, west, east, north_in, south_in, out):
    width = NARROW
    core = part(ref, index, slice(0, ROWS), slice(0, COLS))
    for half in range(2):
        cols = slice(LANES * half, LANES * half + LANES)
        top = EROWS * half
        out[top : top + ROWS, :] = core[:, cols]
        out[top + ROWS : top + EROWS, :] = jnp.zeros((8, LANES), F32)
        out[top + ROWS : top + ROWS + width, :] = north_in[place : place + width, cols]
        out[top + EROWS - width : top + EROWS, :] = south_in[place : place + width, cols]
    lane = lane_iota(8)
    packed = jnp.zeros((8, LANES), F32)
    for k in range(EROWS // 8):
        rows = slice(8 * k, 8 * k + 8)
        here = (lane >= 4 * k) & (lane < 4 * k + width)
        packed = jnp.where(here, turned(west[rows, :], 4 * k - place), packed)
        here = (lane >= 4 * k + width) & (lane < 4 * k + 4)
        packed = jnp.where(here, turned(east[rows, :], 4 * k + width - place), packed)
    out[2 * EROWS : PACKED, :] = packed


def total_kernel(
    density, current_east, current_north, sea_mask, adjoint, west_in, east_in, north_in, south_in, swim, spread, mass,
    total_out, tail_out, density_out, flow_out, west, east,
):
    strips(west_in, east_in, north_in, south_in, west, east)
    narrow_field(adjoint, 0, ADJOINT, west, east, north_in, south_in, tail_out)
    lane = lane_iota(EROWS)
    wide = [(density, c, DENSITY + WIDE * c, density_out.at[c]) for c in range(N)]
    wide += [(current_east, None, EAST, flow_out.at[0]), (current_north, None, NORTH, flow_out.at[1])]
    wide += [(sea_mask, None, SEA, flow_out.at[2])]
    for ref, index, place, out in wide:
        out[0:ROWS, 0:COLS] = part(ref, index, slice(0, ROWS), slice(0, COLS))
        out[ROWS : ROWS + WIDE, 0:COLS] = north_in[place : place + WIDE, :]
        out[EROWS - WIDE : EROWS, 0:COLS] = south_in[place : place + WIDE, :]
        side = jnp.where(lane < WIDE, turned(east[...], -place), 0.0)
        side = jnp.where(lane >= LANES - WIDE, turned(west[...], LANES - WIDE - place), side)
        out[:, COLS:ECOLS] = side
    sums = [jnp.zeros((EROWS, ECOLS), F32) for _ in range(6)]
    for c in range(N):
        u, d, s = density_out[c], spread[c], swim[c]
        factors = (mass[c], mass[c] * d, mass[c] * s, mass[c] * d * d, mass[c] * d * s, mass[c] * s * s)
        sums = [total + factor * u for total, factor in zip(sums, factors, strict=True)]
    rate, sea = rates(flow_out), flow_out[2]
    out_rate = (rate[0] + rate[1]) + (rate[2] + rate[3])
    first = [
        sea * (sums[a] + spreading(sums[b]) + drifting(sums[c], rate, out_rate))
        for a, b, c in ((0, 1, 2), (1, 3, 4), (2, 4, 5))
    ]
    total = sea * (first[0] + spreading(first[1]) + drifting(first[2], rate, out_rate))
    slots = total_out.shape[0]
    at_all(total_out, slots, slice(0, EROWS), total[:, 0:LANES])
    at_all(total_out, slots, slice(EROWS, 2 * EROWS), total[:, LANES:COLS])
    sides = [total[8 * k : 8 * k + 8, COLS:ECOLS] for k in range(EROWS // 8)]
    at_all(total_out, slots, slice(2 * EROWS, PACKED), packed_side(sides))


def fleet_kernel(
    adjoint, effort, mask, region, habitat, west_in, east_in, north_in, south_in, density, flow,
    swim, spread, mortality, selectivity,
    settled_out, fishing_out, reported_out, region_out, carried_out, habitat_out, west, east, efforts,
):
    strips(west_in, east_in, north_in, south_in, west, east)

    def narrow(ref, index, place, out):
        narrow_field(ref, index, place, west, east, north_in, south_in, out)

    for k in range(N):
        narrow(adjoint, k, ADJOINT + NARROW * k, carried_out.at[k])
        narrow(effort, k, EFFORT + NARROW * k, efforts.at[k])
        narrow(mask, k, MASK + NARROW * k, reported_out.at[k])
    narrow(region, None, REGION, region_out)
    narrow(habitat, None, HABITAT, habitat_out)

    def tile(t, carry):
        rows = pl.ds(pl.multiple_of(t * 8, 8), 8)
        harvest = [efforts[f, rows, :] for f in range(N)]
        for f in range(N):
            reported_out[f, rows, :] = reported_out[f, rows, :] * harvest[f]
        for c in range(N):
            fishing = mortality[c] + selectivity[0, c] * harvest[0]
            for f in range(1, N):
                fishing = fishing + selectivity[f, c] * harvest[f]
            fishing_out[c, rows, :] = fishing
        return carry

    lax.fori_loop(0, PACKED // 8, tile, 0)

    def cohort(c, carry):
        coefs, sea = coeffs(flow, swim[c], spread[c]), flow[2]
        pack_into(settled_out, c, advance(advance(density[c], coefs, sea), coefs, sea))
        return carry

    lax.fori_loop(0, N, cohort, 0)


def catch_kernel(
    age, received, settled, fishing, reported, region, mass, selectivity, mort_out, catch_out, older, fleets
):
    shard = age[0]
    older[...] = picked(received, lambda slot: slot > shard)

    def pair(t, carry):
        places = [pl.ds(pl.multiple_of(t * 8, 8), 8), pl.ds(pl.multiple_of(EROWS + t * 8, 8), 8)]
        for rows in places:
            run = older[rows, :]
            taken = [jnp.zeros((8, LANES), F32) for _ in range(N)]
            for c in reversed(range(N)):
                total_mort = fishing[c, rows, :] + 0.02 * run
                mort_out[c, rows, :] = total_mort
                weighted = mass[c] * settled[c, rows, :]
                landed = weighted * ((1.0 - jnp.exp(-total_mort)) / total_mort)
                for f in range(N):
                    taken[f] = taken[f] + selectivity[f, c] * landed
                run = run + weighted
            for f in range(N):
                fleets[f, rows, :] = taken[f] * reported[f, rows, :]
        return carry

    lax.fori_loop(0, EROWS // 8, pair, 0)
    rows = slice(2 * EROWS, PACKED)
    run = older[rows, :]
    for c in reversed(range(N)):
        mort_out[c, rows, :] = fishing[c, rows, :] + 0.02 * run
        run = run + mass[c] * settled[c, rows, :]

    lane = lane_iota(N)
    fleet = lax.broadcasted_iota(jnp.int32, (N, LANES), 0)

    def one_region(r, table):
        sums = [jnp.zeros((8, LANES), F32) for _ in range(N)]
        for half in range(2):
            for t in range(ROWS // 8):
                rows = slice(EROWS * half + 8 * t, EROWS * half + 8 * t + 8)
                here = region[rows, :] == r.astype(F32)
                for f in range(N):
                    sums[f] = sums[f] + jnp.where(here, fleets[f, rows, :], 0.0)
        for f in range(N):
            column = jnp.sum(sums[f], axis=0, keepdims=True)
            column = jnp.sum(column, axis=1, keepdims=True)
            table = jnp.where((fleet == f) & (lane == r + 16 * f), column, table)
        return table

    table = lax.fori_loop(0, 16, one_region, jnp.zeros((N, LANES), F32))
    row = jnp.sum(table, axis=0, keepdims=True)
    catch_out[...] = jnp.broadcast_to(row, catch_out.shape)


def relay_kernel(catches, out):
    out[...] = jnp.broadcast_to(jnp.sum(catches[...], axis=0, keepdims=True), out.shape)


def slope_kernel(
    age, mort, settled, reported, carried, habitat, tail, mass, selectivity,
    still_out, reach_out, kept_out, yield_out, slope_out,
):
    last = age[0] == age[1] - 1

    def tile(t, carry):
        rows = pl.ds(pl.multiple_of(t * 8, 8), 8)
        still = jnp.zeros((8, LANES), F32)
        reach = [jnp.zeros((8, LANES), F32) for _ in range(N)]
        for c in range(N):
            total_mort, settled_c = mort[c, rows, :], settled[c, rows, :]
            survive = jnp.exp(-total_mort)
            yield_frac = (1.0 - survive) / total_mort
            if c + 1 < N:
                coming = carried[c + 1, rows, :]
            else:
                coming = jnp.where(last, carried[c, rows, :], tail[rows, :])
            kept = coming * habitat[rows, :] * survive
            slope = mass[c] * settled_c * (survive - yield_frac) / total_mort
            kept_out[c, rows, :] = kept
            yield_out[c, rows, :] = mass[c] * yield_frac
            slope_out[c, rows, :] = slope
            still = still - kept * settled_c
            for f in range(N):
                reach[f] = reach[f] + selectivity[f, c] * slope
        still_out[rows, :] = still
        for f in range(N):
            reach_out[f, rows, :] = reach[f] * reported[f, rows, :]
        return carry

    lax.fori_loop(0, PACKED // 8, tile, 0)


def press_kernel(catches, observed, region, still, reach, misfit_out, total_out, *, unit):
    predicted = jnp.sum(catches[...], axis=0, keepdims=True) * unit
    misfit = jnp.broadcast_to(1.0 - observed[...] / (1.0 + predicted), (8, LANES))
    misfit_out[...] = misfit
    for t in range(PACKED // 8):
        rows = slice(8 * t, 8 * t + 8)
        place = region[rows, :].astype(jnp.int32)
        total = still[rows, :]
        for f in range(N):
            total = total + jnp.take_along_axis(misfit, place + 16 * f, axis=1) * reach[f, rows, :]
        at_all(total_out, total_out.shape[0], rows, total)


def own_kernel(
    misfit_in, region, reported, settled, kept, yields, slope, flow, swim, spread, mass, selectivity,
    grad_out, bars, wide,
):
    misfit = misfit_in[...]

    def tile(t, carry):
        rows = pl.ds(pl.multiple_of(t * 8, 8), 8)
        place = region[rows, :].astype(jnp.int32)
        spread_back = [
            jnp.take_along_axis(misfit, place + 16 * f, axis=1) * reported[f, rows, :] for f in range(N)
        ]
        run = jnp.zeros((8, LANES), F32)
        for c in range(N):
            pull = selectivity[0, c] * spread_back[0]
            for f in range(1, N):
                pull = pull + selectivity[f, c] * spread_back[f]
            kept_c = kept[c, rows, :]
            bars[c, rows, :] = kept_c + yields[c, rows, :] * pull + (0.02 * mass[c]) * run
            run = run + (slope[c, rows, :] * pull - kept_c * settled[c, rows, :])
        return carry

    lax.fori_loop(0, PACKED // 8, tile, 0)

    def cohort(c, carry):
        coefs, sea = coeffs(flow, swim[c], spread[c]), flow[2]
        unpack_into(wide, bars[c])
        grad_out[c] = retreat(sea * retreat(sea * wide[...], coefs), coefs)[0:ROWS, 0:COLS]
        return carry

    lax.fori_loop(0, N, cohort, 0)


def final_kernel(age, received, own, flow, swim, spread, mass, grad_out, wide, basis):
    shard = age[0]
    unpack_into(wide, picked(received, lambda slot: slot < shard))
    rate, sea = rates(flow), flow[2]
    out_rate = (rate[0] + rate[1]) + (rate[2] + rate[3])
    plain = sea * wide[...]
    spread_once, drift_once = spreading(plain), drifting_back(plain, rate, out_rate)
    spread_sea, drift_sea = sea * spread_once, sea * drift_once
    fields = (
        plain,
        spread_sea + spread_once,
        drift_sea + drift_once,
        spreading(spread_sea),
        spreading(drift_sea) + drifting_back(spread_sea, rate, out_rate),
        drifting_back(drift_sea, rate, out_rate),
    )
    for k, field in enumerate(fields):
        basis[k] = field[0:ROWS, 0:COLS]
    for t in range(ROWS // 8):
        rows = slice(8 * t, 8 * t + 8)
        here = [basis[k, rows, :] for k in range(6)]
        for c in range(N):
            m, d, s = 0.02 * mass[c], spread[c], swim[c]
            younger = m * here[0] + (m * d) * here[1] + (m * s) * here[2]
            younger = younger + (m * d * d) * here[3] + (m * d * s) * here[4] + (m * s * s) * here[5]
            grad_out[c, rows, :] = own[c, rows, :] + younger


VMEM = pl.BlockSpec(memory_space=pltpu.VMEM)
SMEM = pl.BlockSpec(memory_space=pltpu.SMEM)


def shape(*dims):
    return pltpu.VMEM(dims, F32)


def far(*dims):
    return pltpu.HBM(dims, F32)


def near(x):
    return pltpu.with_memory_space_constraint(x, pltpu.VMEM)


def distant(*arrays):
    return [pltpu.with_memory_space_constraint(x, pltpu.HBM) for x in arrays]


def call(kernel, name, in_specs, outs, scratch=()):
    return pl.pallas_call(
        kernel,
        name=name,
        in_specs=in_specs,
        out_specs=[VMEM] * len(outs),
        out_shape=outs,
        scratch_shapes=[pltpu.VMEM(dims, F32) for dims in scratch],
        compiler_params=pltpu.CompilerParams(vmem_limit_bytes=24 << 20),
    )


def local(
    density, adjoint_next, current_east, current_north, swim_speed, diffusion, mortality, cohort_mass,
    selectivity, effort, catch_mask, region, sea_mask, habitat, observed,
):
    lons, lats, ages = (lax.axis_size(axis) for axis in ("lon", "lat", "age"))
    age = jnp.stack([lax.axis_index("age"), jnp.int32(ages)])
    inputs = distant(
        density, adjoint_next, effort, catch_mask, current_east, current_north, region, sea_mask, habitat
    )
    density, adjoint_next, effort, catch_mask, current_east, current_north, region, sea_mask, habitat = inputs
    strip_rows = STRIP + 8

    to_east, to_west, to_north, to_south = call(
        pack_kernel,
        "pack",
        [VMEM] * 9,
        [shape(ROWS, LANES), shape(ROWS, LANES), shape(strip_rows, COLS), shape(strip_rows, COLS)],
    )(*inputs)
    from_west = near(lax.ppermute(to_east, "lon", [(i, (i + 1) % lons) for i in range(lons)]))
    from_east = near(lax.ppermute(to_west, "lon", [((i + 1) % lons, i) for i in range(lons)]))
    to_north, to_south = pl.pallas_call(
        corner_kernel,
        name="corner",
        in_specs=[VMEM] * 4,
        out_specs=[VMEM, VMEM],
        out_shape=[shape(strip_rows, COLS)] * 2,
        input_output_aliases={0: 0, 1: 1},
        compiler_params=pltpu.CompilerParams(vmem_limit_bytes=4 << 20),
    )(near(to_north), near(to_south), from_west, from_east)
    from_south = near(lax.ppermute(to_north, "lat", [(i, i + 1) for i in range(lats - 1)]))
    from_north = near(lax.ppermute(to_south, "lat", [(i + 1, i) for i in range(lats - 1)]))
    halos = (from_west, from_east, from_north, from_south)

    packed = (PACKED, LANES)
    extended = (EROWS, ECOLS)
    totals, tail, density_ext, flow = call(
        total_kernel,
        "total",
        [VMEM] * 9 + [SMEM] * 3,
        [shape(ages, *packed), shape(*packed), shape(N, *extended), far(3, *extended)],
        [(EROWS, LANES), (EROWS, LANES)],
    )(density, current_east, current_north, sea_mask, adjoint_next, *halos, swim_speed, diffusion, cohort_mass)
    totals = lax.all_to_all(totals, "age", 0, 0, tiled=True)
    tail = lax.ppermute(tail, "age", [(i + 1, i) for i in range(ages - 1)])

    settled, fishing, reported, regions, carried, habitats = call(
        fleet_kernel,
        "fleet",
        [VMEM] * 11 + [SMEM] * 4,
        [shape(N, *packed)] * 3 + [shape(*packed), far(N, *packed), far(*packed)],
        [(EROWS, LANES), (EROWS, LANES), (N, *packed)],
    )(
        adjoint_next, effort, catch_mask, region, habitat, *halos, near(density_ext), *distant(flow),
        swim_speed, diffusion, mortality, selectivity,
    )
    settled, reported, regions = near(settled), near(reported), near(regions)

    mort, catches = call(
        catch_kernel,
        "catch",
        [SMEM] + [VMEM] * 5 + [SMEM] * 2,
        [shape(N, *packed), shape(lons, LANES)],
        [packed, (N, *packed)],
    )(age, near(totals), settled, near(fishing), reported, regions, cohort_mass, selectivity)
    catches = near(lax.all_to_all(catches, "lon", 0, 0, tiled=True))
    (catches,) = call(relay_kernel, "relay", [VMEM], [shape(lats * ages, LANES)])(catches)
    catches = near(lax.all_to_all(catches, ("lat", "age"), 0, 0, tiled=True))

    still, reach, kept, yields, slope = call(
        slope_kernel,
        "slope",
        [SMEM] + [VMEM] * 6 + [SMEM] * 2,
        [shape(*packed), shape(N, *packed)] + [far(N, *packed)] * 3,
    )(age, near(mort), settled, reported, *distant(carried, habitats), near(tail), cohort_mass, selectivity)

    unit = observed.shape[1] / (ROWS * COLS * lons * lats)
    misfit, totals = call(
        functools.partial(press_kernel, unit=unit),
        "press",
        [VMEM] * 5,
        [shape(8, LANES), shape(ages, *packed)],
    )(catches, observed.reshape(1, LANES), regions, near(still), near(reach))
    totals = lax.all_to_all(totals, "age", 0, 0, tiled=True)

    kept, yields, slope, flow = distant(kept, yields, slope, flow)
    (own,) = call(
        own_kernel,
        "own",
        [VMEM] * 8 + [SMEM] * 4,
        [shape(N, ROWS, COLS)],
        [(N, *packed), extended],
    )(near(misfit), regions, reported, settled, kept, yields, slope, flow, swim_speed, diffusion, cohort_mass, selectivity)
    (grad,) = call(
        final_kernel,
        "final",
        [SMEM] + [VMEM] * 3 + [SMEM] * 3,
        [far(N, ROWS, COLS)],
        [extended, (6, ROWS, COLS)],
    )(age, near(totals), near(own), flow, swim_speed, diffusion, cohort_mass)
    return grad


def solution(mesh):
    placed = (
        P("age", "lat", "lon"),
        P("age", "lat", "lon"),
        P("lat", "lon"),
        P("lat", "lon"),
        P("age"),
        P("age"),
        P("age"),
        P("age"),
        P(None, "age"),
        P(None, "lat", "lon"),
        P(None, "lat", "lon"),
        P("lat", "lon"),
        P("lat", "lon"),
        P("lat", "lon"),
        P(),
    )
    return jax.shard_map(
        local, mesh=mesh, in_specs=placed, out_specs=P("age", "lat", "lon"), check_vma=False
    )
```

time: 136 us -> 124 us (0.912)
  blocking collectives: 22.9 us -> 13.9 us
  waiting for transfers between devices: 31.3 us -> 29.4 us
    all_to_all x1 -> x2, waiting for transfers between devices: 1.54 us -> 18.4 us  [local(): totals = lax.all_to_all(totals, 'age', 0, 0, tiled=True)]
    ppermute x1, waiting for transfers between devices: 10.5 us -> 0.01 us  [local(): tail = lax.ppermute(tail, 'age', [(i + 1, i) for i in range(ages - 1)])]
    all_to_all x1, blocking collectives: 22.9 us -> 13.9 us  [local(): catches = near(lax.all_to_all(catches, 'lon', 0, 0, tiled=True))]
    all_to_all x1, waiting for transfers between devices: 16 us -> 8.31 us  [local(): catches = near(lax.all_to_all(catches, ('lat', 'age'), 0, 0, tiled=True))]
    all_to_all x1, starting transfers between devices: 15.7 us -> 12.3 us  [local(): catches = near(lax.all_to_all(catches, ('lat', 'age'), 0, 0, tiled=True))]
    all_to_all x1 -> x2, starting transfers between devices: 6.96 us -> 10.4 us  [local(): totals = lax.all_to_all(totals, 'age', 0, 0, tiled=True)]
    pallas_call x5 -> x9, Pallas kernels: 26.1 us -> 26.4 us  [the longest x1 5.93 us: local(): call(own_kernel, 'own', [VMEM] * 8 + [SMEM] * 4, [shape(N, ROWS, COLS)],...]
    unnamed x18 -> x20, local copies, waits for them, and re-layouts: 2.8 us -> 2.48 us
  transfers between devices with their start and end apart: 7 -> 8, of which waited for: 6 -> 6; matrix products, arithmetic and copies ran while one was open for 1% -> 0% of each run, Pallas kernels for 0% -> 16%
where the time goes in v2:
time: 124 us; the launch traced here: 123 us
  starting transfers between devices  48.3 us (39%)
  waiting for transfers between devices  29.4 us (24%)
  Pallas kernels  28.7 us (23%)
  blocking collectives  13.9 us (11%)
  local copies, waits for them, and re-layouts  2.56 us (2%)
    all_to_all x2, waiting for transfers between devices, local(): totals = lax.all_to_all(totals, 'age', 0, 0, tiled=True)  18.4 us
    all_to_all x1, blocking collectives, local(): catches = near(lax.all_to_all(catches, 'lon', 0, 0, tiled=True))  13.9 us
    all_to_all x1, starting transfers between devices, local(): catches = near(lax.all_to_all(catches, ('lat', 'age'), 0, 0, tiled=True))  12.3 us
    all_to_all x2, starting transfers between devices, local(): totals = lax.all_to_all(totals, 'age', 0, 0, tiled=True)  10.4 us
    all_to_all x1, waiting for transfers between devices, local(): catches = near(lax.all_to_all(catches, ('lat', 'age'), 0, 0, tiled=True))  8.31 us
    ppermute x1, starting transfers between devices, local(): lax.ppermute(to_west, 'lon', [((i + 1) % lons, i) for i in range(lons)])  7.73 us
    ppermute x1, starting transfers between devices, local(): lax.ppermute(to_south, 'lat', [(i + 1, i) for i in range(lats - 1)])  6.65 us
    pallas_call x1, Pallas kernels, local(): call(own_kernel, 'own', [VMEM] * 8 + [SMEM] * 4, [shape(N, ROWS, COLS)],...  5.93 us
  transfers between devices with their start and end apart: 8, of which 6 were waited for; matrix products, arithmetic and copies ran while one was open for 0% of the time, Pallas kernels for 16%

profile of v2, /device:TPU:1, one launch (start us, length us, event | category | flops | bytes accessed | tf_op | source)
XLA Modules:
  0.0 123.1 jit_solution(11449399925440790711)
XLA Ops:
  0.0 2.3 %pack.1 = (f32[64,128]{1,0:T(8,128)S(1)}, f32[64,128]{1,0:T(8,128)S(1)}, f32[104,256]{1,0:T(8,128)S(1)}, f32[104,256]{1,0:T(8,128)S(1)}) custom-call(f32[8,64,256]{2,1,0:T(8,128)} %density.1, f32[8,64,256]{2,1,0:T(8,128)} %adjoint.3, f32[8,64,256]{2,1,0:T(8,128)} %effort.1, s32[8,64,256]{2,1,0:T(8,128)} %mask.1, f32[64,256]{1,0:T(8,128)} %current_east.1, ...), custom_call_target="tpu_custom_call" | custom-call | tf_op jit(solution)/shard_map/pack/pallas_call | solution.py:487
  2.3 4.8 %collective-permute-start = (f32[64,128]{1,0:T(8,128)S(1)}, f32[64,128]{1,0:T(8,128)S(1)}, u32[]{:S(2)}, u32[]{:S(2)}) collective-permute-start(f32[64,128]{1,0:T(8,128)S(1)} %get-tuple-element.30), channel_id=1, source_target_pairs={{0,32},{32,64},{64,96},{96,128},{128,160},{160,192},{192,224},{224... | collective-permute-start | bytes 98312 | tf_op jit(solution)/shard_map/ppermute | solution.py:493
  7.1 7.7 %collective-permute-start.1 = (f32[64,128]{1,0:T(8,128)S(1)}, f32[64,128]{1,0:T(8,128)S(1)}, u32[]{:S(2)}, u32[]{:S(2)}) collective-permute-start(f32[64,128]{1,0:T(8,128)S(1)} %get-tuple-element.31), channel_id=1, source_target_pairs={{32,0},{64,32},{96,64},{128,96},{160,128},{192,160},{224,192},{256... | collective-permute-start | bytes 98312 | tf_op jit(solution)/shard_map/ppermute | solution.py:494
  14.9 1.0 collective-permute-done.1.east.east_in
  15.9 6.7 %collective-permute-start.2 = (f32[104,256]{1,0:T(8,128)S(1)}, f32[104,256]{1,0:T(8,128)S(1)}, u32[]{:S(2)}, u32[]{:S(2)}) collective-permute-start(f32[104,256]{1,0:T(8,128)S(1)} %get-tuple-element.34), channel_id=1, source_target_pairs={{8,0},{16,8},{24,16},{9,1},{17,9},{25,17},{10,2},{18,10},{26,18},{... | collective-permute-start | bytes 319496 | tf_op jit(solution)/shard_map/ppermute | solution.py:505
  22.6 5.2 %collective-permute-start.3 = (f32[104,256]{1,0:T(8,128)S(1)}, f32[104,256]{1,0:T(8,128)S(1)}, u32[]{:S(2)}, u32[]{:S(2)}) collective-permute-start(f32[104,256]{1,0:T(8,128)S(1)} %get-tuple-element.35), channel_id=1, source_target_pairs={{0,8},{8,16},{16,24},{1,9},{9,17},{17,25},{2,10},{10,18},{18,26},{... | collective-permute-start | bytes 319496 | tf_op jit(solution)/shard_map/ppermute | solution.py:504
  28.2 1.2 %collective-permute-done.3.south_in = f32[104,256]{1,0:T(8,128)S(1)} collective-permute-done((f32[104,256]{1,0:T(8,128)S(1)}, f32[104,256]{1,0:T(8,128)S(1)}, u32[]{:S(2)}, u32[]{:S(2)}) %collective-permute-start.3) | collective-permute-done | bytes 106528 | tf_op jit(solution)/shard_map/ppermute | solution.py:504
  29.5 3.4 %total.1 = (f32[8,152,128]{2,1,0:T(8,128)}, f32[152,128]{1,0:T(8,128)}, f32[8,72,384]{2,1,0:T(8,128)S(1)}, f32[3,72,384]{2,1,0:T(8,128)}) custom-call(f32[8,64,256]{2,1,0:T(8,128)} %density.1, f32[64,256]{1,0:T(8,128)} %current_east.1, f32[64,256]{1,0:T(8,128)} %current_north.1, s32[64,256]{1,0:T(8,128)} %sea_mask.1, f32[8,64,256]{2,1,0:T(8,128)} %adjoint.3, ...), custom_call_target="tpu_custom_call" | custom-call | tf_op jit(solution)/shard_map/total/pallas_call | solution.py:510
  32.9 6.8 %all-to-all-start = ((f32[8,152,128]{2,1,0:T(8,128)}), f32[8,152,128]{2,1,0:T(8,128)S(1)}, u32[]{:S(2)}, u32[]{:S(2)}) async-start(f32[8,152,128]{2,1,0:T(8,128)} %get-tuple-element.36), calls=%async_computation | async-start | bytes 1245184 | tf_op jit(solution)/shard_map/all_to_all | solution.py:517
  39.7 1.3 %collective-permute-start.4 = (f32[152,128]{1,0:T(8,128)}, f32[152,128]{1,0:T(8,128)}, u32[]{:S(2)}, u32[]{:S(2)}) collective-permute-start(f32[152,128]{1,0:T(8,128)} %get-tuple-element.47), channel_id=1, source_target_pairs={{1,0},{2,1},{3,2},{4,3},{5,4},{6,5},{7,6},{9,8},{10,9},{11,10},{12... | collective-permute-start | bytes 233480 | tf_op jit(solution)/shard_map/ppermute | solution.py:518
  41.7 0.9 copy-done.1
  42.6 0.9 copy-done.3
  43.5 5.8 %fleet.1 = (f32[8,152,128]{2,1,0:T(8,128)S(1)}, f32[8,152,128]{2,1,0:T(8,128)S(1)}, f32[8,152,128]{2,1,0:T(8,128)S(1)}, f32[152,128]{1,0:T(8,128)S(1)}, f32[8,152,128]{2,1,0:T(8,128)}, /*index=5*/f32[152,128]{1,0:T(8,128)}) custom-call(f32[8,64,256]{2,1,0:T(8,128)} %adjoint.3, f32[8,64,256]{2,1,0:T(8,128)} %effort.1, s32[8,64,256]{2,1,0:T(8,128)} %mask.1, ...), custom_call_target="tpu_custom_call" | custom-call | tf_op jit(solution)/shard_map/fleet/pallas_call | solution.py:520
  49.3 4.4 %all-to-all-done.received = f32[8,152,128]{2,1,0:T(8,128)S(1)} async-done(((f32[8,152,128]{2,1,0:T(8,128)}), f32[8,152,128]{2,1,0:T(8,128)S(1)}, u32[]{:S(2)}, u32[]{:S(2)}) %all-to-all-start) | async-done | bytes 622624 | tf_op jit(solution)/shard_map/all_to_all | solution.py:517
  53.7 3.6 %catch.1 = (f32[8,152,128]{2,1,0:T(8,128)S(1)}, f32[16,128]{1,0:T(8,128)S(1)}) custom-call(s32[2]{0:T(128)S(1)} %pad_add_fusion.age, f32[8,152,128]{2,1,0:T(8,128)S(1)} %all-to-all-done.received, f32[8,152,128]{2,1,0:T(8,128)S(1)} %get-tuple-element.39.settled, f32[8,152,128]{2,1,0:T(8,128)S(1)} %get-tuple-element.40.fishing, ...), custom_call_target="tpu_custom_call" | custom-call | tf_op jit(solution)/shard_map/catch/pallas_call | solution.py:532
  57.3 13.9 %all_to_all.32 = f32[16,1,128]{2,1,0:T(1,128)S(1)} all-to-all(f32[16,1,128]{2,1,0:T(1,128)S(1)} %bitcast.11), channel_id=1, replica_groups=mesh['lon'=16,'lat'=4,'age'=8] {'lon'}, dimensions={0} | all-to-all | bytes 16384 | tf_op jit(solution)/shard_map/all_to_all | solution.py:539
  71.8 12.3 %all-to-all-start.2 = ((f32[32,1,128]{2,1,0:T(1,128)}), f32[32,1,128]{2,1,0:T(1,128)S(1)}, u32[]{:S(2)}, u32[]{:S(2)}) async-start(f32[32,1,128]{2,1,0:T(1,128)} %bitcast.5), calls=%async_computation.2 | async-start | bytes 32768 | tf_op jit(solution)/shard_map/all_to_all | solution.py:541
  84.1 3.4 %slope.1 = (f32[152,128]{1,0:T(8,128)S(1)}, f32[8,152,128]{2,1,0:T(8,128)S(1)}, f32[8,152,128]{2,1,0:T(8,128)}, f32[8,152,128]{2,1,0:T(8,128)}, f32[8,152,128]{2,1,0:T(8,128)}) custom-call(s32[2]{0:T(128)S(1)} %pad_add_fusion.age, f32[8,152,128]{2,1,0:T(8,128)S(1)} %get-tuple-element.44.mort, f32[8,152,128]{2,1,0:T(8,128)S(1)} %get-tuple-element.39.settled, ...), custom_call_target="tpu_custom_call" | custom-call | tf_op jit(solution)/shard_map/slope/pallas_call | solution.py:543
  87.5 8.3 %all-to-all-done.2 = f32[32,1,128]{2,1,0:T(1,128)S(1)} async-done(((f32[32,1,128]{2,1,0:T(1,128)}), f32[32,1,128]{2,1,0:T(1,128)S(1)}, u32[]{:S(2)}, u32[]{:S(2)}) %all-to-all-start.2) | async-done | bytes 16416 | tf_op jit(solution)/shard_map/all_to_all | solution.py:541
  95.8 1.4 %press.1 = (f32[8,128]{1,0:T(8,128)S(1)}, f32[8,152,128]{2,1,0:T(8,128)}) custom-call(f32[32,128]{1,0:T(8,128)S(1)} %bitcast.9, f32[1,128]{1,0:T(1,128)S(1)} %reshape.7.observed, f32[152,128]{1,0:T(8,128)S(1)} %get-tuple-element.42.region, f32[152,128]{1,0:T(8,128)S(1)} %get-tuple-element.48.still, f32[8,152,128]{2,1,0:T(8,128)S(1)} %get-tuple-element.49.reach), custom_call_target="tpu_custom_call" | custom-call | tf_op jit(solution)/shard_map/press/pallas_call | solution.py:551
  97.1 3.5 %all-to-all-start.3 = ((f32[8,152,128]{2,1,0:T(8,128)}), f32[8,152,128]{2,1,0:T(8,128)S(1)}, u32[]{:S(2)}, u32[]{:S(2)}) async-start(f32[8,152,128]{2,1,0:T(8,128)} %get-tuple-element.50), calls=%async_computation.3 | async-start | bytes 1245184 | tf_op jit(solution)/shard_map/all_to_all | solution.py:557
  100.7 5.9 %own.1 = f32[8,64,256]{2,1,0:T(8,128)S(1)} custom-call(f32[8,128]{1,0:T(8,128)S(1)} %get-tuple-element.51.misfit_in, f32[152,128]{1,0:T(8,128)S(1)} %get-tuple-element.42.region, f32[8,152,128]{2,1,0:T(8,128)S(1)} %get-tuple-element.41.reported, f32[8,152,128]{2,1,0:T(8,128)S(1)} %get-tuple-element.39.settled, f32[8,152,128]{2,1,0:T(8,128)} %get-tuple-element.52.kept, ...), custom_call_target="tpu_custom_call" | custom-call | tf_op jit(solution)/shard_map/own/pallas_call | solution.py:560
  106.6 14.0 %all-to-all-done.3.received = f32[8,152,128]{2,1,0:T(8,128)S(1)} async-done(((f32[8,152,128]{2,1,0:T(8,128)}), f32[8,152,128]{2,1,0:T(8,128)S(1)}, u32[]{:S(2)}, u32[]{:S(2)}) %all-to-all-start.3) | async-done | bytes 622624 | tf_op jit(solution)/shard_map/all_to_all | solution.py:557
  120.7 2.5 %final.1 = f32[8,64,256]{2,1,0:T(8,128)} custom-call(s32[2]{0:T(128)S(1)} %pad_add_fusion.age, f32[8,152,128]{2,1,0:T(8,128)S(1)} %all-to-all-done.3.received, f32[8,64,256]{2,1,0:T(8,128)S(1)} %own.1, f32[3,72,384]{2,1,0:T(8,128)} %get-tuple-element.38.flow, f32[8]{0:T(128)S(1)} %copy-done.6, f32[8]{0:T(128)S(1)} %copy-done.7, f32[8]{0:T(128)S(1)} %copy-done.5), custom_call_target="tpu_custom_call" | custom-call | tf_op jit(solution)/shard_map/final/pallas_call | solution.py:567
  (25 shorter events, 1.9 us)
Async XLA Ops:
  2.3 12.6 %collective-permute-start = (f32[64,128]{1,0:T(8,128)S(1)}, f32[64,128]{1,0:T(8,128)S(1)}, u32[]{:S(2)}, u32[]{:S(2)}) collective-permute-start(f32[64,128]{1,0:T(8,128)S(1)} %get-tuple-element.30), channel_id=1, source_target_pairs={{0,32},{32,64},{64,96},{96,128},{128,160},{160,192},{192,224},{224... | collective-permute-start | bytes 98312 | tf_op jit(solution)/shard_map/ppermute | solution.py:493
  7.1 8.7 %collective-permute-start.1 = (f32[64,128]{1,0:T(8,128)S(1)}, f32[64,128]{1,0:T(8,128)S(1)}, u32[]{:S(2)}, u32[]{:S(2)}) collective-permute-start(f32[64,128]{1,0:T(8,128)S(1)} %get-tuple-element.31), channel_id=1, source_target_pairs={{32,0},{64,32},{96,64},{128,96},{160,128},{192,160},{224,192},{256... | collective-permute-start | bytes 98312 | tf_op jit(solution)/shard_map/ppermute | solution.py:494
  15.9 13.6 %copy-start.5 = (f32[8]{0:T(128)S(1)}, f32[8]{0:T(128)}, u32[]{:S(2)}) copy-start(f32[8]{0:T(128)} %mass.9) | copy-start | bytes 100
  15.9 13.6 %copy-start.6 = (f32[8]{0:T(128)S(1)}, f32[8]{0:T(128)}, u32[]{:S(2)}) copy-start(f32[8]{0:T(128)} %swim.7) | copy-start | bytes 100
  15.9 13.6 %copy-start.7 = (f32[8]{0:T(128)S(1)}, f32[8]{0:T(128)}, u32[]{:S(2)}) copy-start(f32[8]{0:T(128)} %spread.7) | copy-start | bytes 100
  15.9 12.3 %collective-permute-start.2 = (f32[104,256]{1,0:T(8,128)S(1)}, f32[104,256]{1,0:T(8,128)S(1)}, u32[]{:S(2)}, u32[]{:S(2)}) collective-permute-start(f32[104,256]{1,0:T(8,128)S(1)} %get-tuple-element.34), channel_id=1, source_target_pairs={{8,0},{16,8},{24,16},{9,1},{17,9},{25,17},{10,2},{18,10},{26,18},{... | collective-permute-start | bytes 319496 | tf_op jit(solution)/shard_map/ppermute | solution.py:505
  22.6 6.9 %collective-permute-start.3 = (f32[104,256]{1,0:T(8,128)S(1)}, f32[104,256]{1,0:T(8,128)S(1)}, u32[]{:S(2)}, u32[]{:S(2)}) collective-permute-start(f32[104,256]{1,0:T(8,128)S(1)} %get-tuple-element.35), channel_id=1, source_target_pairs={{0,8},{8,16},{16,24},{1,9},{9,17},{17,25},{2,10},{10,18},{18,26},{... | collective-permute-start | bytes 319496 | tf_op jit(solution)/shard_map/ppermute | solution.py:504
  28.2 4.6 %copy-start = (f32[104,256]{1,0:T(8,128)}, f32[104,256]{1,0:T(8,128)S(1)}, u32[]{:S(2)}) copy-start(f32[104,256]{1,0:T(8,128)S(1)} %collective-permute-done.2.north_in) | copy-start | bytes 319492
  29.5 3.4 %copy-start.2 = (f32[104,256]{1,0:T(8,128)}, f32[104,256]{1,0:T(8,128)S(1)}, u32[]{:S(2)}) copy-start(f32[104,256]{1,0:T(8,128)S(1)} %collective-permute-done.3.south_in) | copy-start | bytes 319492
  32.9 20.8 %all-to-all-start = ((f32[8,152,128]{2,1,0:T(8,128)}), f32[8,152,128]{2,1,0:T(8,128)S(1)}, u32[]{:S(2)}, u32[]{:S(2)}) async-start(f32[8,152,128]{2,1,0:T(8,128)} %get-tuple-element.36), calls=%async_computation | async-start | bytes 1245184 | tf_op jit(solution)/shard_map/all_to_all | solution.py:517
  39.7 1.4 %copy-start.4 = (f32[8,8]{1,0:T(8,128)S(1)}, f32[8,8]{1,0:T(8,128)}, u32[]{:S(2)}) copy-start(f32[8,8]{1,0:T(8,128)} %selectivity.7) | copy-start | bytes 772
  39.7 44.4 %collective-permute-start.4 = (f32[152,128]{1,0:T(8,128)}, f32[152,128]{1,0:T(8,128)}, u32[]{:S(2)}, u32[]{:S(2)}) collective-permute-start(f32[152,128]{1,0:T(8,128)} %get-tuple-element.47), channel_id=1, source_target_pairs={{1,0},{2,1},{3,2},{4,3},{5,4},{6,5},{7,6},{9,8},{10,9},{11,10},{12... | collective-permute-start | bytes 233480 | tf_op jit(solution)/shard_map/ppermute | solution.py:518
  41.1 0.7 copy-start.8
  41.7 0.9 copy-start.1
  42.6 0.9 copy-start.3
  71.8 12.3 %copy-start.9 = (f32[8,16]{1,0:T(8,128)S(1)}, f32[8,16]{1,0:T(8,128)}, u32[]{:S(2)}) copy-start(f32[8,16]{1,0:T(8,128)} %param.29) | copy-start | bytes 1540
  71.8 24.0 %all-to-all-start.2 = ((f32[32,1,128]{2,1,0:T(1,128)}), f32[32,1,128]{2,1,0:T(1,128)S(1)}, u32[]{:S(2)}, u32[]{:S(2)}) async-start(f32[32,1,128]{2,1,0:T(1,128)} %bitcast.5), calls=%async_computation.2 | async-start | bytes 32768 | tf_op jit(solution)/shard_map/all_to_all | solution.py:541
  97.1 23.5 %all-to-all-start.3 = ((f32[8,152,128]{2,1,0:T(8,128)}), f32[8,152,128]{2,1,0:T(8,128)S(1)}, u32[]{:S(2)}, u32[]{:S(2)}) async-start(f32[8,152,128]{2,1,0:T(8,128)} %get-tuple-element.50), calls=%async_computation.3 | async-start | bytes 1245184 | tf_op jit(solution)/shard_map/all_to_all | solution.py:557

commit v3 on v2

--- a/solution.py
+++ b/solution.py
@@ -490,8 +490,8 @@
         [VMEM] * 9,
         [shape(ROWS, LANES), shape(ROWS, LANES), shape(strip_rows, COLS), shape(strip_rows, COLS)],
     )(*inputs)
-    from_west = near(lax.ppermute(to_east, "lon", [(i, (i + 1) % lons) for i in range(lons)]))
-    from_east = near(lax.ppermute(to_west, "lon", [((i + 1) % lons, i) for i in range(lons)]))
+    from_west = lax.ppermute(to_east, "lon", [(i, (i + 1) % lons) for i in range(lons)])
+    from_east = lax.ppermute(to_west, "lon", [((i + 1) % lons, i) for i in range(lons)])
     to_north, to_south = pl.pallas_call(
         corner_kernel,
         name="corner",
@@ -500,9 +500,9 @@
         out_shape=[shape(strip_rows, COLS)] * 2,
         input_output_aliases={0: 0, 1: 1},
         compiler_params=pltpu.CompilerParams(vmem_limit_bytes=4 << 20),
-    )(near(to_north), near(to_south), from_west, from_east)
-    from_south = near(lax.ppermute(to_north, "lat", [(i, i + 1) for i in range(lats - 1)]))
-    from_north = near(lax.ppermute(to_south, "lat", [(i + 1, i) for i in range(lats - 1)]))
+    )(near(to_north), near(to_south), near(from_west), near(from_east))
+    from_south = lax.ppermute(to_north, "lat", [(i, i + 1) for i in range(lats - 1)])
+    from_north = lax.ppermute(to_south, "lat", [(i + 1, i) for i in range(lats - 1)])
     halos = (from_west, from_east, from_north, from_south)
 
     packed = (PACKED, LANES)
@@ -513,7 +513,7 @@
         [VMEM] * 9 + [SMEM] * 3,
         [shape(ages, *packed), shape(*packed), shape(N, *extended), far(3, *extended)],
         [(EROWS, LANES), (EROWS, LANES)],
-    )(density, current_east, current_north, sea_mask, adjoint_next, *halos, swim_speed, diffusion, cohort_mass)
+    )(density, current_east, current_north, sea_mask, adjoint_next, *map(near, halos), swim_speed, diffusion, cohort_mass)
     totals = lax.all_to_all(totals, "age", 0, 0, tiled=True)
     tail = lax.ppermute(tail, "age", [(i + 1, i) for i in range(ages - 1)])
 
@@ -524,7 +524,7 @@
         [shape(N, *packed)] * 3 + [shape(*packed), far(N, *packed), far(*packed)],
         [(EROWS, LANES), (EROWS, LANES), (N, *packed)],
     )(
-        adjoint_next, effort, catch_mask, region, habitat, *halos, near(density_ext), *distant(flow),
+        adjoint_next, effort, catch_mask, region, habitat, *distant(*halos), near(density_ext), *distant(flow),
         swim_speed, diffusion, mortality, selectivity,
     )
     settled, reported, regions = near(settled), near(reported), near(regions)
@@ -533,12 +533,12 @@
         catch_kernel,
         "catch",
         [SMEM] + [VMEM] * 5 + [SMEM] * 2,
-        [shape(N, *packed), shape(lons, LANES)],
+        [shape(N, *packed), shape(ages, LANES)],
         [packed, (N, *packed)],
     )(age, near(totals), settled, near(fishing), reported, regions, cohort_mass, selectivity)
-    catches = near(lax.all_to_all(catches, "lon", 0, 0, tiled=True))
-    (catches,) = call(relay_kernel, "relay", [VMEM], [shape(lats * ages, LANES)])(catches)
-    catches = near(lax.all_to_all(catches, ("lat", "age"), 0, 0, tiled=True))
+    catches = near(lax.all_to_all(catches, "age", 0, 0, tiled=True))
+    (catches,) = call(relay_kernel, "relay", [VMEM], [shape(lons * lats, LANES)])(catches)
+    catches = near(lax.all_to_all(catches, ("lon", "lat"), 0, 0, tiled=True))
 
     still, reach, kept, yields, slope = call(
         slope_kernel,

time: 124 us -> 118 us (0.952)
  blocking collectives: 13.9 us -> 8.92 us
  local copies, waits for them, and re-layouts: 2.56 us -> 0.77 us
    all_to_all x1, blocking collectives: 13.9 us -> 8.92 us  [local(): catches = near(lax.all_to_all(catches, 'age', 0, 0, tiled=True))]
    all_to_all x1, waiting for transfers between devices: 8.31 us -> 5.93 us  [local(): catches = near(lax.all_to_all(catches, ('lon', 'lat'), 0, 0, tiled=True))]
    unnamed x20, local copies, waits for them, and re-layouts: 2.48 us -> 0.69 us
    all_to_all x2, waiting for transfers between devices: 18.4 us -> 20.1 us  [local(): totals = lax.all_to_all(totals, 'age', 0, 0, tiled=True)]
  transfers between devices with their start and end apart: 8 -> 8, of which waited for: 6 -> 6; matrix products, arithmetic and copies ran while one was open for 0% -> 0% of each run, Pallas kernels for 16% -> 17%
where the time goes in v3:
time: 118 us; the launch traced here: 117 us
  starting transfers between devices  49.5 us (42%)
  Pallas kernels  28.9 us (24%)
  waiting for transfers between devices  28.7 us (24%)
  blocking collectives  8.92 us (8%)
    all_to_all x2, waiting for transfers between devices, local(): totals = lax.all_to_all(totals, 'age', 0, 0, tiled=True)  20.1 us
    all_to_all x1, starting transfers between devices, local(): catches = near(lax.all_to_all(catches, ('lon', 'lat'), 0, 0, tiled=True))  13.4 us
    all_to_all x2, starting transfers between devices, local(): totals = lax.all_to_all(totals, 'age', 0, 0, tiled=True)  10.4 us
    all_to_all x1, blocking collectives, local(): catches = near(lax.all_to_all(catches, 'age', 0, 0, tiled=True))  8.92 us
    ppermute x1, starting transfers between devices, local(): lax.ppermute(to_west, 'lon', [((i + 1) % lons, i) for i in range(lons)])  7.73 us
    ppermute x1, starting transfers between devices, local(): lax.ppermute(to_south, 'lat', [(i + 1, i) for i in range(lats - 1)])  6.65 us
    all_to_all x1, waiting for transfers between devices, local(): catches = near(lax.all_to_all(catches, ('lon', 'lat'), 0, 0, tiled=True))  5.93 us
    pallas_call x1, Pallas kernels, local(): call(own_kernel, 'own', [VMEM] * 8 + [SMEM] * 4, [shape(N, ROWS, COLS)],...  5.93 us
  transfers between devices with their start and end apart: 8, of which 6 were waited for; matrix products, arithmetic and copies ran while one was open for 0% of the time, Pallas kernels for 17%

profile of v3, /device:TPU:1, one launch (start us, length us, event | category | flops | bytes accessed | tf_op | source)
XLA Modules:
  0.0 117.0 jit_solution(17031541983206751021)
XLA Ops:
  0.0 2.3 %pack.1 = (f32[64,128]{1,0:T(8,128)S(1)}, f32[64,128]{1,0:T(8,128)S(1)}, f32[104,256]{1,0:T(8,128)S(1)}, f32[104,256]{1,0:T(8,128)S(1)}) custom-call(f32[8,64,256]{2,1,0:T(8,128)} %density.1, f32[8,64,256]{2,1,0:T(8,128)} %adjoint.3, f32[8,64,256]{2,1,0:T(8,128)} %effort.1, s32[8,64,256]{2,1,0:T(8,128)} %mask.1, f32[64,256]{1,0:T(8,128)} %current_east.1, ...), custom_call_target="tpu_custom_call" | custom-call | tf_op jit(solution)/shard_map/pack/pallas_call | solution.py:487
  2.3 4.8 %collective-permute-start = (f32[64,128]{1,0:T(8,128)S(1)}, f32[64,128]{1,0:T(8,128)S(1)}, u32[]{:S(2)}, u32[]{:S(2)}) collective-permute-start(f32[64,128]{1,0:T(8,128)S(1)} %get-tuple-element.30), channel_id=1, source_target_pairs={{0,32},{32,64},{64,96},{96,128},{128,160},{160,192},{192,224},{224... | collective-permute-start | bytes 98312 | tf_op jit(solution)/shard_map/ppermute | solution.py:493
  7.1 7.7 %collective-permute-start.1 = (f32[64,128]{1,0:T(8,128)S(1)}, f32[64,128]{1,0:T(8,128)S(1)}, u32[]{:S(2)}, u32[]{:S(2)}) collective-permute-start(f32[64,128]{1,0:T(8,128)S(1)} %get-tuple-element.31), channel_id=1, source_target_pairs={{32,0},{64,32},{96,64},{128,96},{160,128},{192,160},{224,192},{256... | collective-permute-start | bytes 98312 | tf_op jit(solution)/shard_map/ppermute | solution.py:494
  14.9 1.0 collective-permute-done.1.east.east_in
  15.9 6.7 %collective-permute-start.2 = (f32[104,256]{1,0:T(8,128)S(1)}, f32[104,256]{1,0:T(8,128)S(1)}, u32[]{:S(2)}, u32[]{:S(2)}) collective-permute-start(f32[104,256]{1,0:T(8,128)S(1)} %get-tuple-element.34), channel_id=1, source_target_pairs={{8,0},{16,8},{24,16},{9,1},{17,9},{25,17},{10,2},{18,10},{26,18},{... | collective-permute-start | bytes 319496 | tf_op jit(solution)/shard_map/ppermute | solution.py:505
  22.6 5.2 %collective-permute-start.3 = (f32[104,256]{1,0:T(8,128)S(1)}, f32[104,256]{1,0:T(8,128)S(1)}, u32[]{:S(2)}, u32[]{:S(2)}) collective-permute-start(f32[104,256]{1,0:T(8,128)S(1)} %get-tuple-element.35), channel_id=1, source_target_pairs={{0,8},{8,16},{16,24},{1,9},{9,17},{17,25},{2,10},{10,18},{18,26},{... | collective-permute-start | bytes 319496 | tf_op jit(solution)/shard_map/ppermute | solution.py:504
  28.2 1.2 %collective-permute-done.3.south_in = f32[104,256]{1,0:T(8,128)S(1)} collective-permute-done((f32[104,256]{1,0:T(8,128)S(1)}, f32[104,256]{1,0:T(8,128)S(1)}, u32[]{:S(2)}, u32[]{:S(2)}) %collective-permute-start.3) | collective-permute-done | bytes 106528 | tf_op jit(solution)/shard_map/ppermute | solution.py:504
  29.5 3.4 %total.1 = (f32[8,152,128]{2,1,0:T(8,128)}, f32[152,128]{1,0:T(8,128)}, f32[8,72,384]{2,1,0:T(8,128)S(1)}, f32[3,72,384]{2,1,0:T(8,128)}) custom-call(f32[8,64,256]{2,1,0:T(8,128)} %density.1, f32[64,256]{1,0:T(8,128)} %current_east.1, f32[64,256]{1,0:T(8,128)} %current_north.1, s32[64,256]{1,0:T(8,128)} %sea_mask.1, f32[8,64,256]{2,1,0:T(8,128)} %adjoint.3, ...), custom_call_target="tpu_custom_call" | custom-call | tf_op jit(solution)/shard_map/total/pallas_call | solution.py:510
  32.9 6.8 %all-to-all-start = ((f32[8,152,128]{2,1,0:T(8,128)}), f32[8,152,128]{2,1,0:T(8,128)S(1)}, u32[]{:S(2)}, u32[]{:S(2)}) async-start(f32[8,152,128]{2,1,0:T(8,128)} %get-tuple-element.36), calls=%async_computation | async-start | bytes 1245184 | tf_op jit(solution)/shard_map/all_to_all | solution.py:517
  39.7 1.3 %collective-permute-start.4 = (f32[152,128]{1,0:T(8,128)}, f32[152,128]{1,0:T(8,128)S(1)}, u32[]{:S(2)}, u32[]{:S(2)}) collective-permute-start(f32[152,128]{1,0:T(8,128)} %get-tuple-element.47), channel_id=1, source_target_pairs={{1,0},{2,1},{3,2},{4,3},{5,4},{6,5},{7,6},{9,8},{10,9},{11,10},{12... | collective-permute-start | bytes 233480 | tf_op jit(solution)/shard_map/ppermute | solution.py:518
  41.1 0.7 copy-done.8
  41.8 5.9 %fleet.1 = (f32[8,152,128]{2,1,0:T(8,128)S(1)}, f32[8,152,128]{2,1,0:T(8,128)S(1)}, f32[8,152,128]{2,1,0:T(8,128)S(1)}, f32[152,128]{1,0:T(8,128)S(1)}, f32[8,152,128]{2,1,0:T(8,128)}, /*index=5*/f32[152,128]{1,0:T(8,128)}) custom-call(f32[8,64,256]{2,1,0:T(8,128)} %adjoint.3, f32[8,64,256]{2,1,0:T(8,128)} %effort.1, s32[8,64,256]{2,1,0:T(8,128)} %mask.1, ...), custom_call_target="tpu_custom_call" | custom-call | tf_op jit(solution)/shard_map/fleet/pallas_call | solution.py:520
  47.6 6.1 %all-to-all-done.received = f32[8,152,128]{2,1,0:T(8,128)S(1)} async-done(((f32[8,152,128]{2,1,0:T(8,128)}), f32[8,152,128]{2,1,0:T(8,128)S(1)}, u32[]{:S(2)}, u32[]{:S(2)}) %all-to-all-start) | async-done | bytes 622624 | tf_op jit(solution)/shard_map/all_to_all | solution.py:517
  53.7 3.6 %catch.1 = (f32[8,152,128]{2,1,0:T(8,128)S(1)}, f32[8,128]{1,0:T(8,128)S(1)}) custom-call(s32[2]{0:T(128)S(1)} %pad_add_fusion.age, f32[8,152,128]{2,1,0:T(8,128)S(1)} %all-to-all-done.received, f32[8,152,128]{2,1,0:T(8,128)S(1)} %get-tuple-element.39.settled, f32[8,152,128]{2,1,0:T(8,128)S(1)} %get-tuple-element.40.fishing, ...), custom_call_target="tpu_custom_call" | custom-call | tf_op jit(solution)/shard_map/catch/pallas_call | solution.py:532
  57.3 8.9 %all_to_all.32 = f32[8,1,128]{2,1,0:T(1,128)S(1)} all-to-all(f32[8,1,128]{2,1,0:T(1,128)S(1)} %bitcast.11), channel_id=1, replica_groups=mesh['lon'=16,'lat'=4,'age'=8] {'age'}, dimensions={0} | all-to-all | bytes 8192 | tf_op jit(solution)/shard_map/all_to_all | solution.py:539
  66.2 0.6 relay.1
  66.8 13.4 %all-to-all-start.2 = ((f32[64,1,128]{2,1,0:T(1,128)}), f32[64,1,128]{2,1,0:T(1,128)S(1)}, u32[]{:S(2)}, u32[]{:S(2)}) async-start(f32[64,1,128]{2,1,0:T(1,128)} %bitcast.5), calls=%async_computation.2 | async-start | bytes 65536 | tf_op jit(solution)/shard_map/all_to_all | solution.py:541
  80.4 3.4 %slope.1 = (f32[152,128]{1,0:T(8,128)S(1)}, f32[8,152,128]{2,1,0:T(8,128)S(1)}, f32[8,152,128]{2,1,0:T(8,128)}, f32[8,152,128]{2,1,0:T(8,128)}, f32[8,152,128]{2,1,0:T(8,128)}) custom-call(s32[2]{0:T(128)S(1)} %pad_add_fusion.age, f32[8,152,128]{2,1,0:T(8,128)S(1)} %get-tuple-element.44.mort, f32[8,152,128]{2,1,0:T(8,128)S(1)} %get-tuple-element.39.settled, ...), custom_call_target="tpu_custom_call" | custom-call | tf_op jit(solution)/shard_map/slope/pallas_call | solution.py:543
  83.8 5.9 %all-to-all-done.2 = f32[64,1,128]{2,1,0:T(1,128)S(1)} async-done(((f32[64,1,128]{2,1,0:T(1,128)}), f32[64,1,128]{2,1,0:T(1,128)S(1)}, u32[]{:S(2)}, u32[]{:S(2)}) %all-to-all-start.2) | async-done | bytes 32800 | tf_op jit(solution)/shard_map/all_to_all | solution.py:541
  89.7 1.4 %press.1 = (f32[8,128]{1,0:T(8,128)S(1)}, f32[8,152,128]{2,1,0:T(8,128)}) custom-call(f32[64,128]{1,0:T(8,128)S(1)} %bitcast.9, f32[1,128]{1,0:T(1,128)S(1)} %reshape.7.observed, f32[152,128]{1,0:T(8,128)S(1)} %get-tuple-element.42.region, f32[152,128]{1,0:T(8,128)S(1)} %get-tuple-element.48.still, f32[8,152,128]{2,1,0:T(8,128)S(1)} %get-tuple-element.49.reach), custom_call_target="tpu_custom_call" | custom-call | tf_op jit(solution)/shard_map/press/pallas_call | solution.py:551
  91.1 3.5 %all-to-all-start.3 = ((f32[8,152,128]{2,1,0:T(8,128)}), f32[8,152,128]{2,1,0:T(8,128)S(1)}, u32[]{:S(2)}, u32[]{:S(2)}) async-start(f32[8,152,128]{2,1,0:T(8,128)} %get-tuple-element.50), calls=%async_computation.3 | async-start | bytes 1245184 | tf_op jit(solution)/shard_map/all_to_all | solution.py:557
  94.6 5.9 %own.1 = f32[8,64,256]{2,1,0:T(8,128)S(1)} custom-call(f32[8,128]{1,0:T(8,128)S(1)} %get-tuple-element.51.misfit_in, f32[152,128]{1,0:T(8,128)S(1)} %get-tuple-element.42.region, f32[8,152,128]{2,1,0:T(8,128)S(1)} %get-tuple-element.41.reported, f32[8,152,128]{2,1,0:T(8,128)S(1)} %get-tuple-element.39.settled, f32[8,152,128]{2,1,0:T(8,128)} %get-tuple-element.52.kept, ...), custom_call_target="tpu_custom_call" | custom-call | tf_op jit(solution)/shard_map/own/pallas_call | solution.py:560
  100.5 14.0 %all-to-all-done.3.received = f32[8,152,128]{2,1,0:T(8,128)S(1)} async-done(((f32[8,152,128]{2,1,0:T(8,128)}), f32[8,152,128]{2,1,0:T(8,128)S(1)}, u32[]{:S(2)}, u32[]{:S(2)}) %all-to-all-start.3) | async-done | bytes 622624 | tf_op jit(solution)/shard_map/all_to_all | solution.py:557
  114.6 2.5 %final.1 = f32[8,64,256]{2,1,0:T(8,128)} custom-call(s32[2]{0:T(128)S(1)} %pad_add_fusion.age, f32[8,152,128]{2,1,0:T(8,128)S(1)} %all-to-all-done.3.received, f32[8,64,256]{2,1,0:T(8,128)S(1)} %own.1, f32[3,72,384]{2,1,0:T(8,128)} %get-tuple-element.38.flow, f32[8]{0:T(128)S(1)} %copy-done.6, f32[8]{0:T(128)S(1)} %copy-done.7, f32[8]{0:T(128)S(1)} %copy-done.5), custom_call_target="tpu_custom_call" | custom-call | tf_op jit(solution)/shard_map/final/pallas_call | solution.py:567
  (25 shorter events, 0.7 us)
Async XLA Ops:
  2.3 12.6 %collective-permute-start = (f32[64,128]{1,0:T(8,128)S(1)}, f32[64,128]{1,0:T(8,128)S(1)}, u32[]{:S(2)}, u32[]{:S(2)}) collective-permute-start(f32[64,128]{1,0:T(8,128)S(1)} %get-tuple-element.30), channel_id=1, source_target_pairs={{0,32},{32,64},{64,96},{96,128},{128,160},{160,192},{192,224},{224... | collective-permute-start | bytes 98312 | tf_op jit(solution)/shard_map/ppermute | solution.py:493
  7.1 8.7 %collective-permute-start.1 = (f32[64,128]{1,0:T(8,128)S(1)}, f32[64,128]{1,0:T(8,128)S(1)}, u32[]{:S(2)}, u32[]{:S(2)}) collective-permute-start(f32[64,128]{1,0:T(8,128)S(1)} %get-tuple-element.31), channel_id=1, source_target_pairs={{32,0},{64,32},{96,64},{128,96},{160,128},{192,160},{224,192},{256... | collective-permute-start | bytes 98312 | tf_op jit(solution)/shard_map/ppermute | solution.py:494
  14.9 14.6 %copy-start.2 = (f32[64,128]{1,0:T(8,128)}, f32[64,128]{1,0:T(8,128)S(1)}, u32[]{:S(2)}) copy-start(f32[64,128]{1,0:T(8,128)S(1)} %collective-permute-done.west.west_in) | copy-start | bytes 98308
  15.9 13.6 %copy-start.3 = (f32[64,128]{1,0:T(8,128)}, f32[64,128]{1,0:T(8,128)S(1)}, u32[]{:S(2)}) copy-start(f32[64,128]{1,0:T(8,128)S(1)} %collective-permute-done.1.east.east_in) | copy-start | bytes 98308
  15.9 13.6 %copy-start.5 = (f32[8]{0:T(128)S(1)}, f32[8]{0:T(128)}, u32[]{:S(2)}) copy-start(f32[8]{0:T(128)} %mass.9) | copy-start | bytes 100
  15.9 13.6 %copy-start.6 = (f32[8]{0:T(128)S(1)}, f32[8]{0:T(128)}, u32[]{:S(2)}) copy-start(f32[8]{0:T(128)} %swim.7) | copy-start | bytes 100
  15.9 13.6 %copy-start.7 = (f32[8]{0:T(128)S(1)}, f32[8]{0:T(128)}, u32[]{:S(2)}) copy-start(f32[8]{0:T(128)} %spread.7) | copy-start | bytes 100
  15.9 12.3 %collective-permute-start.2 = (f32[104,256]{1,0:T(8,128)S(1)}, f32[104,256]{1,0:T(8,128)S(1)}, u32[]{:S(2)}, u32[]{:S(2)}) collective-permute-start(f32[104,256]{1,0:T(8,128)S(1)} %get-tuple-element.34), channel_id=1, source_target_pairs={{8,0},{16,8},{24,16},{9,1},{17,9},{25,17},{10,2},{18,10},{26,18},{... | collective-permute-start | bytes 319496 | tf_op jit(solution)/shard_map/ppermute | solution.py:505
  22.6 6.9 %collective-permute-start.3 = (f32[104,256]{1,0:T(8,128)S(1)}, f32[104,256]{1,0:T(8,128)S(1)}, u32[]{:S(2)}, u32[]{:S(2)}) collective-permute-start(f32[104,256]{1,0:T(8,128)S(1)} %get-tuple-element.35), channel_id=1, source_target_pairs={{0,8},{8,16},{16,24},{1,9},{9,17},{17,25},{2,10},{10,18},{18,26},{... | collective-permute-start | bytes 319496 | tf_op jit(solution)/shard_map/ppermute | solution.py:504
  28.2 4.7 %copy-start = (f32[104,256]{1,0:T(8,128)}, f32[104,256]{1,0:T(8,128)S(1)}, u32[]{:S(2)}) copy-start(f32[104,256]{1,0:T(8,128)S(1)} %collective-permute-done.2.north_in) | copy-start | bytes 319492
  29.5 3.4 %copy-start.1 = (f32[104,256]{1,0:T(8,128)}, f32[104,256]{1,0:T(8,128)S(1)}, u32[]{:S(2)}) copy-start(f32[104,256]{1,0:T(8,128)S(1)} %collective-permute-done.3.south_in) | copy-start | bytes 319492
  32.9 20.8 %all-to-all-start = ((f32[8,152,128]{2,1,0:T(8,128)}), f32[8,152,128]{2,1,0:T(8,128)S(1)}, u32[]{:S(2)}, u32[]{:S(2)}) async-start(f32[8,152,128]{2,1,0:T(8,128)} %get-tuple-element.36), calls=%async_computation | async-start | bytes 1245184 | tf_op jit(solution)/shard_map/all_to_all | solution.py:517
  39.7 1.4 %copy-start.4 = (f32[8,8]{1,0:T(8,128)S(1)}, f32[8,8]{1,0:T(8,128)}, u32[]{:S(2)}) copy-start(f32[8,8]{1,0:T(8,128)} %selectivity.7) | copy-start | bytes 772
  39.7 40.6 %collective-permute-start.4 = (f32[152,128]{1,0:T(8,128)}, f32[152,128]{1,0:T(8,128)S(1)}, u32[]{:S(2)}, u32[]{:S(2)}) collective-permute-start(f32[152,128]{1,0:T(8,128)} %get-tuple-element.47), channel_id=1, source_target_pairs={{1,0},{2,1},{3,2},{4,3},{5,4},{6,5},{7,6},{9,8},{10,9},{11,10},{12... | collective-permute-start | bytes 233480 | tf_op jit(solution)/shard_map/ppermute | solution.py:518
  41.1 0.7 copy-start.8
  66.8 13.4 %copy-start.9 = (f32[8,16]{1,0:T(8,128)S(1)}, f32[8,16]{1,0:T(8,128)}, u32[]{:S(2)}) copy-start(f32[8,16]{1,0:T(8,128)} %param.29) | copy-start | bytes 1540
  66.8 22.8 %all-to-all-start.2 = ((f32[64,1,128]{2,1,0:T(1,128)}), f32[64,1,128]{2,1,0:T(1,128)S(1)}, u32[]{:S(2)}, u32[]{:S(2)}) async-start(f32[64,1,128]{2,1,0:T(1,128)} %bitcast.5), calls=%async_computation.2 | async-start | bytes 65536 | tf_op jit(solution)/shard_map/all_to_all | solution.py:541
  91.1 23.5 %all-to-all-start.3 = ((f32[8,152,128]{2,1,0:T(8,128)}), f32[8,152,128]{2,1,0:T(8,128)S(1)}, u32[]{:S(2)}, u32[]{:S(2)}) async-start(f32[8,152,128]{2,1,0:T(8,128)} %get-tuple-element.50), calls=%async_computation.3 | async-start | bytes 1245184 | tf_op jit(solution)/shard_map/all_to_all | solution.py:557

commit v4 on v3

--- a/solution.py
+++ b/solution.py
@@ -6,6 +6,7 @@
 from jax.experimental import pallas as pl
 from jax.experimental.pallas import tpu as pltpu
 from jax.sharding import PartitionSpec as P
+
 
 ROWS, COLS = 64, 256
 EROWS, ECOLS = ROWS + 8, COLS + 128
@@ -17,6 +18,7 @@
 STRIP = 96
 PACKED = 2 * EROWS + 8
 F32 = jnp.float32
+SEPARATE = False
 
 
 def every_field(density, adjoint, effort, mask, east, north, region, sea, habitat):
@@ -113,7 +115,7 @@
 
 
 def picked(received, keep):
-    total = jnp.zeros((PACKED, LANES), F32)
+    total = jnp.zeros(received.shape[1:], F32)
     for slot in range(received.shape[0]):
         total = total + jnp.where(keep(slot), received[slot], 0.0)
     return total
@@ -180,16 +182,20 @@
     east[ROWS + 4 : EROWS, :] = south_in[STRIP : STRIP + 4, LANES:COLS]
 
 
-def narrow_field(ref, index, place, west, east, north_in, south_in, out):
+def own_cells(ref, index, out):
+    core = part(ref, index, slice(0, ROWS), slice(0, COLS))
+    out[0:ROWS, :] = core[:, 0:LANES]
+    out[EROWS : EROWS + ROWS, :] = core[:, LANES:COLS]
+
+
+def halo_cells(place, west, east, north_in, south_in):
     width = NARROW
-    core = part(ref, index, slice(0, ROWS), slice(0, COLS))
+    tiles = []
     for half in range(2):
         cols = slice(LANES * half, LANES * half + LANES)
-        top = EROWS * half
-        out[top : top + ROWS, :] = core[:, cols]
-        out[top + ROWS : top + EROWS, :] = jnp.zeros((8, LANES), F32)
-        out[top + ROWS : top + ROWS + width, :] = north_in[place : place + width, cols]
-        out[top + EROWS - width : top + EROWS, :] = south_in[place : place + width, cols]
+        blank = jnp.zeros((8 - 2 * width, LANES), F32)
+        rows = slice(place, place + width)
+        tiles.append(jnp.concatenate([north_in[rows, cols], blank, south_in[rows, cols]], axis=0))
     lane = lane_iota(8)
     packed = jnp.zeros((8, LANES), F32)
     for k in range(EROWS // 8):
@@ -198,13 +204,105 @@
         packed = jnp.where(here, turned(west[rows, :], 4 * k - place), packed)
         here = (lane >= 4 * k + width) & (lane < 4 * k + 4)
         packed = jnp.where(here, turned(east[rows, :], 4 * k + width - place), packed)
+    tiles.append(packed)
+    return tiles
+
+
+HALO_ROWS = (ROWS, EROWS + ROWS, 2 * EROWS)
+
+
+def narrow_field(ref, index, place, west, east, north_in, south_in, out):
+    own_cells(ref, index, out)
+    for top, tile in zip(HALO_ROWS, halo_cells(place, west, east, north_in, south_in), strict=True):
+        out[top : top + 8, :] = tile
+
+
+def summed_settled(densities, flow, swim, spread, mass):
+    sums = [0.0] * 6
+    for c in range(N):
+        u, d, s = densities[c], spread[c], swim[c]
+        factors = (mass[c], mass[c] * d, mass[c] * s, mass[c] * d * d, mass[c] * d * s, mass[c] * s * s)
+        sums = [total + factor * u for total, factor in zip(sums, factors, strict=True)]
+    rate, sea = rates(flow), flow[2]
+    out_rate = (rate[0] + rate[1]) + (rate[2] + rate[3])
+    first = [
+        sea * (sums[a] + spreading(sums[b]) + drifting(sums[c], rate, out_rate))
+        for a, b, c in ((0, 1, 2), (1, 3, 4), (2, 4, 5))
+    ]
+    return sea * (first[0] + spreading(first[1]) + drifting(first[2], rate, out_rate))
+
+
+def inner_kernel(density, current_east, current_north, sea_mask, after, swim, spread, mass, total_out):
+    del after
+    flow = (current_east[...], current_north[...], sea_mask[...].astype(F32))
+    total = summed_settled(density, flow, swim, spread, mass)
+    slots = total_out.shape[0]
+    at_all(total_out, slots, slice(0, ROWS), total[:, 0:LANES])
+    at_all(total_out, slots, slice(ROWS, 2 * ROWS), total[:, LANES:COLS])
+
+
+def ring_of(total):
+    row = lax.broadcasted_iota(jnp.int32, (8, LANES), 0)
+    outer = (row < 2) | (row >= 6)
+    parts = []
+    for half in range(2):
+        cols = slice(LANES * half, LANES * half + LANES)
+        edge = jnp.where(row < 2, total[0:8, cols], total[ROWS - 8 : ROWS, cols])
+        parts.append(jnp.where(outer, total[ROWS:EROWS, cols], pltpu.roll(edge, 4, 0)))
+    lane = lane_iota(8)
+    sides = jnp.zeros((8, LANES), F32)
+    for k in range(EROWS // 8):
+        rows = slice(8 * k, 8 * k + 8)
+        low, high = total[rows, 0:LANES], total[rows, LANES:COLS]
+        side = total[rows, COLS:ECOLS]
+        base = 8 * k
+        for offset, tile, by in (
+            (0, high, base - (LANES - 2)),
+            (2, side, base + 2),
+            (4, side, base + 4 - (LANES - 2)),
+            (6, low, base + 6),
+        ):
+            here = (lane >= base + offset) & (lane < base + offset + 2)
+            sides = jnp.where(here, turned(tile, by), sides)
+    parts.append(sides)
+    return parts
+
+
+def with_ring(inner, ring, out):
+    row = lax.broadcasted_iota(jnp.int32, (8, LANES), 0)
+    lane = lane_iota(8)
+    sides = ring[16:24]
+    for half in range(2):
+        lat = ring[8 * half : 8 * half + 8]
+        edge = pltpu.roll(lat, 4, 0)
+        for k in range(EROWS // 8):
+            if k < ROWS // 8:
+                tile = inner[ROWS * half + 8 * k : ROWS * half + 8 * k + 8]
+            else:
+                tile = lat
+            if k == 0:
+                tile = jnp.where(row < 2, edge, tile)
+            if k == ROWS // 8 - 1:
+                tile = jnp.where(row >= 6, edge, tile)
+            if half == 0:
+                tile = jnp.where(lane < 2, turned(sides, -(8 * k + 6)), tile)
+            else:
+                tile = jnp.where(lane >= LANES - 2, turned(sides, LANES - 2 - 8 * k), tile)
+            out[EROWS * half + 8 * k : EROWS * half + 8 * k + 8, :] = tile
+    packed = jnp.zeros((8, LANES), F32)
+    for k in range(EROWS // 8):
+        here = (lane >= 4 * k) & (lane < 4 * k + 2)
+        packed = jnp.where(here, turned(sides, -(4 * k + 4)), packed)
+        here = (lane >= 4 * k + 2) & (lane < 4 * k + 4)
+        packed = jnp.where(here, turned(sides, -4 * k), packed)
     out[2 * EROWS : PACKED, :] = packed
 
 
 def total_kernel(
-    density, current_east, current_north, sea_mask, adjoint, west_in, east_in, north_in, south_in, swim, spread, mass,
-    total_out, tail_out, density_out, flow_out, west, east,
+    density, current_east, current_north, sea_mask, adjoint, west_in, east_in, north_in, south_in, after, after_too,
+    swim, spread, mass, total_out, tail_out, density_out, flow_out, west, east,
 ):
+    del after, after_too
     strips(west_in, east_in, north_in, south_in, west, east)
     narrow_field(adjoint, 0, ADJOINT, west, east, north_in, south_in, tail_out)
     lane = lane_iota(EROWS)
@@ -218,55 +316,62 @@
         side = jnp.where(lane < WIDE, turned(east[...], -place), 0.0)
         side = jnp.where(lane >= LANES - WIDE, turned(west[...], LANES - WIDE - place), side)
         out[:, COLS:ECOLS] = side
-    sums = [jnp.zeros((EROWS, ECOLS), F32) for _ in range(6)]
+    total = summed_settled(density_out, flow_out, swim, spread, mass)
+    for k, ring in enumerate(ring_of(total)):
+        at_all(total_out, total_out.shape[0], slice(8 * k, 8 * k + 8), ring)
+
+
+def fleet_rows(rows, efforts, reported_out, fishing_out, mortality, selectivity):
+    harvest = [efforts[f, rows, :] for f in range(N)]
+    for f in range(N):
+        reported_out[f, rows, :] = reported_out[f, rows, :] * harvest[f]
     for c in range(N):
-        u, d, s = density_out[c], spread[c], swim[c]
-        factors = (mass[c], mass[c] * d, mass[c] * s, mass[c] * d * d, mass[c] * d * s, mass[c] * s * s)
-        sums = [total + factor * u for total, factor in zip(sums, factors, strict=True)]
-    rate, sea = rates(flow_out), flow_out[2]
-    out_rate = (rate[0] + rate[1]) + (rate[2] + rate[3])
-    first = [
-        sea * (sums[a] + spreading(sums[b]) + drifting(sums[c], rate, out_rate))
-        for a, b, c in ((0, 1, 2), (1, 3, 4), (2, 4, 5))
-    ]
-    total = sea * (first[0] + spreading(first[1]) + drifting(first[2], rate, out_rate))
-    slots = total_out.shape[0]
-    at_all(total_out, slots, slice(0, EROWS), total[:, 0:LANES])
-    at_all(total_out, slots, slice(EROWS, 2 * EROWS), total[:, LANES:COLS])
-    sides = [total[8 * k : 8 * k + 8, COLS:ECOLS] for k in range(EROWS // 8)]
-    at_all(total_out, slots, slice(2 * EROWS, PACKED), packed_side(sides))
+        fishing = mortality[c] + selectivity[0, c] * harvest[0]
+        for f in range(1, N):
+            fishing = fishing + selectivity[f, c] * harvest[f]
+        fishing_out[c, rows, :] = fishing
 
 
 def fleet_kernel(
-    adjoint, effort, mask, region, habitat, west_in, east_in, north_in, south_in, density, flow,
+    effort, mask, region, after, mortality, selectivity, fishing_out, reported_out, region_out, efforts
+):
+    del after
+    for k in range(N):
+        own_cells(effort, k, efforts.at[k])
+        own_cells(mask, k, reported_out.at[k])
+    own_cells(region, None, region_out)
+
+    def tile(t, carry):
+        for top in (0, EROWS):
+            rows = pl.ds(pl.multiple_of(top + t * 8, 8), 8)
+            fleet_rows(rows, efforts, reported_out, fishing_out, mortality, selectivity)
+        return carry
+
+    lax.fori_loop(0, ROWS // 8, tile, 0)
+
+
+def settle_kernel(
+    fishing, reported, region, adjoint, habitat, west_in, east_in, north_in, south_in, density, flow,
     swim, spread, mortality, selectivity,
     settled_out, fishing_out, reported_out, region_out, carried_out, habitat_out, west, east, efforts,
 ):
+    for source, out in ((fishing, fishing_out), (reported, reported_out), (region, region_out)):
+        if SEPARATE:
+            out[...] = source[...]
     strips(west_in, east_in, north_in, south_in, west, east)
 
-    def narrow(ref, index, place, out):
-        narrow_field(ref, index, place, west, east, north_in, south_in, out)
+    def halo(place, out):
+        for top, tile in zip(HALO_ROWS, halo_cells(place, west, east, north_in, south_in), strict=True):
+            out[top : top + 8, :] = tile
 
     for k in range(N):
-        narrow(adjoint, k, ADJOINT + NARROW * k, carried_out.at[k])
-        narrow(effort, k, EFFORT + NARROW * k, efforts.at[k])
-        narrow(mask, k, MASK + NARROW * k, reported_out.at[k])
-    narrow(region, None, REGION, region_out)
-    narrow(habitat, None, HABITAT, habitat_out)
-
-    def tile(t, carry):
-        rows = pl.ds(pl.multiple_of(t * 8, 8), 8)
-        harvest = [efforts[f, rows, :] for f in range(N)]
-        for f in range(N):
-            reported_out[f, rows, :] = reported_out[f, rows, :] * harvest[f]
-        for c in range(N):
-            fishing = mortality[c] + selectivity[0, c] * harvest[0]
-            for f in range(1, N):
-                fishing = fishing + selectivity[f, c] * harvest[f]
-            fishing_out[c, rows, :] = fishing
-        return carry
-
-    lax.fori_loop(0, PACKED // 8, tile, 0)
+        narrow_field(adjoint, k, ADJOINT + NARROW * k, west, east, north_in, south_in, carried_out.at[k])
+        halo(EFFORT + NARROW * k, efforts.at[k])
+        halo(MASK + NARROW * k, reported_out.at[k])
+    halo(REGION, region_out)
+    narrow_field(habitat, None, HABITAT, west, east, north_in, south_in, habitat_out)
+    for top in HALO_ROWS:
+        fleet_rows(slice(top, top + 8), efforts, reported_out, fishing_out, mortality, selectivity)
 
     def cohort(c, carry):
         coefs, sea = coeffs(flow, swim[c], spread[c]), flow[2]
@@ -277,10 +382,10 @@
 
 
 def catch_kernel(
-    age, received, settled, fishing, reported, region, mass, selectivity, mort_out, catch_out, older, fleets
+    age, received, ring, settled, fishing, reported, region, mass, selectivity, mort_out, catch_out, older, fleets
 ):
     shard = age[0]
-    older[...] = picked(received, lambda slot: slot > shard)
+    with_ring(picked(received, lambda slot: slot > shard), picked(ring, lambda slot: slot > shard), older)
 
     def pair(t, carry):
         places = [pl.ds(pl.multiple_of(t * 8, 8), 8), pl.ds(pl.multiple_of(EROWS + t * 8, 8), 8)]
@@ -460,19 +565,19 @@
     return [pltpu.with_memory_space_constraint(x, pltpu.HBM) for x in arrays]
 
 
-def call(kernel, name, in_specs, outs, scratch=()):
+def call(kernel, in_specs, outs, scratch=(), aliases=None):
     return pl.pallas_call(
         kernel,
-        name=name,
         in_specs=in_specs,
         out_specs=[VMEM] * len(outs),
         out_shape=outs,
         scratch_shapes=[pltpu.VMEM(dims, F32) for dims in scratch],
+        input_output_aliases=aliases or {},
         compiler_params=pltpu.CompilerParams(vmem_limit_bytes=24 << 20),
     )
 
 
-def local(
+def month(
     density, adjoint_next, current_east, current_north, swim_speed, diffusion, mortality, cohort_mass,
     selectivity, effort, catch_mask, region, sea_mask, habitat, observed,
 ):
@@ -486,12 +591,17 @@
 
     to_east, to_west, to_north, to_south = call(
         pack_kernel,
-        "pack",
         [VMEM] * 9,
         [shape(ROWS, LANES), shape(ROWS, LANES), shape(strip_rows, COLS), shape(strip_rows, COLS)],
     )(*inputs)
     from_west = lax.ppermute(to_east, "lon", [(i, (i + 1) % lons) for i in range(lons)])
     from_east = lax.ppermute(to_west, "lon", [((i + 1) % lons, i) for i in range(lons)])
+    packed = (PACKED, LANES)
+    extended = (EROWS, ECOLS)
+    (inner,) = call(
+        inner_kernel, [VMEM] * 5 + [SMEM] * 3, [shape(ages, 2 * ROWS, LANES)]
+    )(density, current_east, current_north, sea_mask, near(to_east), swim_speed, diffusion, cohort_mass)
+    inner = lax.all_to_all(inner, "age", 0, 0, tiled=True)
     to_north, to_south = pl.pallas_call(
         corner_kernel,
         name="corner",
@@ -505,71 +615,56 @@
     from_north = lax.ppermute(to_south, "lat", [(i + 1, i) for i in range(lats - 1)])
     halos = (from_west, from_east, from_north, from_south)
 
-    packed = (PACKED, LANES)
-    extended = (EROWS, ECOLS)
-    totals, tail, density_ext, flow = call(
+    fishing, reported, regions = call(
+        fleet_kernel, [VMEM] * 4 + [SMEM] * 2, [shape(N, *packed)] * 2 + [shape(*packed)], [(N, *packed)]
+    )(effort, catch_mask, region, near(to_north), mortality, selectivity)
+    ring, tail, density_ext, flow = call(
         total_kernel,
-        "total",
-        [VMEM] * 9 + [SMEM] * 3,
-        [shape(ages, *packed), shape(*packed), shape(N, *extended), far(3, *extended)],
+        [VMEM] * 11 + [SMEM] * 3,
+        [shape(ages, 24, LANES), shape(*packed), shape(N, *extended), far(3, *extended)],
         [(EROWS, LANES), (EROWS, LANES)],
-    )(density, current_east, current_north, sea_mask, adjoint_next, *map(near, halos), swim_speed, diffusion, cohort_mass)
-    totals = lax.all_to_all(totals, "age", 0, 0, tiled=True)
+    )(
+        density, current_east, current_north, sea_mask, adjoint_next, *map(near, halos), near(inner), near(regions),
+        swim_speed, diffusion, cohort_mass,
+    )
+    ring = lax.all_to_all(ring, "age", 0, 0, tiled=True)
     tail = lax.ppermute(tail, "age", [(i + 1, i) for i in range(ages - 1)])
 
     settled, fishing, reported, regions, carried, habitats = call(
-        fleet_kernel,
-        "fleet",
+        settle_kernel,
         [VMEM] * 11 + [SMEM] * 4,
         [shape(N, *packed)] * 3 + [shape(*packed), far(N, *packed), far(*packed)],
         [(EROWS, LANES), (EROWS, LANES), (N, *packed)],
+        {0: 1, 1: 2, 2: 3},
     )(
-        adjoint_next, effort, catch_mask, region, habitat, *distant(*halos), near(density_ext), *distant(flow),
-        swim_speed, diffusion, mortality, selectivity,
+        near(fishing), near(reported), near(regions), adjoint_next, habitat,
+        *distant(*halos), near(density_ext), *distant(flow), swim_speed, diffusion, mortality, selectivity,
     )
     settled, reported, regions = near(settled), near(reported), near(regions)
 
     mort, catches = call(
-        catch_kernel,
-        "catch",
-        [SMEM] + [VMEM] * 5 + [SMEM] * 2,
-        [shape(N, *packed), shape(ages, LANES)],
-        [packed, (N, *packed)],
-    )(age, near(totals), settled, near(fishing), reported, regions, cohort_mass, selectivity)
+        catch_kernel, [SMEM] + [VMEM] * 6 + [SMEM] * 2, [shape(N, *packed), shape(ages, LANES)], [packed, (N, *packed)]
+    )(age, near(inner), near(ring), settled, near(fishing), reported, regions, cohort_mass, selectivity)
     catches = near(lax.all_to_all(catches, "age", 0, 0, tiled=True))
-    (catches,) = call(relay_kernel, "relay", [VMEM], [shape(lons * lats, LANES)])(catches)
+    (catches,) = call(relay_kernel, [VMEM], [shape(lons * lats, LANES)])(catches)
     catches = near(lax.all_to_all(catches, ("lon", "lat"), 0, 0, tiled=True))
 
     still, reach, kept, yields, slope = call(
-        slope_kernel,
-        "slope",
-        [SMEM] + [VMEM] * 6 + [SMEM] * 2,
-        [shape(*packed), shape(N, *packed)] + [far(N, *packed)] * 3,
+        slope_kernel, [SMEM] + [VMEM] * 6 + [SMEM] * 2, [shape(*packed), shape(N, *packed)] + [far(N, *packed)] * 3
     )(age, near(mort), settled, reported, *distant(carried, habitats), near(tail), cohort_mass, selectivity)
 
     unit = observed.shape[1] / (ROWS * COLS * lons * lats)
     misfit, totals = call(
-        functools.partial(press_kernel, unit=unit),
-        "press",
-        [VMEM] * 5,
-        [shape(8, LANES), shape(ages, *packed)],
+        functools.partial(press_kernel, unit=unit), [VMEM] * 5, [shape(8, LANES), shape(ages, *packed)]
     )(catches, observed.reshape(1, LANES), regions, near(still), near(reach))
     totals = lax.all_to_all(totals, "age", 0, 0, tiled=True)
 
     kept, yields, slope, flow = distant(kept, yields, slope, flow)
     (own,) = call(
-        own_kernel,
-        "own",
-        [VMEM] * 8 + [SMEM] * 4,
-        [shape(N, ROWS, COLS)],
-        [(N, *packed), extended],
+        own_kernel, [VMEM] * 8 + [SMEM] * 4, [shape(N, ROWS, COLS)], [(N, *packed), extended]
     )(near(misfit), regions, reported, settled, kept, yields, slope, flow, swim_speed, diffusion, cohort_mass, selectivity)
     (grad,) = call(
-        final_kernel,
-        "final",
-        [SMEM] + [VMEM] * 3 + [SMEM] * 3,
-        [far(N, ROWS, COLS)],
-        [extended, (6, ROWS, COLS)],
+        final_kernel, [SMEM] + [VMEM] * 3 + [SMEM] * 3, [far(N, ROWS, COLS)], [extended, (6, ROWS, COLS)]
     )(age, near(totals), near(own), flow, swim_speed, diffusion, cohort_mass)
     return grad
 
@@ -592,6 +687,4 @@
         P("lat", "lon"),
         P(),
     )
-    return jax.shard_map(
-        local, mesh=mesh, in_specs=placed, out_specs=P("age", "lat", "lon"), check_vma=False
-    )
+    return jax.shard_map(month, mesh=mesh, in_specs=placed, out_specs=P("age", "lat", "lon"), check_vma=False)

time: 118 us -> 126 us (1.068)
  blocking collectives: 8.92 us -> 12.6 us
  Pallas kernels: 28.9 us -> 32.1 us
  starting transfers between devices: 49.5 us -> 51.4 us
    all_to_all x3 -> x4, waiting for transfers between devices: 26 us -> 21.3 us  [the longest x1 14 us: month(): totals = lax.all_to_all(totals, 'age', 0, 0, tiled=True)]
    ppermute x5, waiting for transfers between devices: 2.68 us -> 7.18 us  [the longest x1 6.19 us: month(): lax.ppermute(to_south, 'lat', [(i + 1, i) for i in range(lats - 1)])]
    all_to_all x1, blocking collectives: 8.92 us -> 12.6 us  [month(): catches = near(lax.all_to_all(catches, 'age', 0, 0, tiled=True))]
    pallas_call x10 -> x12, Pallas kernels: 28.9 us -> 32.1 us  [the longest x1 5.93 us: month(): call(own_kernel, [VMEM] * 8 + [SMEM] * 4, [shape(N, ROWS, COLS)], [(N, *p...]
    all_to_all x3 -> x4, starting transfers between devices: 23.8 us -> 26.4 us  [the longest x1 8.3 us: month(): catches = near(lax.all_to_all(catches, ('lon', 'lat'), 0, 0, tiled=True))]
  transfers between devices with their start and end apart: 8 -> 9, of which waited for: 6 -> 5; matrix products, arithmetic and copies ran while one was open for 0% -> 0% of each run, Pallas kernels for 17% -> 16%
where the time goes in v4:
time: 126 us
  starting transfers between devices  51.4 us (41%)
  Pallas kernels  32.1 us (25%)
  waiting for transfers between devices  28.5 us (23%)
  blocking collectives  12.6 us (10%)
    all_to_all x1, waiting for transfers between devices, month(): totals = lax.all_to_all(totals, 'age', 0, 0, tiled=True)  14 us
    all_to_all x1, blocking collectives, month(): catches = near(lax.all_to_all(catches, 'age', 0, 0, tiled=True))  12.6 us
    ppermute x1, starting transfers between devices, month(): lax.ppermute(to_north, 'lat', [(i, i + 1) for i in range(lats - 1)])  10.1 us
    all_to_all x1, starting transfers between devices, month(): catches = near(lax.all_to_all(catches, ('lon', 'lat'), 0, 0, tiled=True))  8.3 us
    ppermute x1, starting transfers between devices, month(): lax.ppermute(to_west, 'lon', [((i + 1) % lons, i) for i in range(lons)])  7.73 us
    all_to_all x1, starting transfers between devices, month(): inner = lax.all_to_all(inner, 'age', 0, 0, tiled=True)  7.64 us
    all_to_all x1, starting transfers between devices, month(): ring = lax.all_to_all(ring, 'age', 0, 0, tiled=True)  6.94 us
    ppermute x1, waiting for transfers between devices, month(): lax.ppermute(to_south, 'lat', [(i + 1, i) for i in range(lats - 1)])  6.19 us
  transfers between devices with their start and end apart: 9, of which 5 were waited for; matrix products, arithmetic and copies ran while one was open for 0% of the time, Pallas kernels for 16%

profile of v4, /device:TPU:1, one launch (start us, length us, event | category | flops | bytes accessed | tf_op | source)
XLA Modules:
  0.0 125.6 jit_solution(12684002228497343642)
XLA Ops:
  0.0 2.3 %shard_map.145 = (f32[64,128]{1,0:T(8,128)S(1)}, f32[64,128]{1,0:T(8,128)S(1)}, f32[104,256]{1,0:T(8,128)S(1)}, f32[104,256]{1,0:T(8,128)S(1)}) custom-call(f32[8,64,256]{2,1,0:T(8,128)} %density.3, f32[8,64,256]{2,1,0:T(8,128)} %adjoint.3, f32[8,64,256]{2,1,0:T(8,128)} %effort.1, s32[8,64,256]{2,1,0:T(8,128)} %mask.1, f32[64,256]{1,0:T(8,128)} %current_east.3, ...), custom_call_target="tpu_custom_call" | custom-call | tf_op jit(solution)/shard_map/pallas_call | solution.py:592
  3.0 2.5 %shard_map.146 = f32[8,128,128]{2,1,0:T(8,128)} custom-call(f32[8,64,256]{2,1,0:T(8,128)} %density.3, f32[64,256]{1,0:T(8,128)} %current_east.3, f32[64,256]{1,0:T(8,128)} %current_north.3, s32[64,256]{1,0:T(8,128)} %sea_mask.3, f32[64,128]{1,0:T(8,128)S(1)} %get-tuple-element.33.after, f32[8]{0:T(128)S(1)} %copy-done.6, f32[8]{0:T(128)S(1)} %copy-done.7, ...), custom_call_target="tpu_custom_call" | custom-call | tf_op jit(solution)/shard_map/pallas_call | solution.py:601
  5.5 7.6 %all-to-all-start = ((f32[8,128,128]{2,1,0:T(8,128)}), f32[8,128,128]{2,1,0:T(8,128)S(1)}, u32[]{:S(2)}, u32[]{:S(2)}) async-start(f32[8,128,128]{2,1,0:T(8,128)} %shard_map.146), calls=%async_computation | async-start | bytes 1048576 | tf_op jit(solution)/shard_map/all_to_all | solution.py:604
  13.1 4.0 %collective-permute-start = (f32[64,128]{1,0:T(8,128)S(1)}, f32[64,128]{1,0:T(8,128)S(1)}, u32[]{:S(2)}, u32[]{:S(2)}) collective-permute-start(f32[64,128]{1,0:T(8,128)S(1)} %get-tuple-element.33.after), channel_id=1, source_target_pairs={{0,32},{32,64},{64,96},{96,128},{128,160},{160,192},{192,224},{224... | collective-permute-start | bytes 98312 | tf_op jit(solution)/shard_map/ppermute | solution.py:597
  17.1 7.7 %collective-permute-start.1 = (f32[64,128]{1,0:T(8,128)S(1)}, f32[64,128]{1,0:T(8,128)S(1)}, u32[]{:S(2)}, u32[]{:S(2)}) collective-permute-start(f32[64,128]{1,0:T(8,128)S(1)} %get-tuple-element.34), channel_id=1, source_target_pairs={{32,0},{64,32},{96,64},{128,96},{160,128},{192,160},{224,192},{256... | collective-permute-start | bytes 98312 | tf_op jit(solution)/shard_map/ppermute | solution.py:598
  25.9 10.1 %collective-permute-start.3 = (f32[104,256]{1,0:T(8,128)S(1)}, f32[104,256]{1,0:T(8,128)S(1)}, u32[]{:S(2)}, u32[]{:S(2)}) collective-permute-start(f32[104,256]{1,0:T(8,128)S(1)} %get-tuple-element.38.after), channel_id=1, source_target_pairs={{0,8},{8,16},{16,24},{1,9},{9,17},{17,25},{2,10},{10,18},{18,26},{... | collective-permute-start | bytes 319496 | tf_op jit(solution)/shard_map/ppermute | solution.py:614
  35.9 1.9 %collective-permute-start.2 = (f32[104,256]{1,0:T(8,128)S(1)}, f32[104,256]{1,0:T(8,128)S(1)}, u32[]{:S(2)}, u32[]{:S(2)}) collective-permute-start(f32[104,256]{1,0:T(8,128)S(1)} %get-tuple-element.37), channel_id=1, source_target_pairs={{8,0},{16,8},{24,16},{9,1},{17,9},{25,17},{10,2},{18,10},{26,18},{... | collective-permute-start | bytes 319496 | tf_op jit(solution)/shard_map/ppermute | solution.py:615
  37.9 1.8 %shard_map.147 = (f32[8,152,128]{2,1,0:T(8,128)S(1)}, f32[8,152,128]{2,1,0:T(8,128)S(1)}, f32[152,128]{1,0:T(8,128)S(1)}) custom-call(f32[8,64,256]{2,1,0:T(8,128)} %effort.1, s32[8,64,256]{2,1,0:T(8,128)} %mask.1, s32[64,256]{1,0:T(8,128)} %region.1, f32[104,256]{1,0:T(8,128)S(1)} %get-tuple-element.38.after, f32[8]{0:T(128)S(1)} %copy-done.8, ...), custom_call_target="tpu_custom_call" | custom-call | tf_op jit(solution)/shard_map/pallas_call | solution.py:618
  39.7 6.2 %collective-permute-done.2.north_in = f32[104,256]{1,0:T(8,128)S(1)} collective-permute-done((f32[104,256]{1,0:T(8,128)S(1)}, f32[104,256]{1,0:T(8,128)S(1)}, u32[]{:S(2)}, u32[]{:S(2)}) %collective-permute-start.2) | collective-permute-done | bytes 106528 | tf_op jit(solution)/shard_map/ppermute | solution.py:615
  45.9 3.3 %shard_map.148 = (f32[8,24,128]{2,1,0:T(8,128)}, f32[152,128]{1,0:T(8,128)}, f32[8,72,384]{2,1,0:T(8,128)S(1)}, f32[3,72,384]{2,1,0:T(8,128)}) custom-call(f32[8,64,256]{2,1,0:T(8,128)} %density.3, f32[64,256]{1,0:T(8,128)} %current_east.3, f32[64,256]{1,0:T(8,128)} %current_north.3, s32[64,256]{1,0:T(8,128)} %sea_mask.3, f32[8,64,256]{2,1,0:T(8,128)} %adjoint.3, ...), custom_call_target="tpu_custom_call" | custom-call | tf_op jit(solution)/shard_map/pallas_call | solution.py:621
  49.2 6.9 %all-to-all-start.1 = ((f32[8,24,128]{2,1,0:T(8,128)}), f32[8,24,128]{2,1,0:T(8,128)S(1)}, u32[]{:S(2)}, u32[]{:S(2)}) async-start(f32[8,24,128]{2,1,0:T(8,128)} %get-tuple-element.40), calls=%async_computation.1 | async-start | bytes 196608 | tf_op jit(solution)/shard_map/all_to_all | solution.py:630
  56.1 1.3 %collective-permute-start.4 = (f32[152,128]{1,0:T(8,128)}, f32[152,128]{1,0:T(8,128)}, u32[]{:S(2)}, u32[]{:S(2)}) collective-permute-start(f32[152,128]{1,0:T(8,128)} %get-tuple-element.53), channel_id=1, source_target_pairs={{1,0},{2,1},{3,2},{4,3},{5,4},{6,5},{7,6},{9,8},{10,9},{11,10},{12... | collective-permute-start | bytes 233480 | tf_op jit(solution)/shard_map/ppermute | solution.py:631
  57.5 4.9 %shard_map.149 = (f32[8,152,128]{2,1,0:T(8,128)S(1)}, f32[8,152,128]{2,1,0:T(8,128)S(1)}, f32[8,152,128]{2,1,0:T(8,128)S(1)}, f32[152,128]{1,0:T(8,128)S(1)}, f3...) custom-call(f32[8,152,128]{2,1,0:T(8,128)S(1)} %get-tuple-element.41.fishing,, ...), custom_call_target="tpu_custom_call", output_to_operand_aliasing={{1}: (0, {}), {2}: (1, {}), {3}: (2, {})} | custom-call | tf_op jit(solution)/shard_map/pallas_call | solution.py:633
  62.3 1.3 %all-to-all-done.1.ring = f32[8,24,128]{2,1,0:T(8,128)S(1)} async-done(((f32[8,24,128]{2,1,0:T(8,128)}), f32[8,24,128]{2,1,0:T(8,128)S(1)}, u32[]{:S(2)}, u32[]{:S(2)}) %all-to-all-start.1) | async-done | bytes 98336 | tf_op jit(solution)/shard_map/all_to_all | solution.py:630
  63.7 3.6 %shard_map.150 = (f32[8,152,128]{2,1,0:T(8,128)S(1)}, f32[8,128]{1,0:T(8,128)S(1)}) custom-call(s32[2]{0:T(128)S(1)} %pad_add_fusion.age, f32[8,128,128]{2,1,0:T(8,128)S(1)} %all-to-all-done.after.received, f32[8,24,128]{2,1,0:T(8,128)S(1)} %all-to-all-done.1.ring, f32[8,152,128]{2,1,0:T(8,128)S(1)} %get-tuple-element.45.settled, ...), custom_call_target="tpu_custom_call" | custom-call | tf_op jit(solution)/shard_map/pallas_call | solution.py:645
  67.3 12.6 %all_to_all.37 = f32[8,1,128]{2,1,0:T(1,128)S(1)} all-to-all(f32[8,1,128]{2,1,0:T(1,128)S(1)} %bitcast.11), channel_id=1, replica_groups=mesh['lon'=16,'lat'=4,'age'=8] {'age'}, dimensions={0} | all-to-all | bytes 8192 | tf_op jit(solution)/shard_map/all_to_all | solution.py:648
  80.5 8.3 %all-to-all-start.3 = ((f32[64,1,128]{2,1,0:T(1,128)}), f32[64,1,128]{2,1,0:T(1,128)S(1)}, u32[]{:S(2)}, u32[]{:S(2)}) async-start(f32[64,1,128]{2,1,0:T(1,128)} %bitcast.5), calls=%async_computation.3 | async-start | bytes 65536 | tf_op jit(solution)/shard_map/all_to_all | solution.py:650
  88.9 3.4 %shard_map.152 = (f32[152,128]{1,0:T(8,128)S(1)}, f32[8,152,128]{2,1,0:T(8,128)S(1)}, f32[8,152,128]{2,1,0:T(8,128)}, f32[8,152,128]{2,1,0:T(8,128)}, f32[8,152,128]{2,1,0:T(8,128)}) custom-call(s32[2]{0:T(128)S(1)} %pad_add_fusion.age, f32[8,152,128]{2,1,0:T(8,128)S(1)} %get-tuple-element.50.mort, f32[8,152,128]{2,1,0:T(8,128)S(1)} %get-tuple-element.45.settled, ...), custom_call_target="tpu_custom_call" | custom-call | tf_op jit(solution)/shard_map/pallas_call | solution.py:652
  92.3 5.9 %all-to-all-done.3 = f32[64,1,128]{2,1,0:T(1,128)S(1)} async-done(((f32[64,1,128]{2,1,0:T(1,128)}), f32[64,1,128]{2,1,0:T(1,128)S(1)}, u32[]{:S(2)}, u32[]{:S(2)}) %all-to-all-start.3) | async-done | bytes 32800 | tf_op jit(solution)/shard_map/all_to_all | solution.py:650
  98.2 1.4 %shard_map.153 = (f32[8,128]{1,0:T(8,128)S(1)}, f32[8,152,128]{2,1,0:T(8,128)}) custom-call(f32[64,128]{1,0:T(8,128)S(1)} %bitcast.9, f32[1,128]{1,0:T(1,128)S(1)} %reshape.7.observed, f32[152,128]{1,0:T(8,128)S(1)} %get-tuple-element.48.region, f32[152,128]{1,0:T(8,128)S(1)} %get-tuple-element.54.still, f32[8,152,128]{2,1,0:T(8,128)S(1)} %get-tuple-element.55.reach), custom_call_target="tpu_custom_call" | custom-call | tf_op jit(solution)/shard_map/pallas_call | solution.py:657
  99.6 3.5 %all-to-all-start.4 = ((f32[8,152,128]{2,1,0:T(8,128)}), f32[8,152,128]{2,1,0:T(8,128)S(1)}, u32[]{:S(2)}, u32[]{:S(2)}) async-start(f32[8,152,128]{2,1,0:T(8,128)} %get-tuple-element.56), calls=%async_computation.4 | async-start | bytes 1245184 | tf_op jit(solution)/shard_map/all_to_all | solution.py:660
  103.1 5.9 %shard_map.154.own = f32[8,64,256]{2,1,0:T(8,128)S(1)} custom-call(f32[8,128]{1,0:T(8,128)S(1)} %get-tuple-element.57.misfit_in, f32[152,128]{1,0:T(8,128)S(1)} %get-tuple-element.48.region, f32[8,152,128]{2,1,0:T(8,128)S(1)} %get-tuple-element.47.reported, f32[8,152,128]{2,1,0:T(8,128)S(1)} %get-tuple-element.45.settled, ...), custom_call_target="tpu_custom_call" | custom-call | tf_op jit(solution)/shard_map/pallas_call | solution.py:663
  109.1 14.0 %all-to-all-done.4.received = f32[8,152,128]{2,1,0:T(8,128)S(1)} async-done(((f32[8,152,128]{2,1,0:T(8,128)}), f32[8,152,128]{2,1,0:T(8,128)S(1)}, u32[]{:S(2)}, u32[]{:S(2)}) %all-to-all-start.4) | async-done | bytes 622624 | tf_op jit(solution)/shard_map/all_to_all | solution.py:660
  123.1 2.5 %shard_map.155 = f32[8,64,256]{2,1,0:T(8,128)} custom-call(s32[2]{0:T(128)S(1)} %pad_add_fusion.age, f32[8,152,128]{2,1,0:T(8,128)S(1)} %all-to-all-done.4.received, f32[8,64,256]{2,1,0:T(8,128)S(1)} %shard_map.154.own, f32[3,72,384]{2,1,0:T(8,128)} %get-tuple-element.44.flow, f32[8]{0:T(128)S(1)} %copy-done.6, f32[8]{0:T(128)S(1)} %copy-done.7, f32[8]{0:T(128)S(1)} %copy-done.5), custom_call_target="tpu_custom_call" | custom-call | tf_op jit(solution)/shard_map/pallas_call | solution.py:666
  (29 shorter events, 2.5 us)
Async XLA Ops:
  2.3 0.7 copy-start.5
  2.3 0.7 copy-start.6
  2.3 0.7 copy-start.7
  5.5 40.4 %all-to-all-start = ((f32[8,128,128]{2,1,0:T(8,128)}), f32[8,128,128]{2,1,0:T(8,128)S(1)}, u32[]{:S(2)}, u32[]{:S(2)}) async-start(f32[8,128,128]{2,1,0:T(8,128)} %shard_map.146), calls=%async_computation | async-start | bytes 1048576 | tf_op jit(solution)/shard_map/all_to_all | solution.py:604
  13.1 11.7 %collective-permute-start = (f32[64,128]{1,0:T(8,128)S(1)}, f32[64,128]{1,0:T(8,128)S(1)}, u32[]{:S(2)}, u32[]{:S(2)}) collective-permute-start(f32[64,128]{1,0:T(8,128)S(1)} %get-tuple-element.33.after), channel_id=1, source_target_pairs={{0,32},{32,64},{64,96},{96,128},{128,160},{160,192},{192,224},{224... | collective-permute-start | bytes 98312 | tf_op jit(solution)/shard_map/ppermute | solution.py:597
  17.1 8.7 %collective-permute-start.1 = (f32[64,128]{1,0:T(8,128)S(1)}, f32[64,128]{1,0:T(8,128)S(1)}, u32[]{:S(2)}, u32[]{:S(2)}) collective-permute-start(f32[64,128]{1,0:T(8,128)S(1)} %get-tuple-element.34), channel_id=1, source_target_pairs={{32,0},{64,32},{96,64},{128,96},{160,128},{192,160},{224,192},{256... | collective-permute-start | bytes 98312 | tf_op jit(solution)/shard_map/ppermute | solution.py:598
  24.8 21.1 %copy-start.2 = (f32[64,128]{1,0:T(8,128)}, f32[64,128]{1,0:T(8,128)S(1)}, u32[]{:S(2)}) copy-start(f32[64,128]{1,0:T(8,128)S(1)} %collective-permute-done.west.west_in) | copy-start | bytes 98308
  25.8 20.1 %copy-start.3 = (f32[64,128]{1,0:T(8,128)}, f32[64,128]{1,0:T(8,128)S(1)}, u32[]{:S(2)}) copy-start(f32[64,128]{1,0:T(8,128)S(1)} %collective-permute-done.1.east.east_in) | copy-start | bytes 98308
  25.8 12.0 %copy-start.4 = (f32[8,8]{1,0:T(8,128)S(1)}, f32[8,8]{1,0:T(8,128)}, u32[]{:S(2)}) copy-start(f32[8,8]{1,0:T(8,128)} %selectivity.9) | copy-start | bytes 772
  25.9 12.0 %copy-start.8 = (f32[8]{0:T(128)S(1)}, f32[8]{0:T(128)}, u32[]{:S(2)}) copy-start(f32[8]{0:T(128)} %mortality.3) | copy-start | bytes 100
  25.9 13.8 %collective-permute-start.3 = (f32[104,256]{1,0:T(8,128)S(1)}, f32[104,256]{1,0:T(8,128)S(1)}, u32[]{:S(2)}, u32[]{:S(2)}) collective-permute-start(f32[104,256]{1,0:T(8,128)S(1)} %get-tuple-element.38.after), channel_id=1, source_target_pairs={{0,8},{8,16},{16,24},{1,9},{9,17},{17,25},{2,10},{10,18},{18,26},{... | collective-permute-start | bytes 319496 | tf_op jit(solution)/shard_map/ppermute | solution.py:614
  35.9 9.9 %collective-permute-start.2 = (f32[104,256]{1,0:T(8,128)S(1)}, f32[104,256]{1,0:T(8,128)S(1)}, u32[]{:S(2)}, u32[]{:S(2)}) collective-permute-start(f32[104,256]{1,0:T(8,128)S(1)} %get-tuple-element.37), channel_id=1, source_target_pairs={{8,0},{16,8},{24,16},{9,1},{17,9},{25,17},{10,2},{18,10},{26,18},{... | collective-permute-start | bytes 319496 | tf_op jit(solution)/shard_map/ppermute | solution.py:615
  39.7 9.5 %copy-start = (f32[104,256]{1,0:T(8,128)}, f32[104,256]{1,0:T(8,128)S(1)}, u32[]{:S(2)}) copy-start(f32[104,256]{1,0:T(8,128)S(1)} %collective-permute-done.3.south_in) | copy-start | bytes 319492
  45.9 3.3 %copy-start.1 = (f32[104,256]{1,0:T(8,128)}, f32[104,256]{1,0:T(8,128)S(1)}, u32[]{:S(2)}) copy-start(f32[104,256]{1,0:T(8,128)S(1)} %collective-permute-done.2.north_in) | copy-start | bytes 319492
  49.2 14.5 %all-to-all-start.1 = ((f32[8,24,128]{2,1,0:T(8,128)}), f32[8,24,128]{2,1,0:T(8,128)S(1)}, u32[]{:S(2)}, u32[]{:S(2)}) async-start(f32[8,24,128]{2,1,0:T(8,128)} %get-tuple-element.40), calls=%async_computation.1 | async-start | bytes 196608 | tf_op jit(solution)/shard_map/all_to_all | solution.py:630
  56.1 32.8 %collective-permute-start.4 = (f32[152,128]{1,0:T(8,128)}, f32[152,128]{1,0:T(8,128)}, u32[]{:S(2)}, u32[]{:S(2)}) collective-permute-start(f32[152,128]{1,0:T(8,128)} %get-tuple-element.53), channel_id=1, source_target_pairs={{1,0},{2,1},{3,2},{4,3},{5,4},{6,5},{7,6},{9,8},{10,9},{11,10},{12... | collective-permute-start | bytes 233480 | tf_op jit(solution)/shard_map/ppermute | solution.py:631
  80.5 8.3 %copy-start.9 = (f32[8,16]{1,0:T(8,128)S(1)}, f32[8,16]{1,0:T(8,128)}, u32[]{:S(2)}) copy-start(f32[8,16]{1,0:T(8,128)} %param.29) | copy-start | bytes 1540
  80.5 17.7 %all-to-all-start.3 = ((f32[64,1,128]{2,1,0:T(1,128)}), f32[64,1,128]{2,1,0:T(1,128)S(1)}, u32[]{:S(2)}, u32[]{:S(2)}) async-start(f32[64,1,128]{2,1,0:T(1,128)} %bitcast.5), calls=%async_computation.3 | async-start | bytes 65536 | tf_op jit(solution)/shard_map/all_to_all | solution.py:650
  99.6 23.5 %all-to-all-start.4 = ((f32[8,152,128]{2,1,0:T(8,128)}), f32[8,152,128]{2,1,0:T(8,128)S(1)}, u32[]{:S(2)}, u32[]{:S(2)}) async-start(f32[8,152,128]{2,1,0:T(8,128)} %get-tuple-element.56), calls=%async_computation.4 | async-start | bytes 1245184 | tf_op jit(solution)/shard_map/all_to_all | solution.py:660

commit v5 on v4

--- a/solution.py
+++ b/solution.py
@@ -15,7 +15,10 @@
 WIDE, NARROW = 4, 2
 DENSITY, EAST, NORTH, SEA = 0, 32, 36, 40
 ADJOINT, EFFORT, MASK, REGION, HABITAT = 44, 60, 76, 92, 94
+FIRST_NARROW = ADJOINT
+CORNER = FIRST_NARROW
 STRIP = 96
+WIDE_ROWS, NARROW_ROWS = CORNER + 4, 56
 PACKED = 2 * EROWS + 8
 F32 = jnp.float32
 SEPARATE = False
@@ -52,7 +55,7 @@
 
 
 def pack_kernel(*refs):
-    inputs, (to_east, to_west, to_north, to_south) = refs[:9], refs[9:]
+    inputs, (to_east, to_west) = refs[:9], refs[9:]
     lane = lane_iota(ROWS)
     everything = slice(0, ROWS)
     right = jnp.zeros((ROWS, LANES), F32)
@@ -61,23 +64,30 @@
         here = (lane >= place) & (lane < place + width)
         right = jnp.where(here, turned(part(ref, index, everything, slice(LANES, COLS)), place + width), right)
         left = jnp.where(here, turned(part(ref, index, everything, slice(0, LANES)), place), left)
-        columns = slice(0, COLS)
-        to_north[place : place + width, :] = part(ref, index, slice(ROWS - width, ROWS), columns)
-        to_south[place : place + width, :] = part(ref, index, slice(0, width), columns)
     to_east[...] = right
     to_west[...] = left
 
 
+def rows_kernel(*refs):
+    inputs, north, south = refs[:9], refs[10:12], refs[12:14]
+    for ref, index, place, width in every_field(*inputs):
+        narrow = place >= FIRST_NARROW
+        at = place - FIRST_NARROW if narrow else place
+        north[narrow][at : at + width, :] = part(ref, index, slice(ROWS - width, ROWS), slice(0, COLS))
+        south[narrow][at : at + width, :] = part(ref, index, slice(0, width), slice(0, COLS))
+    used = STRIP - FIRST_NARROW
+    for out in (north[1], south[1]):
+        out[used:NARROW_ROWS, :] = jnp.zeros((NARROW_ROWS - used, COLS), F32)
+
+
 def corner_kernel(north_in, south_in, west, east, to_north, to_south):
-    if north_in is not to_north:
-        to_north[0:STRIP, :] = north_in[0:STRIP, :]
-        to_south[0:STRIP, :] = south_in[0:STRIP, :]
-    to_north[STRIP : STRIP + 4, 0:LANES] = west[ROWS - 4 : ROWS, :]
-    to_north[STRIP : STRIP + 4, LANES:COLS] = east[ROWS - 4 : ROWS, :]
-    to_south[STRIP : STRIP + 4, 0:LANES] = west[0:4, :]
-    to_south[STRIP : STRIP + 4, LANES:COLS] = east[0:4, :]
-    to_north[STRIP + 4 :, :] = jnp.zeros((4, COLS), F32)
-    to_south[STRIP + 4 :, :] = jnp.zeros((4, COLS), F32)
+    if SEPARATE:
+        to_north[0:CORNER, :] = north_in[0:CORNER, :]
+        to_south[0:CORNER, :] = south_in[0:CORNER, :]
+    to_north[CORNER:WIDE_ROWS, 0:LANES] = west[ROWS - 4 : ROWS, :]
+    to_north[CORNER:WIDE_ROWS, LANES:COLS] = east[ROWS - 4 : ROWS, :]
+    to_south[CORNER:WIDE_ROWS, 0:LANES] = west[0:4, :]
+    to_south[CORNER:WIDE_ROWS, LANES:COLS] = east[0:4, :]
 
 
 def at_all(out, slots, rows, value):
@@ -176,10 +186,10 @@
 def strips(west_in, east_in, north_in, south_in, west, east):
     west[0:ROWS, :] = west_in[...]
     east[0:ROWS, :] = east_in[...]
-    west[ROWS : ROWS + 4, :] = north_in[STRIP : STRIP + 4, 0:LANES]
-    east[ROWS : ROWS + 4, :] = north_in[STRIP : STRIP + 4, LANES:COLS]
-    west[ROWS + 4 : EROWS, :] = south_in[STRIP : STRIP + 4, 0:LANES]
-    east[ROWS + 4 : EROWS, :] = south_in[STRIP : STRIP + 4, LANES:COLS]
+    west[ROWS : ROWS + 4, :] = north_in[CORNER:WIDE_ROWS, 0:LANES]
+    east[ROWS : ROWS + 4, :] = north_in[CORNER:WIDE_ROWS, LANES:COLS]
+    west[ROWS + 4 : EROWS, :] = south_in[CORNER:WIDE_ROWS, 0:LANES]
+    east[ROWS + 4 : EROWS, :] = south_in[CORNER:WIDE_ROWS, LANES:COLS]
 
 
 def own_cells(ref, index, out):
@@ -194,7 +204,7 @@
     for half in range(2):
         cols = slice(LANES * half, LANES * half + LANES)
         blank = jnp.zeros((8 - 2 * width, LANES), F32)
-        rows = slice(place, place + width)
+        rows = slice(place - FIRST_NARROW, place - FIRST_NARROW + width)
         tiles.append(jnp.concatenate([north_in[rows, cols], blank, south_in[rows, cols]], axis=0))
     lane = lane_iota(8)
     packed = jnp.zeros((8, LANES), F32)
@@ -232,79 +242,13 @@
     return sea * (first[0] + spreading(first[1]) + drifting(first[2], rate, out_rate))
 
 
-def inner_kernel(density, current_east, current_north, sea_mask, after, swim, spread, mass, total_out):
+def total_kernel(
+    density, current_east, current_north, sea_mask, adjoint, west_in, east_in, north_in, south_in,
+    narrow_north, narrow_south, after, swim, spread, mass, total_out, tail_out, density_out, flow_out, west, east,
+):
     del after
-    flow = (current_east[...], current_north[...], sea_mask[...].astype(F32))
-    total = summed_settled(density, flow, swim, spread, mass)
-    slots = total_out.shape[0]
-    at_all(total_out, slots, slice(0, ROWS), total[:, 0:LANES])
-    at_all(total_out, slots, slice(ROWS, 2 * ROWS), total[:, LANES:COLS])
-
-
-def ring_of(total):
-    row = lax.broadcasted_iota(jnp.int32, (8, LANES), 0)
-    outer = (row < 2) | (row >= 6)
-    parts = []
-    for half in range(2):
-        cols = slice(LANES * half, LANES * half + LANES)
-        edge = jnp.where(row < 2, total[0:8, cols], total[ROWS - 8 : ROWS, cols])
-        parts.append(jnp.where(outer, total[ROWS:EROWS, cols], pltpu.roll(edge, 4, 0)))
-    lane = lane_iota(8)
-    sides = jnp.zeros((8, LANES), F32)
-    for k in range(EROWS // 8):
-        rows = slice(8 * k, 8 * k + 8)
-        low, high = total[rows, 0:LANES], total[rows, LANES:COLS]
-        side = total[rows, COLS:ECOLS]
-        base = 8 * k
-        for offset, tile, by in (
-            (0, high, base - (LANES - 2)),
-            (2, side, base + 2),
-            (4, side, base + 4 - (LANES - 2)),
-            (6, low, base + 6),
-        ):
-            here = (lane >= base + offset) & (lane < base + offset + 2)
-            sides = jnp.where(here, turned(tile, by), sides)
-    parts.append(sides)
-    return parts
-
-
-def with_ring(inner, ring, out):
-    row = lax.broadcasted_iota(jnp.int32, (8, LANES), 0)
-    lane = lane_iota(8)
-    sides = ring[16:24]
-    for half in range(2):
-        lat = ring[8 * half : 8 * half + 8]
-        edge = pltpu.roll(lat, 4, 0)
-        for k in range(EROWS // 8):
-            if k < ROWS // 8:
-                tile = inner[ROWS * half + 8 * k : ROWS * half + 8 * k + 8]
-            else:
-                tile = lat
-            if k == 0:
-                tile = jnp.where(row < 2, edge, tile)
-            if k == ROWS // 8 - 1:
-                tile = jnp.where(row >= 6, edge, tile)
-            if half == 0:
-                tile = jnp.where(lane < 2, turned(sides, -(8 * k + 6)), tile)
-            else:
-                tile = jnp.where(lane >= LANES - 2, turned(sides, LANES - 2 - 8 * k), tile)
-            out[EROWS * half + 8 * k : EROWS * half + 8 * k + 8, :] = tile
-    packed = jnp.zeros((8, LANES), F32)
-    for k in range(EROWS // 8):
-        here = (lane >= 4 * k) & (lane < 4 * k + 2)
-        packed = jnp.where(here, turned(sides, -(4 * k + 4)), packed)
-        here = (lane >= 4 * k + 2) & (lane < 4 * k + 4)
-        packed = jnp.where(here, turned(sides, -4 * k), packed)
-    out[2 * EROWS : PACKED, :] = packed
-
-
-def total_kernel(
-    density, current_east, current_north, sea_mask, adjoint, west_in, east_in, north_in, south_in, after, after_too,
-    swim, spread, mass, total_out, tail_out, density_out, flow_out, west, east,
-):
-    del after, after_too
     strips(west_in, east_in, north_in, south_in, west, east)
-    narrow_field(adjoint, 0, ADJOINT, west, east, north_in, south_in, tail_out)
+    narrow_field(adjoint, 0, ADJOINT, west, east, narrow_north, narrow_south, tail_out)
     lane = lane_iota(EROWS)
     wide = [(density, c, DENSITY + WIDE * c, density_out.at[c]) for c in range(N)]
     wide += [(current_east, None, EAST, flow_out.at[0]), (current_north, None, NORTH, flow_out.at[1])]
@@ -317,8 +261,11 @@
         side = jnp.where(lane >= LANES - WIDE, turned(west[...], LANES - WIDE - place), side)
         out[:, COLS:ECOLS] = side
     total = summed_settled(density_out, flow_out, swim, spread, mass)
-    for k, ring in enumerate(ring_of(total)):
-        at_all(total_out, total_out.shape[0], slice(8 * k, 8 * k + 8), ring)
+    slots = total_out.shape[0]
+    at_all(total_out, slots, slice(0, EROWS), total[:, 0:LANES])
+    at_all(total_out, slots, slice(EROWS, 2 * EROWS), total[:, LANES:COLS])
+    sides = [total[8 * k : 8 * k + 8, COLS:ECOLS] for k in range(EROWS // 8)]
+    at_all(total_out, slots, slice(2 * EROWS, PACKED), packed_side(sides))
 
 
 def fleet_rows(rows, efforts, reported_out, fishing_out, mortality, selectivity):
@@ -351,8 +298,8 @@
 
 
 def settle_kernel(
-    fishing, reported, region, adjoint, habitat, west_in, east_in, north_in, south_in, density, flow,
-    swim, spread, mortality, selectivity,
+    fishing, reported, region, adjoint, habitat, west_in, east_in, north_in, south_in,
+    narrow_north, narrow_south, density, flow, swim, spread, mortality, selectivity,
     settled_out, fishing_out, reported_out, region_out, carried_out, habitat_out, west, east, efforts,
 ):
     for source, out in ((fishing, fishing_out), (reported, reported_out), (region, region_out)):
@@ -361,15 +308,15 @@
     strips(west_in, east_in, north_in, south_in, west, east)
 
     def halo(place, out):
-        for top, tile in zip(HALO_ROWS, halo_cells(place, west, east, north_in, south_in), strict=True):
+        for top, tile in zip(HALO_ROWS, halo_cells(place, west, east, narrow_north, narrow_south), strict=True):
             out[top : top + 8, :] = tile
 
     for k in range(N):
-        narrow_field(adjoint, k, ADJOINT + NARROW * k, west, east, north_in, south_in, carried_out.at[k])
+        narrow_field(adjoint, k, ADJOINT + NARROW * k, west, east, narrow_north, narrow_south, carried_out.at[k])
         halo(EFFORT + NARROW * k, efforts.at[k])
         halo(MASK + NARROW * k, reported_out.at[k])
     halo(REGION, region_out)
-    narrow_field(habitat, None, HABITAT, west, east, north_in, south_in, habitat_out)
+    narrow_field(habitat, None, HABITAT, west, east, narrow_north, narrow_south, habitat_out)
     for top in HALO_ROWS:
         fleet_rows(slice(top, top + 8), efforts, reported_out, fishing_out, mortality, selectivity)
 
@@ -382,10 +329,10 @@
 
 
 def catch_kernel(
-    age, received, ring, settled, fishing, reported, region, mass, selectivity, mort_out, catch_out, older, fleets
+    age, received, settled, fishing, reported, region, mass, selectivity, mort_out, catch_out, older, fleets
 ):
     shard = age[0]
-    with_ring(picked(received, lambda slot: slot > shard), picked(ring, lambda slot: slot > shard), older)
+    older[...] = picked(received, lambda slot: slot > shard)
 
     def pair(t, carry):
         places = [pl.ds(pl.multiple_of(t * 8, 8), 8), pl.ds(pl.multiple_of(EROWS + t * 8, 8), 8)]
@@ -486,8 +433,9 @@
 
 def own_kernel(
     misfit_in, region, reported, settled, kept, yields, slope, flow, swim, spread, mass, selectivity,
-    grad_out, bars, wide,
+    grad_out, flow_out, bars, wide,
 ):
+    flow_out[...] = flow[...]
     misfit = misfit_in[...]
 
     def tile(t, carry):
@@ -587,52 +535,45 @@
         density, adjoint_next, effort, catch_mask, current_east, current_north, region, sea_mask, habitat
     )
     density, adjoint_next, effort, catch_mask, current_east, current_north, region, sea_mask, habitat = inputs
-    strip_rows = STRIP + 8
-
-    to_east, to_west, to_north, to_south = call(
-        pack_kernel,
-        [VMEM] * 9,
-        [shape(ROWS, LANES), shape(ROWS, LANES), shape(strip_rows, COLS), shape(strip_rows, COLS)],
-    )(*inputs)
+    packed = (PACKED, LANES)
+    extended = (EROWS, ECOLS)
+    to_east, to_west = call(pack_kernel, [VMEM] * 9, [shape(ROWS, LANES)] * 2)(*inputs)
     from_west = lax.ppermute(to_east, "lon", [(i, (i + 1) % lons) for i in range(lons)])
     from_east = lax.ppermute(to_west, "lon", [((i + 1) % lons, i) for i in range(lons)])
-    packed = (PACKED, LANES)
-    extended = (EROWS, ECOLS)
-    (inner,) = call(
-        inner_kernel, [VMEM] * 5 + [SMEM] * 3, [shape(ages, 2 * ROWS, LANES)]
-    )(density, current_east, current_north, sea_mask, near(to_east), swim_speed, diffusion, cohort_mass)
-    inner = lax.all_to_all(inner, "age", 0, 0, tiled=True)
-    to_north, to_south = pl.pallas_call(
-        corner_kernel,
-        name="corner",
-        in_specs=[VMEM] * 4,
-        out_specs=[VMEM, VMEM],
-        out_shape=[shape(strip_rows, COLS)] * 2,
-        input_output_aliases={0: 0, 1: 1},
-        compiler_params=pltpu.CompilerParams(vmem_limit_bytes=4 << 20),
+    to_north, narrow_north, to_south, narrow_south = call(
+        rows_kernel, [VMEM] * 10, [shape(WIDE_ROWS, COLS), shape(NARROW_ROWS, COLS)] * 2
+    )(*inputs, near(to_east))
+    northward = [(i, i + 1) for i in range(lats - 1)]
+    southward = [(i + 1, i) for i in range(lats - 1)]
+    narrow_south, narrow_north = (
+        lax.ppermute(narrow_north, "lat", northward),
+        lax.ppermute(narrow_south, "lat", southward),
+    )
+    to_north, to_south = call(
+        corner_kernel, [VMEM] * 4, [shape(WIDE_ROWS, COLS)] * 2, (), {0: 0, 1: 1}
     )(near(to_north), near(to_south), near(from_west), near(from_east))
-    from_south = lax.ppermute(to_north, "lat", [(i, i + 1) for i in range(lats - 1)])
-    from_north = lax.ppermute(to_south, "lat", [(i + 1, i) for i in range(lats - 1)])
-    halos = (from_west, from_east, from_north, from_south)
+    from_south = lax.ppermute(to_north, "lat", northward)
+    from_north = lax.ppermute(to_south, "lat", southward)
+    halos = (from_west, from_east, from_north, from_south, narrow_north, narrow_south)
 
     fishing, reported, regions = call(
         fleet_kernel, [VMEM] * 4 + [SMEM] * 2, [shape(N, *packed)] * 2 + [shape(*packed)], [(N, *packed)]
     )(effort, catch_mask, region, near(to_north), mortality, selectivity)
-    ring, tail, density_ext, flow = call(
+    totals, tail, density_ext, flow = call(
         total_kernel,
-        [VMEM] * 11 + [SMEM] * 3,
-        [shape(ages, 24, LANES), shape(*packed), shape(N, *extended), far(3, *extended)],
+        [VMEM] * 12 + [SMEM] * 3,
+        [shape(ages, *packed), shape(*packed), shape(N, *extended), far(3, *extended)],
         [(EROWS, LANES), (EROWS, LANES)],
     )(
-        density, current_east, current_north, sea_mask, adjoint_next, *map(near, halos), near(inner), near(regions),
+        density, current_east, current_north, sea_mask, adjoint_next, *map(near, halos), near(regions),
         swim_speed, diffusion, cohort_mass,
     )
-    ring = lax.all_to_all(ring, "age", 0, 0, tiled=True)
+    totals = lax.all_to_all(totals, "age", 0, 0, tiled=True)
     tail = lax.ppermute(tail, "age", [(i + 1, i) for i in range(ages - 1)])
 
     settled, fishing, reported, regions, carried, habitats = call(
         settle_kernel,
-        [VMEM] * 11 + [SMEM] * 4,
+        [VMEM] * 13 + [SMEM] * 4,
         [shape(N, *packed)] * 3 + [shape(*packed), far(N, *packed), far(*packed)],
         [(EROWS, LANES), (EROWS, LANES), (N, *packed)],
         {0: 1, 1: 2, 2: 3},
@@ -643,8 +584,8 @@
     settled, reported, regions = near(settled), near(reported), near(regions)
 
     mort, catches = call(
-        catch_kernel, [SMEM] + [VMEM] * 6 + [SMEM] * 2, [shape(N, *packed), shape(ages, LANES)], [packed, (N, *packed)]
-    )(age, near(inner), near(ring), settled, near(fishing), reported, regions, cohort_mass, selectivity)
+        catch_kernel, [SMEM] + [VMEM] * 5 + [SMEM] * 2, [shape(N, *packed), shape(ages, LANES)], [packed, (N, *packed)]
+    )(age, near(totals), settled, near(fishing), reported, regions, cohort_mass, selectivity)
     catches = near(lax.all_to_all(catches, "age", 0, 0, tiled=True))
     (catches,) = call(relay_kernel, [VMEM], [shape(lons * lats, LANES)])(catches)
     catches = near(lax.all_to_all(catches, ("lon", "lat"), 0, 0, tiled=True))
@@ -660,12 +601,12 @@
     totals = lax.all_to_all(totals, "age", 0, 0, tiled=True)
 
     kept, yields, slope, flow = distant(kept, yields, slope, flow)
-    (own,) = call(
-        own_kernel, [VMEM] * 8 + [SMEM] * 4, [shape(N, ROWS, COLS)], [(N, *packed), extended]
+    own, flow_near = call(
+        own_kernel, [VMEM] * 8 + [SMEM] * 4, [shape(N, ROWS, COLS), shape(3, *extended)], [(N, *packed), extended]
     )(near(misfit), regions, reported, settled, kept, yields, slope, flow, swim_speed, diffusion, cohort_mass, selectivity)
     (grad,) = call(
         final_kernel, [SMEM] + [VMEM] * 3 + [SMEM] * 3, [far(N, ROWS, COLS)], [extended, (6, ROWS, COLS)]
-    )(age, near(totals), near(own), flow, swim_speed, diffusion, cohort_mass)
+    )(age, near(totals), near(own), near(flow_near), swim_speed, diffusion, cohort_mass)
     return grad
 
 

time: 126 us -> 121 us (0.960)
  starting transfers between devices: 51.4 us -> 45.2 us
  waiting for transfers between devices: 28.5 us -> 34.3 us
  blocking collectives: 12.6 us -> 8.92 us
  Pallas kernels: 32.1 us -> 30.8 us
    all_to_all x2 -> x0, starting transfers between devices: 14.6 us -> none  [the longest x1 7.64 us: month(): inner = lax.all_to_all(inner, 'age', 0, 0, tiled=True)]
    all_to_all x1 -> x2, waiting for transfers between devices: 14 us -> 22.8 us  [month(): totals = lax.all_to_all(totals, 'age', 0, 0, tiled=True)]
    all_to_all x1 -> x2, starting transfers between devices: 3.54 us -> 10.4 us  [month(): totals = lax.all_to_all(totals, 'age', 0, 0, tiled=True)]
    all_to_all x1, blocking collectives: 12.6 us -> 8.92 us  [month(): catches = near(lax.all_to_all(catches, 'age', 0, 0, tiled=True))]
    ppermute x2 -> x4, starting transfers between devices: 12 us -> 15.5 us  [the longest x1 5.95 us: month(): lax.ppermute(narrow_south, 'lat', southward)]
    all_to_all x1, starting transfers between devices: 8.3 us -> 5.56 us  [month(): catches = near(lax.all_to_all(catches, ('lon', 'lat'), 0, 0, tiled=True))]
    all_to_all x2 -> x0, waiting for transfers between devices: 1.35 us -> none  [the longest x1 1.34 us: month(): ring = lax.all_to_all(ring, 'age', 0, 0, tiled=True)]
    ppermute x2 -> x4, waiting for transfers between devices: 6.19 us -> 5.5 us  [the longest x1 5.49 us: month(): from_north = lax.ppermute(to_south, 'lat', southward)]
  transfers between devices with their start and end apart: 9 -> 10, of which waited for: 5 -> 4; matrix products, arithmetic and copies ran while one was open for 0% -> 0% of each run, Pallas kernels for 16% -> 18%
where the time goes in v5:
time: 121 us; the launch traced here: 120 us
  starting transfers between devices  45.2 us (37%)
  waiting for transfers between devices  34.3 us (28%)
  Pallas kernels  30.8 us (25%)
  blocking collectives  8.92 us (7%)
    all_to_all x2, waiting for transfers between devices, month(): totals = lax.all_to_all(totals, 'age', 0, 0, tiled=True)  22.8 us
    all_to_all x2, starting transfers between devices, month(): totals = lax.all_to_all(totals, 'age', 0, 0, tiled=True)  10.4 us
    all_to_all x1, blocking collectives, month(): catches = near(lax.all_to_all(catches, 'age', 0, 0, tiled=True))  8.92 us
    ppermute x1, starting transfers between devices, month(): lax.ppermute(to_west, 'lon', [((i + 1) % lons, i) for i in range(lons)])  7.73 us
    all_to_all x1, waiting for transfers between devices, month(): catches = near(lax.all_to_all(catches, ('lon', 'lat'), 0, 0, tiled=True))  6 us
    pallas_call x1, Pallas kernels, month(): call(own_kernel, [VMEM] * 8 + [SMEM] * 4, [shape(N, ROWS, COLS), shape(3,...  5.95 us
    ppermute x1, starting transfers between devices, month(): lax.ppermute(narrow_south, 'lat', southward)  5.95 us
    all_to_all x1, starting transfers between devices, month(): catches = near(lax.all_to_all(catches, ('lon', 'lat'), 0, 0, tiled=True))  5.56 us
  transfers between devices with their start and end apart: 10, of which 4 were waited for; matrix products, arithmetic and copies ran while one was open for 0% of the time, Pallas kernels for 18%

profile of v5, /device:TPU:1, one launch (start us, length us, event | category | flops | bytes accessed | tf_op | source)
XLA Modules:
  0.0 119.8 jit_solution(11379444375298274448)
XLA Ops:
  0.0 2.3 %shard_map.145 = (f32[64,128]{1,0:T(8,128)S(1)}, f32[64,128]{1,0:T(8,128)S(1)}) custom-call(f32[8,64,256]{2,1,0:T(8,128)} %density.1, f32[8,64,256]{2,1,0:T(8,128)} %adjoint.3, f32[8,64,256]{2,1,0:T(8,128)} %effort.1, s32[8,64,256]{2,1,0:T(8,128)} %mask.1, f32[64,256]{1,0:T(8,128)} %current_east.1, f32[64,256]{1,0:T(8,128)} %current_north.1, ...), custom_call_target="tpu_custom_call" | custom-call | tf_op jit(solution)/shard_map/pallas_call | solution.py:540
  2.3 4.8 %collective-permute-start = (f32[64,128]{1,0:T(8,128)S(1)}, f32[64,128]{1,0:T(8,128)S(1)}, u32[]{:S(2)}, u32[]{:S(2)}) collective-permute-start(f32[64,128]{1,0:T(8,128)S(1)} %get-tuple-element.37.refs_9_), channel_id=1, source_target_pairs={{0,32},{32,64},{64,96},{96,128},{128,160},{160,192},{192,224},{224... | collective-permute-start | bytes 98312 | tf_op jit(solution)/shard_map/ppermute | solution.py:541
  7.1 7.7 %collective-permute-start.1 = (f32[64,128]{1,0:T(8,128)S(1)}, f32[64,128]{1,0:T(8,128)S(1)}, u32[]{:S(2)}, u32[]{:S(2)}) collective-permute-start(f32[64,128]{1,0:T(8,128)S(1)} %get-tuple-element.38), channel_id=1, source_target_pairs={{32,0},{64,32},{96,64},{128,96},{160,128},{192,160},{224,192},{256... | collective-permute-start | bytes 98312 | tf_op jit(solution)/shard_map/ppermute | solution.py:542
  14.8 1.6 %shard_map.146 = (f32[48,256]{1,0:T(8,128)S(1)}, f32[56,256]{1,0:T(8,128)S(1)}, f32[48,256]{1,0:T(8,128)S(1)}, f32[56,256]{1,0:T(8,128)S(1)}) custom-call(f32[8,64,256]{2,1,0:T(8,128)} %density.1, f32[8,64,256]{2,1,0:T(8,128)} %adjoint.3, f32[8,64,256]{2,1,0:T(8,128)} %effort.1, s32[8,64,256]{2,1,0:T(8,128)} %mask.1, f32[64,256]{1,0:T(8,128)} %current_east.1, ...), custom_call_target="tpu_custom_call" | custom-call | tf_op jit(solution)/shard_map/pallas_call | solution.py:543
  16.5 5.9 %collective-permute-start.4 = (f32[56,256]{1,0:T(8,128)S(1)}, f32[56,256]{1,0:T(8,128)S(1)}, u32[]{:S(2)}, u32[]{:S(2)}) collective-permute-start(f32[56,256]{1,0:T(8,128)S(1)} %get-tuple-element.43), channel_id=1, source_target_pairs={{8,0},{16,8},{24,16},{9,1},{17,9},{25,17},{10,2},{18,10},{26,18},{... | collective-permute-start | bytes 172040 | tf_op jit(solution)/shard_map/ppermute | solution.py:550
  22.4 5.2 %collective-permute-start.5 = (f32[56,256]{1,0:T(8,128)S(1)}, f32[56,256]{1,0:T(8,128)S(1)}, u32[]{:S(2)}, u32[]{:S(2)}) collective-permute-start(f32[56,256]{1,0:T(8,128)S(1)} %get-tuple-element.44), channel_id=1, source_target_pairs={{0,8},{8,16},{16,24},{1,9},{9,17},{17,25},{2,10},{10,18},{18,26},{... | collective-permute-start | bytes 172040 | tf_op jit(solution)/shard_map/ppermute | solution.py:549
  27.7 2.4 %collective-permute-start.3 = (f32[48,256]{1,0:T(8,128)S(1)}, f32[48,256]{1,0:T(8,128)S(1)}, u32[]{:S(2)}, u32[]{:S(2)}) collective-permute-start(f32[48,256]{1,0:T(8,128)S(1)} %get-tuple-element.42.after), channel_id=1, source_target_pairs={{0,8},{8,16},{16,24},{1,9},{9,17},{17,25},{2,10},{10,18},{18,26},{... | collective-permute-start | bytes 147464 | tf_op jit(solution)/shard_map/ppermute | solution.py:555
  30.1 1.9 %collective-permute-start.2 = (f32[48,256]{1,0:T(8,128)S(1)}, f32[48,256]{1,0:T(8,128)S(1)}, u32[]{:S(2)}, u32[]{:S(2)}) collective-permute-start(f32[48,256]{1,0:T(8,128)S(1)} %get-tuple-element.41), channel_id=1, source_target_pairs={{8,0},{16,8},{24,16},{9,1},{17,9},{25,17},{10,2},{18,10},{26,18},{... | collective-permute-start | bytes 147464 | tf_op jit(solution)/shard_map/ppermute | solution.py:556
  32.1 1.8 %shard_map.148 = (f32[8,152,128]{2,1,0:T(8,128)S(1)}, f32[8,152,128]{2,1,0:T(8,128)S(1)}, f32[152,128]{1,0:T(8,128)S(1)}) custom-call(f32[8,64,256]{2,1,0:T(8,128)} %effort.1, s32[8,64,256]{2,1,0:T(8,128)} %mask.1, s32[64,256]{1,0:T(8,128)} %region.1, f32[48,256]{1,0:T(8,128)S(1)} %get-tuple-element.42.after, f32[8]{0:T(128)S(1)} %copy-done.10, ...), custom_call_target="tpu_custom_call" | custom-call | tf_op jit(solution)/shard_map/pallas_call | solution.py:559
  33.9 5.5 %collective-permute-done.2.north_in = f32[48,256]{1,0:T(8,128)S(1)} collective-permute-done((f32[48,256]{1,0:T(8,128)S(1)}, f32[48,256]{1,0:T(8,128)S(1)}, u32[]{:S(2)}, u32[]{:S(2)}) %collective-permute-start.2) | collective-permute-done | bytes 49184 | tf_op jit(solution)/shard_map/ppermute | solution.py:556
  39.5 3.4 %shard_map.149 = (f32[8,152,128]{2,1,0:T(8,128)}, f32[152,128]{1,0:T(8,128)}, f32[8,72,384]{2,1,0:T(8,128)S(1)}, f32[3,72,384]{2,1,0:T(8,128)}) custom-call(f32[8,64,256]{2,1,0:T(8,128)} %density.1, f32[64,256]{1,0:T(8,128)} %current_east.1, f32[64,256]{1,0:T(8,128)} %current_north.1, s32[64,256]{1,0:T(8,128)} %sea_mask.1, f32[8,64,256]{2,1,0:T(8,128)} %adjoint.3, ...), custom_call_target="tpu_custom_call" | custom-call | tf_op jit(solution)/shard_map/pallas_call | solution.py:562
  42.9 6.8 %all-to-all-start = ((f32[8,152,128]{2,1,0:T(8,128)}), f32[8,152,128]{2,1,0:T(8,128)S(1)}, u32[]{:S(2)}, u32[]{:S(2)}) async-start(f32[8,152,128]{2,1,0:T(8,128)} %get-tuple-element.46), calls=%async_computation | async-start | bytes 1245184 | tf_op jit(solution)/shard_map/all_to_all | solution.py:571
  51.1 4.9 %shard_map.150 = (f32[8,152,128]{2,1,0:T(8,128)S(1)}, f32[8,152,128]{2,1,0:T(8,128)S(1)}, f32[8,152,128]{2,1,0:T(8,128)S(1)}, f32[152,128]{1,0:T(8,128)S(1)}, f3...) custom-call(f32[8,152,128]{2,1,0:T(8,128)S(1)} %get-tuple-element.47.fishing,, ...), custom_call_target="tpu_custom_call", output_to_operand_aliasing={{1}: (0, {}), {2}: (1, {}), {3}: (2, {})} | custom-call | tf_op jit(solution)/shard_map/pallas_call | solution.py:574
  55.9 8.8 %all-to-all-done.received = f32[8,152,128]{2,1,0:T(8,128)S(1)} async-done(((f32[8,152,128]{2,1,0:T(8,128)}), f32[8,152,128]{2,1,0:T(8,128)S(1)}, u32[]{:S(2)}, u32[]{:S(2)}) %all-to-all-start) | async-done | bytes 622624 | tf_op jit(solution)/shard_map/all_to_all | solution.py:571
  64.7 3.6 %shard_map.151 = (f32[8,152,128]{2,1,0:T(8,128)S(1)}, f32[8,128]{1,0:T(8,128)S(1)}) custom-call(s32[2]{0:T(128)S(1)} %pad_add_fusion.age, f32[8,152,128]{2,1,0:T(8,128)S(1)} %all-to-all-done.received, f32[8,152,128]{2,1,0:T(8,128)S(1)} %get-tuple-element.51.settled, f32[8,152,128]{2,1,0:T(8,128)S(1)} %get-tuple-element.52.fishing, ...), custom_call_target="tpu_custom_call" | custom-call | tf_op jit(solution)/shard_map/pallas_call | solution.py:586
  68.3 8.9 %all_to_all.32 = f32[8,1,128]{2,1,0:T(1,128)S(1)} all-to-all(f32[8,1,128]{2,1,0:T(1,128)S(1)} %bitcast.11), channel_id=1, replica_groups=mesh['lon'=16,'lat'=4,'age'=8] {'age'}, dimensions={0} | all-to-all | bytes 8192 | tf_op jit(solution)/shard_map/all_to_all | solution.py:589
  77.9 5.6 %all-to-all-start.2 = ((f32[64,1,128]{2,1,0:T(1,128)}), f32[64,1,128]{2,1,0:T(1,128)S(1)}, u32[]{:S(2)}, u32[]{:S(2)}) async-start(f32[64,1,128]{2,1,0:T(1,128)} %bitcast.5), calls=%async_computation.2 | async-start | bytes 65536 | tf_op jit(solution)/shard_map/all_to_all | solution.py:591
  83.5 3.4 %shard_map.153 = (f32[152,128]{1,0:T(8,128)S(1)}, f32[8,152,128]{2,1,0:T(8,128)S(1)}, f32[8,152,128]{2,1,0:T(8,128)}, f32[8,152,128]{2,1,0:T(8,128)}, f32[8,152,128]{2,1,0:T(8,128)}) custom-call(s32[2]{0:T(128)S(1)} %pad_add_fusion.age, f32[8,152,128]{2,1,0:T(8,128)S(1)} %get-tuple-element.56.mort, f32[8,152,128]{2,1,0:T(8,128)S(1)} %get-tuple-element.51.settled, ...), custom_call_target="tpu_custom_call" | custom-call | tf_op jit(solution)/shard_map/pallas_call | solution.py:593
  86.9 6.0 %all-to-all-done.2 = f32[64,1,128]{2,1,0:T(1,128)S(1)} async-done(((f32[64,1,128]{2,1,0:T(1,128)}), f32[64,1,128]{2,1,0:T(1,128)S(1)}, u32[]{:S(2)}, u32[]{:S(2)}) %all-to-all-start.2) | async-done | bytes 32800 | tf_op jit(solution)/shard_map/all_to_all | solution.py:591
  92.9 1.4 %shard_map.154 = (f32[8,128]{1,0:T(8,128)S(1)}, f32[8,152,128]{2,1,0:T(8,128)}) custom-call(f32[64,128]{1,0:T(8,128)S(1)} %bitcast.9, f32[1,128]{1,0:T(1,128)S(1)} %reshape.7.observed, f32[152,128]{1,0:T(8,128)S(1)} %get-tuple-element.54.region, f32[152,128]{1,0:T(8,128)S(1)} %get-tuple-element.60.still, f32[8,152,128]{2,1,0:T(8,128)S(1)} %get-tuple-element.61.reach), custom_call_target="tpu_custom_call" | custom-call | tf_op jit(solution)/shard_map/pallas_call | solution.py:598
  94.2 3.5 %all-to-all-start.3 = ((f32[8,152,128]{2,1,0:T(8,128)}), f32[8,152,128]{2,1,0:T(8,128)S(1)}, u32[]{:S(2)}, u32[]{:S(2)}) async-start(f32[8,152,128]{2,1,0:T(8,128)} %get-tuple-element.62), calls=%async_computation.3 | async-start | bytes 1245184 | tf_op jit(solution)/shard_map/all_to_all | solution.py:601
  97.8 6.0 %shard_map.155 = (f32[8,64,256]{2,1,0:T(8,128)S(1)}, f32[3,72,384]{2,1,0:T(8,128)S(1)}) custom-call(f32[8,128]{1,0:T(8,128)S(1)} %get-tuple-element.63.misfit_in, f32[152,128]{1,0:T(8,128)S(1)} %get-tuple-element.54.region, f32[8,152,128]{2,1,0:T(8,128)S(1)} %get-tuple-element.53.reported, f32[8,152,128]{2,1,0:T(8,128)S(1)} %get-tuple-element.51.settled, ...), custom_call_target="tpu_custom_call" | custom-call | tf_op jit(solution)/shard_map/pallas_call | solution.py:604
  103.8 14.0 %all-to-all-done.3.received = f32[8,152,128]{2,1,0:T(8,128)S(1)} async-done(((f32[8,152,128]{2,1,0:T(8,128)}), f32[8,152,128]{2,1,0:T(8,128)S(1)}, u32[]{:S(2)}, u32[]{:S(2)}) %all-to-all-start.3) | async-done | bytes 622624 | tf_op jit(solution)/shard_map/all_to_all | solution.py:601
  117.8 2.0 %shard_map.156 = f32[8,64,256]{2,1,0:T(8,128)} custom-call(s32[2]{0:T(128)S(1)} %pad_add_fusion.age, f32[8,152,128]{2,1,0:T(8,128)S(1)} %all-to-all-done.3.received, f32[8,64,256]{2,1,0:T(8,128)S(1)} %get-tuple-element.67.own, f32[3,72,384]{2,1,0:T(8,128)S(1)} %get-tuple-element.68.flow, f32[8]{0:T(128)S(1)} %copy-done.8, f32[8]{0:T(128)S(1)} %copy-done.9, ...), custom_call_target="tpu_custom_call" | custom-call | tf_op jit(solution)/shard_map/pallas_call | solution.py:607
  (35 shorter events, 2.1 us)
Async XLA Ops:
  2.3 25.4 %collective-permute-start = (f32[64,128]{1,0:T(8,128)S(1)}, f32[64,128]{1,0:T(8,128)S(1)}, u32[]{:S(2)}, u32[]{:S(2)}) collective-permute-start(f32[64,128]{1,0:T(8,128)S(1)} %get-tuple-element.37.refs_9_), channel_id=1, source_target_pairs={{0,32},{32,64},{64,96},{96,128},{128,160},{160,192},{192,224},{224... | collective-permute-start | bytes 98312 | tf_op jit(solution)/shard_map/ppermute | solution.py:541
  7.1 20.6 %collective-permute-start.1 = (f32[64,128]{1,0:T(8,128)S(1)}, f32[64,128]{1,0:T(8,128)S(1)}, u32[]{:S(2)}, u32[]{:S(2)}) collective-permute-start(f32[64,128]{1,0:T(8,128)S(1)} %get-tuple-element.38), channel_id=1, source_target_pairs={{32,0},{64,32},{96,64},{128,96},{160,128},{192,160},{224,192},{256... | collective-permute-start | bytes 98312 | tf_op jit(solution)/shard_map/ppermute | solution.py:542
  16.5 17.4 %collective-permute-start.4 = (f32[56,256]{1,0:T(8,128)S(1)}, f32[56,256]{1,0:T(8,128)S(1)}, u32[]{:S(2)}, u32[]{:S(2)}) collective-permute-start(f32[56,256]{1,0:T(8,128)S(1)} %get-tuple-element.43), channel_id=1, source_target_pairs={{8,0},{16,8},{24,16},{9,1},{17,9},{25,17},{10,2},{18,10},{26,18},{... | collective-permute-start | bytes 172040 | tf_op jit(solution)/shard_map/ppermute | solution.py:550
  22.4 11.5 %collective-permute-start.5 = (f32[56,256]{1,0:T(8,128)S(1)}, f32[56,256]{1,0:T(8,128)S(1)}, u32[]{:S(2)}, u32[]{:S(2)}) collective-permute-start(f32[56,256]{1,0:T(8,128)S(1)} %get-tuple-element.44), channel_id=1, source_target_pairs={{0,8},{8,16},{16,24},{1,9},{9,17},{17,25},{2,10},{10,18},{18,26},{... | collective-permute-start | bytes 172040 | tf_op jit(solution)/shard_map/ppermute | solution.py:549
  27.6 11.8 %copy-start = (f32[64,128]{1,0:T(8,128)}, f32[64,128]{1,0:T(8,128)S(1)}, u32[]{:S(2)}) copy-start(f32[64,128]{1,0:T(8,128)S(1)} %collective-permute-done.west.west_in) | copy-start | bytes 98308
  27.6 11.8 %copy-start.1 = (f32[64,128]{1,0:T(8,128)}, f32[64,128]{1,0:T(8,128)S(1)}, u32[]{:S(2)}) copy-start(f32[64,128]{1,0:T(8,128)S(1)} %collective-permute-done.1.east.east_in) | copy-start | bytes 98308
  27.7 4.4 %copy-start.6 = (f32[8,8]{1,0:T(8,128)S(1)}, f32[8,8]{1,0:T(8,128)}, u32[]{:S(2)}) copy-start(f32[8,8]{1,0:T(8,128)} %selectivity.9) | copy-start | bytes 772
  27.7 4.4 %copy-start.10 = (f32[8]{0:T(128)S(1)}, f32[8]{0:T(128)}, u32[]{:S(2)}) copy-start(f32[8]{0:T(128)} %mortality.3) | copy-start | bytes 100
  27.7 6.2 %collective-permute-start.3 = (f32[48,256]{1,0:T(8,128)S(1)}, f32[48,256]{1,0:T(8,128)S(1)}, u32[]{:S(2)}, u32[]{:S(2)}) collective-permute-start(f32[48,256]{1,0:T(8,128)S(1)} %get-tuple-element.42.after), channel_id=1, source_target_pairs={{0,8},{8,16},{16,24},{1,9},{9,17},{17,25},{2,10},{10,18},{18,26},{... | collective-permute-start | bytes 147464 | tf_op jit(solution)/shard_map/ppermute | solution.py:555
  30.1 9.3 %collective-permute-start.2 = (f32[48,256]{1,0:T(8,128)S(1)}, f32[48,256]{1,0:T(8,128)S(1)}, u32[]{:S(2)}, u32[]{:S(2)}) collective-permute-start(f32[48,256]{1,0:T(8,128)S(1)} %get-tuple-element.41), channel_id=1, source_target_pairs={{8,0},{16,8},{24,16},{9,1},{17,9},{25,17},{10,2},{18,10},{26,18},{... | collective-permute-start | bytes 147464 | tf_op jit(solution)/shard_map/ppermute | solution.py:556
  33.8 5.6 %copy-start.7 = (f32[8]{0:T(128)S(1)}, f32[8]{0:T(128)}, u32[]{:S(2)}) copy-start(f32[8]{0:T(128)} %mass.9) | copy-start | bytes 100
  33.8 5.6 %copy-start.8 = (f32[8]{0:T(128)S(1)}, f32[8]{0:T(128)}, u32[]{:S(2)}) copy-start(f32[8]{0:T(128)} %swim.7) | copy-start | bytes 100
  33.9 5.6 %copy-start.9 = (f32[8]{0:T(128)S(1)}, f32[8]{0:T(128)}, u32[]{:S(2)}) copy-start(f32[8]{0:T(128)} %spread.7) | copy-start | bytes 100
  33.9 9.0 %copy-start.2 = (f32[56,256]{1,0:T(8,128)}, f32[56,256]{1,0:T(8,128)S(1)}, u32[]{:S(2)}) copy-start(f32[56,256]{1,0:T(8,128)S(1)} %collective-permute-done.4.narrow_north) | copy-start | bytes 172036
  33.9 8.9 %copy-start.3 = (f32[56,256]{1,0:T(8,128)}, f32[56,256]{1,0:T(8,128)S(1)}, u32[]{:S(2)}) copy-start(f32[56,256]{1,0:T(8,128)S(1)} %collective-permute-done.5.narrow_south) | copy-start | bytes 172036
  33.9 8.9 %copy-start.4 = (f32[48,256]{1,0:T(8,128)}, f32[48,256]{1,0:T(8,128)S(1)}, u32[]{:S(2)}) copy-start(f32[48,256]{1,0:T(8,128)S(1)} %collective-permute-done.3.south_in) | copy-start | bytes 147460
  39.4 3.4 %copy-start.5 = (f32[48,256]{1,0:T(8,128)}, f32[48,256]{1,0:T(8,128)S(1)}, u32[]{:S(2)}) copy-start(f32[48,256]{1,0:T(8,128)S(1)} %collective-permute-done.2.north_in) | copy-start | bytes 147460
  42.9 21.9 %all-to-all-start = ((f32[8,152,128]{2,1,0:T(8,128)}), f32[8,152,128]{2,1,0:T(8,128)S(1)}, u32[]{:S(2)}, u32[]{:S(2)}) async-start(f32[8,152,128]{2,1,0:T(8,128)} %get-tuple-element.46), calls=%async_computation | async-start | bytes 1245184 | tf_op jit(solution)/shard_map/all_to_all | solution.py:571
  49.7 33.8 %collective-permute-start.6 = (f32[152,128]{1,0:T(8,128)}, f32[152,128]{1,0:T(8,128)}, u32[]{:S(2)}, u32[]{:S(2)}) collective-permute-start(f32[152,128]{1,0:T(8,128)} %get-tuple-element.59), channel_id=1, source_target_pairs={{1,0},{2,1},{3,2},{4,3},{5,4},{6,5},{7,6},{9,8},{10,9},{11,10},{12... | collective-permute-start | bytes 233480 | tf_op jit(solution)/shard_map/ppermute | solution.py:572
  77.9 5.6 %copy-start.11 = (f32[8,16]{1,0:T(8,128)S(1)}, f32[8,16]{1,0:T(8,128)}, u32[]{:S(2)}) copy-start(f32[8,16]{1,0:T(8,128)} %param.29) | copy-start | bytes 1540
  77.9 15.0 %all-to-all-start.2 = ((f32[64,1,128]{2,1,0:T(1,128)}), f32[64,1,128]{2,1,0:T(1,128)S(1)}, u32[]{:S(2)}, u32[]{:S(2)}) async-start(f32[64,1,128]{2,1,0:T(1,128)} %bitcast.5), calls=%async_computation.2 | async-start | bytes 65536 | tf_op jit(solution)/shard_map/all_to_all | solution.py:591
  94.2 23.5 %all-to-all-start.3 = ((f32[8,152,128]{2,1,0:T(8,128)}), f32[8,152,128]{2,1,0:T(8,128)S(1)}, u32[]{:S(2)}, u32[]{:S(2)}) async-start(f32[8,152,128]{2,1,0:T(8,128)} %get-tuple-element.62), calls=%async_computation.3 | async-start | bytes 1245184 | tf_op jit(solution)/shard_map/all_to_all | solution.py:601

commit v6 on v5

--- a/solution.py
+++ b/solution.py
@@ -12,13 +12,12 @@
 EROWS, ECOLS = ROWS + 8, COLS + 128
 LANES = 128
 N = 8
+REGIONS = 16
 WIDE, NARROW = 4, 2
 DENSITY, EAST, NORTH, SEA = 0, 32, 36, 40
 ADJOINT, EFFORT, MASK, REGION, HABITAT = 44, 60, 76, 92, 94
-FIRST_NARROW = ADJOINT
-CORNER = FIRST_NARROW
-STRIP = 96
-WIDE_ROWS, NARROW_ROWS = CORNER + 4, 56
+CORNER = 96
+STRIP = CORNER + 4
 PACKED = 2 * EROWS + 8
 F32 = jnp.float32
 SEPARATE = False
@@ -55,7 +54,7 @@
 
 
 def pack_kernel(*refs):
-    inputs, (to_east, to_west) = refs[:9], refs[9:]
+    inputs, (to_east, to_west, to_north, to_south) = refs[:9], refs[9:]
     lane = lane_iota(ROWS)
     everything = slice(0, ROWS)
     right = jnp.zeros((ROWS, LANES), F32)
@@ -64,30 +63,21 @@
         here = (lane >= place) & (lane < place + width)
         right = jnp.where(here, turned(part(ref, index, everything, slice(LANES, COLS)), place + width), right)
         left = jnp.where(here, turned(part(ref, index, everything, slice(0, LANES)), place), left)
+        columns = slice(0, COLS)
+        to_north[place : place + width, :] = part(ref, index, slice(ROWS - width, ROWS), columns)
+        to_south[place : place + width, :] = part(ref, index, slice(0, width), columns)
     to_east[...] = right
     to_west[...] = left
-
-
-def rows_kernel(*refs):
-    inputs, north, south = refs[:9], refs[10:12], refs[12:14]
-    for ref, index, place, width in every_field(*inputs):
-        narrow = place >= FIRST_NARROW
-        at = place - FIRST_NARROW if narrow else place
-        north[narrow][at : at + width, :] = part(ref, index, slice(ROWS - width, ROWS), slice(0, COLS))
-        south[narrow][at : at + width, :] = part(ref, index, slice(0, width), slice(0, COLS))
-    used = STRIP - FIRST_NARROW
-    for out in (north[1], south[1]):
-        out[used:NARROW_ROWS, :] = jnp.zeros((NARROW_ROWS - used, COLS), F32)
 
 
 def corner_kernel(north_in, south_in, west, east, to_north, to_south):
     if SEPARATE:
         to_north[0:CORNER, :] = north_in[0:CORNER, :]
         to_south[0:CORNER, :] = south_in[0:CORNER, :]
-    to_north[CORNER:WIDE_ROWS, 0:LANES] = west[ROWS - 4 : ROWS, :]
-    to_north[CORNER:WIDE_ROWS, LANES:COLS] = east[ROWS - 4 : ROWS, :]
-    to_south[CORNER:WIDE_ROWS, 0:LANES] = west[0:4, :]
-    to_south[CORNER:WIDE_ROWS, LANES:COLS] = east[0:4, :]
+    to_north[CORNER:STRIP, 0:LANES] = west[ROWS - 4 : ROWS, :]
+    to_north[CORNER:STRIP, LANES:COLS] = east[ROWS - 4 : ROWS, :]
+    to_south[CORNER:STRIP, 0:LANES] = west[0:4, :]
+    to_south[CORNER:STRIP, LANES:COLS] = east[0:4, :]
 
 
 def at_all(out, slots, rows, value):
@@ -186,10 +176,10 @@
 def strips(west_in, east_in, north_in, south_in, west, east):
     west[0:ROWS, :] = west_in[...]
     east[0:ROWS, :] = east_in[...]
-    west[ROWS : ROWS + 4, :] = north_in[CORNER:WIDE_ROWS, 0:LANES]
-    east[ROWS : ROWS + 4, :] = north_in[CORNER:WIDE_ROWS, LANES:COLS]
-    west[ROWS + 4 : EROWS, :] = south_in[CORNER:WIDE_ROWS, 0:LANES]
-    east[ROWS + 4 : EROWS, :] = south_in[CORNER:WIDE_ROWS, LANES:COLS]
+    west[ROWS : ROWS + 4, :] = north_in[CORNER:STRIP, 0:LANES]
+    east[ROWS : ROWS + 4, :] = north_in[CORNER:STRIP, LANES:COLS]
+    west[ROWS + 4 : EROWS, :] = south_in[CORNER:STRIP, 0:LANES]
+    east[ROWS + 4 : EROWS, :] = south_in[CORNER:STRIP, LANES:COLS]
 
 
 def own_cells(ref, index, out):
@@ -204,7 +194,7 @@
     for half in range(2):
         cols = slice(LANES * half, LANES * half + LANES)
         blank = jnp.zeros((8 - 2 * width, LANES), F32)
-        rows = slice(place - FIRST_NARROW, place - FIRST_NARROW + width)
+        rows = slice(place, place + width)
         tiles.append(jnp.concatenate([north_in[rows, cols], blank, south_in[rows, cols]], axis=0))
     lane = lane_iota(8)
     packed = jnp.zeros((8, LANES), F32)
@@ -242,30 +232,73 @@
     return sea * (first[0] + spreading(first[1]) + drifting(first[2], rate, out_rate))
 
 
+def inner_kernel(density, current_east, current_north, sea_mask, after, swim, spread, mass, inner_out):
+    del after
+    flow = (current_east[...], current_north[...], sea_mask[...].astype(F32))
+    inner_out[...] = summed_settled(density, flow, swim, spread, mass)
+
+
+def wide_fields(density, current_east, current_north, sea_mask):
+    for c in range(N):
+        yield density, c, DENSITY + WIDE * c
+    yield current_east, None, EAST
+    yield current_north, None, NORTH
+    yield sea_mask, None, SEA
+
+
+def lat_tile(north_in, south_in, place):
+    rows = slice(place, place + WIDE)
+    return jnp.concatenate([north_in[rows, :], south_in[rows, :]], axis=0)
+
+
 def total_kernel(
-    density, current_east, current_north, sea_mask, adjoint, west_in, east_in, north_in, south_in,
-    narrow_north, narrow_south, after, swim, spread, mass, total_out, tail_out, density_out, flow_out, west, east,
+    density, current_east, current_north, sea_mask, adjoint, west_in, east_in, north_in, south_in, after, inner, swim, spread, mass, total_out, tail_out, west, east,
 ):
     del after
     strips(west_in, east_in, north_in, south_in, west, east)
-    narrow_field(adjoint, 0, ADJOINT, west, east, narrow_north, narrow_south, tail_out)
+    narrow_field(adjoint, 0, ADJOINT, west, east, north_in, south_in, tail_out)
     lane = lane_iota(EROWS)
-    wide = [(density, c, DENSITY + WIDE * c, density_out.at[c]) for c in range(N)]
-    wide += [(current_east, None, EAST, flow_out.at[0]), (current_north, None, NORTH, flow_out.at[1])]
-    wide += [(sea_mask, None, SEA, flow_out.at[2])]
-    for ref, index, place, out in wide:
-        out[0:ROWS, 0:COLS] = part(ref, index, slice(0, ROWS), slice(0, COLS))
-        out[ROWS : ROWS + WIDE, 0:COLS] = north_in[place : place + WIDE, :]
-        out[EROWS - WIDE : EROWS, 0:COLS] = south_in[place : place + WIDE, :]
-        side = jnp.where(lane < WIDE, turned(east[...], -place), 0.0)
-        side = jnp.where(lane >= LANES - WIDE, turned(west[...], LANES - WIDE - place), side)
-        out[:, COLS:ECOLS] = side
-    total = summed_settled(density_out, flow_out, swim, spread, mass)
+    half = LANES // 2
+    row_band, lane_band = [], []
+    for ref, index, place in wide_fields(density, current_east, current_north, sea_mask):
+        lat = lat_tile(north_in, south_in, place)
+        everything, whole = slice(0, ROWS), slice(0, COLS)
+        top = part(ref, index, slice(ROWS - 8, ROWS), whole)
+        bottom = part(ref, index, slice(0, 8), whole)
+        row_band.append(jnp.concatenate([top, lat, bottom], axis=0))
+        low = part(ref, index, everything, slice(0, LANES))
+        high = part(ref, index, everything, slice(LANES, COLS))
+        low = jnp.concatenate([low, lat[:, 0:LANES]], axis=0)
+        high = jnp.concatenate([high, lat[:, LANES:COLS]], axis=0)
+        band = jnp.where(lane < half // 2, low, turned(high, half))
+        band = jnp.where(lane >= half, turned(east[...], half - place), band)
+        band = jnp.where(lane >= half + half // 2, turned(west[...], LANES - WIDE - place), band)
+        lane_band.append(band)
+    rows_total = summed_settled(row_band[0:N], row_band[N:], swim, spread, mass)
+    sides_total = summed_settled(lane_band[0:N], lane_band[N:], swim, spread, mass)
     slots = total_out.shape[0]
-    at_all(total_out, slots, slice(0, EROWS), total[:, 0:LANES])
-    at_all(total_out, slots, slice(EROWS, 2 * EROWS), total[:, LANES:COLS])
-    sides = [total[8 * k : 8 * k + 8, COLS:ECOLS] for k in range(EROWS // 8)]
-    at_all(total_out, slots, slice(2 * EROWS, PACKED), packed_side(sides))
+    row = lax.broadcasted_iota(jnp.int32, (8, LANES), 0)
+    lane = lane_iota(8)
+    packed = jnp.zeros((8, LANES), F32)
+    for k in range(EROWS // 8):
+        sides = sides_total[8 * k : 8 * k + 8]
+        for side in range(2):
+            cols = slice(LANES * side, LANES * side + LANES)
+            tile = inner[8 * k : 8 * k + 8, cols] if k < ROWS // 8 else rows_total[8:16, cols]
+            if k == 0:
+                tile = jnp.where(row < 2, rows_total[16:24, cols], tile)
+            if k == ROWS // 8 - 1:
+                tile = jnp.where(row >= 6, rows_total[0:8, cols], tile)
+            if side == 0:
+                tile = jnp.where(lane < NARROW, sides, tile)
+            else:
+                tile = jnp.where(lane >= LANES - NARROW, turned(sides, half), tile)
+            at_all(total_out, slots, slice(EROWS * side + 8 * k, EROWS * side + 8 * k + 8), tile)
+        here = (lane >= 4 * k) & (lane < 4 * k + 2)
+        packed = jnp.where(here, turned(sides, 4 * k + 2), packed)
+        here = (lane >= 4 * k + 2) & (lane < 4 * k + 4)
+        packed = jnp.where(here, turned(sides, 4 * k + 2 - half), packed)
+    at_all(total_out, slots, slice(2 * EROWS, PACKED), packed)
 
 
 def fleet_rows(rows, efforts, reported_out, fishing_out, mortality, selectivity):
@@ -298,9 +331,9 @@
 
 
 def settle_kernel(
-    fishing, reported, region, adjoint, habitat, west_in, east_in, north_in, south_in,
-    narrow_north, narrow_south, density, flow, swim, spread, mortality, selectivity,
-    settled_out, fishing_out, reported_out, region_out, carried_out, habitat_out, west, east, efforts,
+    fishing, reported, region, adjoint, habitat, west_in, east_in, north_in, south_in, density, current_east, current_north, sea_mask, swim, spread, mortality, selectivity,
+    settled_out, fishing_out, reported_out, region_out, carried_out, habitat_out, flow_out, west, east, efforts,
+    density_ext,
 ):
     for source, out in ((fishing, fishing_out), (reported, reported_out), (region, region_out)):
         if SEPARATE:
@@ -308,75 +341,89 @@
     strips(west_in, east_in, north_in, south_in, west, east)
 
     def halo(place, out):
-        for top, tile in zip(HALO_ROWS, halo_cells(place, west, east, narrow_north, narrow_south), strict=True):
+        for top, tile in zip(HALO_ROWS, halo_cells(place, west, east, north_in, south_in), strict=True):
             out[top : top + 8, :] = tile
 
     for k in range(N):
-        narrow_field(adjoint, k, ADJOINT + NARROW * k, west, east, narrow_north, narrow_south, carried_out.at[k])
+        narrow_field(adjoint, k, ADJOINT + NARROW * k, west, east, north_in, south_in, carried_out.at[k])
         halo(EFFORT + NARROW * k, efforts.at[k])
         halo(MASK + NARROW * k, reported_out.at[k])
     halo(REGION, region_out)
-    narrow_field(habitat, None, HABITAT, west, east, narrow_north, narrow_south, habitat_out)
+    narrow_field(habitat, None, HABITAT, west, east, north_in, south_in, habitat_out)
     for top in HALO_ROWS:
         fleet_rows(slice(top, top + 8), efforts, reported_out, fishing_out, mortality, selectivity)
 
+    lane = lane_iota(EROWS)
+    outs = [density_ext.at[c] for c in range(N)] + [flow_out.at[k] for k in range(3)]
+    for (ref, index, place), out in zip(
+        wide_fields(density, current_east, current_north, sea_mask), outs, strict=True
+    ):
+        out[0:ROWS, 0:COLS] = part(ref, index, slice(0, ROWS), slice(0, COLS))
+        out[ROWS:EROWS, 0:COLS] = lat_tile(north_in, south_in, place)
+        side = jnp.where(lane < WIDE, turned(east[...], -place), 0.0)
+        side = jnp.where(lane >= LANES - WIDE, turned(west[...], LANES - WIDE - place), side)
+        out[:, COLS:ECOLS] = side
+
     def cohort(c, carry):
-        coefs, sea = coeffs(flow, swim[c], spread[c]), flow[2]
-        pack_into(settled_out, c, advance(advance(density[c], coefs, sea), coefs, sea))
+        coefs, sea = coeffs(flow_out, swim[c], spread[c]), flow_out[2]
+        pack_into(settled_out, c, advance(advance(density_ext[c], coefs, sea), coefs, sea))
         return carry
 
     lax.fori_loop(0, N, cohort, 0)
 
 
 def catch_kernel(
-    age, received, settled, fishing, reported, region, mass, selectivity, mort_out, catch_out, older, fleets
+    age, received, settled, fishing, reported, region, mass, selectivity, mort_out, catch_out, older, fleets, table
 ):
     shard = age[0]
     older[...] = picked(received, lambda slot: slot > shard)
 
+    def mortality_of(rows):
+        run = older[rows, :]
+        for c in reversed(range(N)):
+            total_mort = fishing[c, rows, :] + 0.02 * run
+            mort_out[c, rows, :] = total_mort
+            weighted = mass[c] * settled[c, rows, :]
+            run = run + weighted
+            yield c, total_mort, weighted
+
     def pair(t, carry):
-        places = [pl.ds(pl.multiple_of(t * 8, 8), 8), pl.ds(pl.multiple_of(EROWS + t * 8, 8), 8)]
-        for rows in places:
-            run = older[rows, :]
+        for top in (0, EROWS):
+            rows = pl.ds(pl.multiple_of(top + t * 8, 8), 8)
             taken = [jnp.zeros((8, LANES), F32) for _ in range(N)]
-            for c in reversed(range(N)):
-                total_mort = fishing[c, rows, :] + 0.02 * run
-                mort_out[c, rows, :] = total_mort
-                weighted = mass[c] * settled[c, rows, :]
+            for c, total_mort, weighted in mortality_of(rows):
                 landed = weighted * ((1.0 - jnp.exp(-total_mort)) / total_mort)
                 for f in range(N):
                     taken[f] = taken[f] + selectivity[f, c] * landed
-                run = run + weighted
             for f in range(N):
                 fleets[f, rows, :] = taken[f] * reported[f, rows, :]
         return carry
 
-    lax.fori_loop(0, EROWS // 8, pair, 0)
-    rows = slice(2 * EROWS, PACKED)
-    run = older[rows, :]
-    for c in reversed(range(N)):
-        mort_out[c, rows, :] = fishing[c, rows, :] + 0.02 * run
-        run = run + mass[c] * settled[c, rows, :]
-
-    lane = lane_iota(N)
-    fleet = lax.broadcasted_iota(jnp.int32, (N, LANES), 0)
-
-    def one_region(r, table):
-        sums = [jnp.zeros((8, LANES), F32) for _ in range(N)]
+    lax.fori_loop(0, ROWS // 8, pair, 0)
+    for top in HALO_ROWS:
+        for _ in mortality_of(slice(top, top + 8)):
+            pass
+    half_regions = REGIONS // 2
+
+    def two_regions(r, carry):
+        sums = [[jnp.zeros((8, LANES), F32) for _ in range(N)] for _ in range(2)]
         for half in range(2):
             for t in range(ROWS // 8):
                 rows = slice(EROWS * half + 8 * t, EROWS * half + 8 * t + 8)
-                here = region[rows, :] == r.astype(F32)
+                place = region[rows, :]
+                here = [place == (r + k * half_regions).astype(F32) for k in range(2)]
                 for f in range(N):
-                    sums[f] = sums[f] + jnp.where(here, fleets[f, rows, :], 0.0)
+                    fleet = fleets[f, rows, :]
+                    for k in range(2):
+                        sums[k][f] = sums[k][f] + jnp.where(here[k], fleet, 0.0)
         for f in range(N):
-            column = jnp.sum(sums[f], axis=0, keepdims=True)
-            column = jnp.sum(column, axis=1, keepdims=True)
-            table = jnp.where((fleet == f) & (lane == r + 16 * f), column, table)
-        return table
-
-    table = lax.fori_loop(0, 16, one_region, jnp.zeros((N, LANES), F32))
-    row = jnp.sum(table, axis=0, keepdims=True)
+            for k in range(2):
+                rows = pl.ds(f * REGIONS + r + k * half_regions, 1)
+                table[rows, :] = jnp.sum(sums[k][f], axis=0, keepdims=True)
+        return carry
+
+    lax.fori_loop(0, half_regions, two_regions, 0)
+    row = jnp.sum(jnp.transpose(table[...]), axis=0, keepdims=True)
     catch_out[...] = jnp.broadcast_to(row, catch_out.shape)
 
 
@@ -537,54 +584,51 @@
     density, adjoint_next, effort, catch_mask, current_east, current_north, region, sea_mask, habitat = inputs
     packed = (PACKED, LANES)
     extended = (EROWS, ECOLS)
-    to_east, to_west = call(pack_kernel, [VMEM] * 9, [shape(ROWS, LANES)] * 2)(*inputs)
+    to_east, to_west, to_north, to_south = call(
+        pack_kernel, [VMEM] * 9, [shape(ROWS, LANES)] * 2 + [shape(STRIP, COLS)] * 2
+    )(*inputs)
     from_west = lax.ppermute(to_east, "lon", [(i, (i + 1) % lons) for i in range(lons)])
     from_east = lax.ppermute(to_west, "lon", [((i + 1) % lons, i) for i in range(lons)])
-    to_north, narrow_north, to_south, narrow_south = call(
-        rows_kernel, [VMEM] * 10, [shape(WIDE_ROWS, COLS), shape(NARROW_ROWS, COLS)] * 2
-    )(*inputs, near(to_east))
-    northward = [(i, i + 1) for i in range(lats - 1)]
-    southward = [(i + 1, i) for i in range(lats - 1)]
-    narrow_south, narrow_north = (
-        lax.ppermute(narrow_north, "lat", northward),
-        lax.ppermute(narrow_south, "lat", southward),
-    )
     to_north, to_south = call(
-        corner_kernel, [VMEM] * 4, [shape(WIDE_ROWS, COLS)] * 2, (), {0: 0, 1: 1}
+        corner_kernel, [VMEM] * 4, [shape(STRIP, COLS)] * 2, (), {0: 0, 1: 1}
     )(near(to_north), near(to_south), near(from_west), near(from_east))
-    from_south = lax.ppermute(to_north, "lat", northward)
-    from_north = lax.ppermute(to_south, "lat", southward)
-    halos = (from_west, from_east, from_north, from_south, narrow_north, narrow_south)
+    from_south = lax.ppermute(to_north, "lat", [(i, i + 1) for i in range(lats - 1)])
+    from_north = lax.ppermute(to_south, "lat", [(i + 1, i) for i in range(lats - 1)])
+    halos = (from_west, from_east, from_north, from_south)
 
     fishing, reported, regions = call(
         fleet_kernel, [VMEM] * 4 + [SMEM] * 2, [shape(N, *packed)] * 2 + [shape(*packed)], [(N, *packed)]
     )(effort, catch_mask, region, near(to_north), mortality, selectivity)
-    totals, tail, density_ext, flow = call(
-        total_kernel,
-        [VMEM] * 12 + [SMEM] * 3,
-        [shape(ages, *packed), shape(*packed), shape(N, *extended), far(3, *extended)],
-        [(EROWS, LANES), (EROWS, LANES)],
+    (inner,) = call(inner_kernel, [VMEM] * 5 + [SMEM] * 3, [shape(ROWS, COLS)])(
+        density, current_east, current_north, sea_mask, near(to_east), swim_speed, diffusion, cohort_mass
+    )
+    totals, tail = call(
+        total_kernel, [VMEM] * 11 + [SMEM] * 3, [shape(ages, *packed), shape(*packed)], [(EROWS, LANES), (EROWS, LANES)]
     )(
-        density, current_east, current_north, sea_mask, adjoint_next, *map(near, halos), near(regions),
+        density, current_east, current_north, sea_mask, adjoint_next, *map(near, halos), near(regions), near(inner),
         swim_speed, diffusion, cohort_mass,
     )
     totals = lax.all_to_all(totals, "age", 0, 0, tiled=True)
     tail = lax.ppermute(tail, "age", [(i + 1, i) for i in range(ages - 1)])
 
-    settled, fishing, reported, regions, carried, habitats = call(
+    settled, fishing, reported, regions, carried, habitats, flow = call(
         settle_kernel,
         [VMEM] * 13 + [SMEM] * 4,
-        [shape(N, *packed)] * 3 + [shape(*packed), far(N, *packed), far(*packed)],
-        [(EROWS, LANES), (EROWS, LANES), (N, *packed)],
+        [shape(N, *packed)] * 3 + [shape(*packed), far(N, *packed), far(*packed), far(3, *extended)],
+        [(EROWS, LANES), (EROWS, LANES), (N, *packed), (N, *extended)],
         {0: 1, 1: 2, 2: 3},
     )(
         near(fishing), near(reported), near(regions), adjoint_next, habitat,
-        *distant(*halos), near(density_ext), *distant(flow), swim_speed, diffusion, mortality, selectivity,
+        *distant(*halos), density, current_east, current_north, sea_mask,
+        swim_speed, diffusion, mortality, selectivity,
     )
     settled, reported, regions = near(settled), near(reported), near(regions)
 
     mort, catches = call(
-        catch_kernel, [SMEM] + [VMEM] * 5 + [SMEM] * 2, [shape(N, *packed), shape(ages, LANES)], [packed, (N, *packed)]
+        catch_kernel,
+        [SMEM] + [VMEM] * 5 + [SMEM] * 2,
+        [shape(N, *packed), shape(ages, LANES)],
+        [packed, (N, *packed), (LANES, LANES)],
     )(age, near(totals), settled, near(fishing), reported, regions, cohort_mass, selectivity)
     catches = near(lax.all_to_all(catches, "age", 0, 0, tiled=True))
     (catches,) = call(relay_kernel, [VMEM], [shape(lons * lats, LANES)])(catches)

time: 121 us -> 117 us (0.967)
  waiting for transfers between devices: 34.3 us -> 32.8 us
    ppermute x4 -> x2, starting transfers between devices: 15.5 us -> 11.8 us  [the longest x1 9.92 us: month(): lax.ppermute(to_north, 'lat', [(i, i + 1) for i in range(lats - 1)])]
    all_to_all x1, starting transfers between devices: 5.56 us -> 8.89 us  [month(): catches = near(lax.all_to_all(catches, ('lon', 'lat'), 0, 0, tiled=True))]
    all_to_all x2, waiting for transfers between devices: 22.8 us -> 21.3 us  [month(): totals = lax.all_to_all(totals, 'age', 0, 0, tiled=True)]
    ppermute x4 -> x2, waiting for transfers between devices: 5.5 us -> 4.52 us  [the longest x1 4.51 us: month(): lax.ppermute(to_south, 'lat', [(i + 1, i) for i in range(lats - 1)])]
  transfers between devices with their start and end apart: 10 -> 8, of which waited for: 4 -> 5; matrix products, arithmetic and copies ran while one was open for 0% -> 0% of each run, Pallas kernels for 18% -> 18%
where the time goes in v6:
time: 117 us
  starting transfers between devices  44.9 us (38%)
  waiting for transfers between devices  32.8 us (28%)
  Pallas kernels  29.7 us (25%)
  blocking collectives  8.92 us (8%)
    all_to_all x2, waiting for transfers between devices, month(): totals = lax.all_to_all(totals, 'age', 0, 0, tiled=True)  21.3 us
    all_to_all x2, starting transfers between devices, month(): totals = lax.all_to_all(totals, 'age', 0, 0, tiled=True)  10.4 us
    ppermute x1, starting transfers between devices, month(): lax.ppermute(to_north, 'lat', [(i, i + 1) for i in range(lats - 1)])  9.92 us
    all_to_all x1, blocking collectives, month(): catches = near(lax.all_to_all(catches, 'age', 0, 0, tiled=True))  8.92 us
    all_to_all x1, starting transfers between devices, month(): catches = near(lax.all_to_all(catches, ('lon', 'lat'), 0, 0, tiled=True))  8.89 us
    ppermute x1, starting transfers between devices, month(): lax.ppermute(to_west, 'lon', [((i + 1) % lons, i) for i in range(lons)])  7.73 us
    all_to_all x1, waiting for transfers between devices, month(): catches = near(lax.all_to_all(catches, ('lon', 'lat'), 0, 0, tiled=True))  6 us
    pallas_call x1, Pallas kernels, month(): call(own_kernel, [VMEM] * 8 + [SMEM] * 4, [shape(N, ROWS, COLS), shape(3,...  5.95 us
  transfers between devices with their start and end apart: 8, of which 5 were waited for; matrix products, arithmetic and copies ran while one was open for 0% of the time, Pallas kernels for 18%

profile of v6, /device:TPU:1, one launch (start us, length us, event | category | flops | bytes accessed | tf_op | source)
XLA Modules:
  0.0 116.8 jit_solution(10298243697401493375)
XLA Ops:
  0.0 2.3 %shard_map.145 = (f32[64,128]{1,0:T(8,128)S(1)}, f32[64,128]{1,0:T(8,128)S(1)}, f32[100,256]{1,0:T(8,128)S(1)}, f32[100,256]{1,0:T(8,128)S(1)}) custom-call(f32[8,64,256]{2,1,0:T(8,128)} %density.5, f32[8,64,256]{2,1,0:T(8,128)} %adjoint.3, f32[8,64,256]{2,1,0:T(8,128)} %effort.1, s32[8,64,256]{2,1,0:T(8,128)} %mask.1, f32[64,256]{1,0:T(8,128)} %current_east.5, ...), custom_call_target="tpu_custom_call" | custom-call | tf_op jit(solution)/shard_map/pallas_call | solution.py:587
  2.3 4.8 %collective-permute-start = (f32[64,128]{1,0:T(8,128)S(1)}, f32[64,128]{1,0:T(8,128)S(1)}, u32[]{:S(2)}, u32[]{:S(2)}) collective-permute-start(f32[64,128]{1,0:T(8,128)S(1)} %get-tuple-element.34.after), channel_id=1, source_target_pairs={{0,32},{32,64},{64,96},{96,128},{128,160},{160,192},{192,224},{224... | collective-permute-start | bytes 98312 | tf_op jit(solution)/shard_map/ppermute | solution.py:590
  7.1 7.7 %collective-permute-start.1 = (f32[64,128]{1,0:T(8,128)S(1)}, f32[64,128]{1,0:T(8,128)S(1)}, u32[]{:S(2)}, u32[]{:S(2)}) collective-permute-start(f32[64,128]{1,0:T(8,128)S(1)} %get-tuple-element.35), channel_id=1, source_target_pairs={{32,0},{64,32},{96,64},{128,96},{160,128},{192,160},{224,192},{256... | collective-permute-start | bytes 98312 | tf_op jit(solution)/shard_map/ppermute | solution.py:591
  14.9 1.0 collective-permute-done.1.east.east_in
  15.9 9.9 %collective-permute-start.3 = (f32[100,256]{1,0:T(8,128)S(1)}, f32[100,256]{1,0:T(8,128)S(1)}, u32[]{:S(2)}, u32[]{:S(2)}) collective-permute-start(f32[100,256]{1,0:T(8,128)S(1)} %get-tuple-element.39.after), channel_id=1, source_target_pairs={{0,8},{8,16},{16,24},{1,9},{9,17},{17,25},{2,10},{10,18},{18,26},{... | collective-permute-start | bytes 307208 | tf_op jit(solution)/shard_map/ppermute | solution.py:595
  25.8 1.9 %collective-permute-start.2 = (f32[100,256]{1,0:T(8,128)S(1)}, f32[100,256]{1,0:T(8,128)S(1)}, u32[]{:S(2)}, u32[]{:S(2)}) collective-permute-start(f32[100,256]{1,0:T(8,128)S(1)} %get-tuple-element.38), channel_id=1, source_target_pairs={{8,0},{16,8},{24,16},{9,1},{17,9},{25,17},{10,2},{18,10},{26,18},{... | collective-permute-start | bytes 307208 | tf_op jit(solution)/shard_map/ppermute | solution.py:596
  27.8 1.6 %shard_map.148.inner = f32[64,256]{1,0:T(8,128)S(1)} custom-call(f32[8,64,256]{2,1,0:T(8,128)} %density.5, f32[64,256]{1,0:T(8,128)} %current_east.5, f32[64,256]{1,0:T(8,128)} %current_north.5, s32[64,256]{1,0:T(8,128)} %sea_mask.5, f32[64,128]{1,0:T(8,128)S(1)} %get-tuple-element.34.after, f32[8]{0:T(128)S(1)} %copy-done.6, f32[8]{0:T(128)S(1)} %copy-done.7, ...), custom_call_target="tpu_custom_call" | custom-call | tf_op jit(solution)/shard_map/pallas_call | solution.py:602
  29.5 1.8 %shard_map.147 = (f32[8,152,128]{2,1,0:T(8,128)S(1)}, f32[8,152,128]{2,1,0:T(8,128)S(1)}, f32[152,128]{1,0:T(8,128)S(1)}) custom-call(f32[8,64,256]{2,1,0:T(8,128)} %effort.1, s32[8,64,256]{2,1,0:T(8,128)} %mask.1, s32[64,256]{1,0:T(8,128)} %region.1, f32[100,256]{1,0:T(8,128)S(1)} %get-tuple-element.39.after, f32[8]{0:T(128)S(1)} %copy-done.8, ...), custom_call_target="tpu_custom_call" | custom-call | tf_op jit(solution)/shard_map/pallas_call | solution.py:599
  31.3 4.5 %collective-permute-done.2.north_in = f32[100,256]{1,0:T(8,128)S(1)} collective-permute-done((f32[100,256]{1,0:T(8,128)S(1)}, f32[100,256]{1,0:T(8,128)S(1)}, u32[]{:S(2)}, u32[]{:S(2)}) %collective-permute-start.2) | collective-permute-done | bytes 102432 | tf_op jit(solution)/shard_map/ppermute | solution.py:596
  35.8 3.0 %shard_map.149 = (f32[8,152,128]{2,1,0:T(8,128)}, f32[152,128]{1,0:T(8,128)S(1)}) custom-call(f32[8,64,256]{2,1,0:T(8,128)} %density.5, f32[64,256]{1,0:T(8,128)} %current_east.5, f32[64,256]{1,0:T(8,128)} %current_north.5, s32[64,256]{1,0:T(8,128)} %sea_mask.5, f32[8,64,256]{2,1,0:T(8,128)} %adjoint.3, f32[64,128]{1,0:T(8,128)S(1)} %collective-permute-done.west.west_in, ...), custom_call_target="tpu_custom_call" | custom-call | tf_op jit(solution)/shard_map/pallas_call | solution.py:605
  38.8 6.8 %all-to-all-start = ((f32[8,152,128]{2,1,0:T(8,128)}), f32[8,152,128]{2,1,0:T(8,128)S(1)}, u32[]{:S(2)}, u32[]{:S(2)}) async-start(f32[8,152,128]{2,1,0:T(8,128)} %get-tuple-element.41), calls=%async_computation | async-start | bytes 1245184 | tf_op jit(solution)/shard_map/all_to_all | solution.py:611
  45.7 1.3 %collective-permute-start.4 = (f32[152,128]{1,0:T(8,128)S(1)}, f32[152,128]{1,0:T(8,128)S(1)}, u32[]{:S(2)}, u32[]{:S(2)}) collective-permute-start(f32[152,128]{1,0:T(8,128)S(1)} %get-tuple-element.52), channel_id=1, source_target_pairs={{1,0},{2,1},{3,2},{4,3},{5,4},{6,5},{7,6},{9,8},{10,9},{11,10},{12... | collective-permute-start | bytes 233480 | tf_op jit(solution)/shard_map/ppermute | solution.py:612
  47.0 5.2 %shard_map.150 = (f32[8,152,128]{2,1,0:T(8,128)S(1)}, f32[8,152,128]{2,1,0:T(8,128)S(1)}, f32[8,152,128]{2,1,0:T(8,128)S(1)}, f32[152,128]{1,0:T(8,128)S(1)}, f3...) custom-call(f32[8,152,128]{2,1,0:T(8,128)S(1)} %get-tuple-element.42, ...), custom_call_target="tpu_custom_call", output_to_operand_aliasing={{1}: (0, {}), {2}: (1, {}), {3}: (2, {})} | custom-call | tf_op jit(solution)/shard_map/pallas_call | solution.py:614
  52.3 7.3 %all-to-all-done.received = f32[8,152,128]{2,1,0:T(8,128)S(1)} async-done(((f32[8,152,128]{2,1,0:T(8,128)}), f32[8,152,128]{2,1,0:T(8,128)S(1)}, u32[]{:S(2)}, u32[]{:S(2)}) %all-to-all-start) | async-done | bytes 622624 | tf_op jit(solution)/shard_map/all_to_all | solution.py:611
  59.6 2.4 %shard_map.151 = (f32[8,152,128]{2,1,0:T(8,128)S(1)}, f32[8,128]{1,0:T(8,128)S(1)}) custom-call(s32[2]{0:T(128)S(1)} %pad_add_fusion.age, f32[8,152,128]{2,1,0:T(8,128)S(1)} %all-to-all-done.received, f32[8,152,128]{2,1,0:T(8,128)S(1)} %get-tuple-element.44.settled, f32[8,152,128]{2,1,0:T(8,128)S(1)} %get-tuple-element.45.fishing, ...), custom_call_target="tpu_custom_call" | custom-call | tf_op jit(solution)/shard_map/pallas_call | solution.py:627
  62.0 8.9 %all_to_all.32 = f32[8,1,128]{2,1,0:T(1,128)S(1)} all-to-all(f32[8,1,128]{2,1,0:T(1,128)S(1)} %bitcast.11), channel_id=1, replica_groups=mesh['lon'=16,'lat'=4,'age'=8] {'age'}, dimensions={0} | all-to-all | bytes 8192 | tf_op jit(solution)/shard_map/all_to_all | solution.py:633
  71.5 8.9 %all-to-all-start.2 = ((f32[64,1,128]{2,1,0:T(1,128)}), f32[64,1,128]{2,1,0:T(1,128)S(1)}, u32[]{:S(2)}, u32[]{:S(2)}) async-start(f32[64,1,128]{2,1,0:T(1,128)} %bitcast.5), calls=%async_computation.2 | async-start | bytes 65536 | tf_op jit(solution)/shard_map/all_to_all | solution.py:635
  80.5 3.4 %shard_map.153 = (f32[152,128]{1,0:T(8,128)S(1)}, f32[8,152,128]{2,1,0:T(8,128)S(1)}, f32[8,152,128]{2,1,0:T(8,128)}, f32[8,152,128]{2,1,0:T(8,128)}, f32[8,152,128]{2,1,0:T(8,128)}) custom-call(s32[2]{0:T(128)S(1)} %pad_add_fusion.age, f32[8,152,128]{2,1,0:T(8,128)S(1)} %get-tuple-element.49.mort, f32[8,152,128]{2,1,0:T(8,128)S(1)} %get-tuple-element.44.settled, ...), custom_call_target="tpu_custom_call" | custom-call | tf_op jit(solution)/shard_map/pallas_call | solution.py:637
  83.9 6.0 %all-to-all-done.2 = f32[64,1,128]{2,1,0:T(1,128)S(1)} async-done(((f32[64,1,128]{2,1,0:T(1,128)}), f32[64,1,128]{2,1,0:T(1,128)S(1)}, u32[]{:S(2)}, u32[]{:S(2)}) %all-to-all-start.2) | async-done | bytes 32800 | tf_op jit(solution)/shard_map/all_to_all | solution.py:635
  89.9 1.3 %shard_map.154 = (f32[8,128]{1,0:T(8,128)S(1)}, f32[8,152,128]{2,1,0:T(8,128)}) custom-call(f32[64,128]{1,0:T(8,128)S(1)} %bitcast.9, f32[1,128]{1,0:T(1,128)S(1)} %reshape.7.observed, f32[152,128]{1,0:T(8,128)S(1)} %get-tuple-element.47.region, f32[152,128]{1,0:T(8,128)S(1)} %get-tuple-element.53.still, f32[8,152,128]{2,1,0:T(8,128)S(1)} %get-tuple-element.54.reach), custom_call_target="tpu_custom_call" | custom-call | tf_op jit(solution)/shard_map/pallas_call | solution.py:642
  91.2 3.5 %all-to-all-start.3 = ((f32[8,152,128]{2,1,0:T(8,128)}), f32[8,152,128]{2,1,0:T(8,128)S(1)}, u32[]{:S(2)}, u32[]{:S(2)}) async-start(f32[8,152,128]{2,1,0:T(8,128)} %get-tuple-element.55), calls=%async_computation.3 | async-start | bytes 1245184 | tf_op jit(solution)/shard_map/all_to_all | solution.py:645
  94.8 6.0 %shard_map.155 = (f32[8,64,256]{2,1,0:T(8,128)S(1)}, f32[3,72,384]{2,1,0:T(8,128)S(1)}) custom-call(f32[8,128]{1,0:T(8,128)S(1)} %get-tuple-element.56.misfit_in, f32[152,128]{1,0:T(8,128)S(1)} %get-tuple-element.47.region, f32[8,152,128]{2,1,0:T(8,128)S(1)} %get-tuple-element.46.reported, f32[8,152,128]{2,1,0:T(8,128)S(1)} %get-tuple-element.44.settled, ...), custom_call_target="tpu_custom_call" | custom-call | tf_op jit(solution)/shard_map/pallas_call | solution.py:648
  100.8 14.0 %all-to-all-done.3.received = f32[8,152,128]{2,1,0:T(8,128)S(1)} async-done(((f32[8,152,128]{2,1,0:T(8,128)}), f32[8,152,128]{2,1,0:T(8,128)S(1)}, u32[]{:S(2)}, u32[]{:S(2)}) %all-to-all-start.3) | async-done | bytes 622624 | tf_op jit(solution)/shard_map/all_to_all | solution.py:645
  114.8 2.0 %shard_map.156 = f32[8,64,256]{2,1,0:T(8,128)} custom-call(s32[2]{0:T(128)S(1)} %pad_add_fusion.age, f32[8,152,128]{2,1,0:T(8,128)S(1)} %all-to-all-done.3.received, f32[8,64,256]{2,1,0:T(8,128)S(1)} %get-tuple-element.61.own, f32[3,72,384]{2,1,0:T(8,128)S(1)} %get-tuple-element.62.flow, f32[8]{0:T(128)S(1)} %copy-done.6, f32[8]{0:T(128)S(1)} %copy-done.7, ...), custom_call_target="tpu_custom_call" | custom-call | tf_op jit(solution)/shard_map/pallas_call | solution.py:651
  (27 shorter events, 0.8 us)
Async XLA Ops:
  2.3 12.6 %collective-permute-start = (f32[64,128]{1,0:T(8,128)S(1)}, f32[64,128]{1,0:T(8,128)S(1)}, u32[]{:S(2)}, u32[]{:S(2)}) collective-permute-start(f32[64,128]{1,0:T(8,128)S(1)} %get-tuple-element.34.after), channel_id=1, source_target_pairs={{0,32},{32,64},{64,96},{96,128},{128,160},{160,192},{192,224},{224... | collective-permute-start | bytes 98312 | tf_op jit(solution)/shard_map/ppermute | solution.py:590
  7.1 8.7 %collective-permute-start.1 = (f32[64,128]{1,0:T(8,128)S(1)}, f32[64,128]{1,0:T(8,128)S(1)}, u32[]{:S(2)}, u32[]{:S(2)}) collective-permute-start(f32[64,128]{1,0:T(8,128)S(1)} %get-tuple-element.35), channel_id=1, source_target_pairs={{32,0},{64,32},{96,64},{128,96},{160,128},{192,160},{224,192},{256... | collective-permute-start | bytes 98312 | tf_op jit(solution)/shard_map/ppermute | solution.py:591
  14.9 20.9 %copy-start.2 = (f32[64,128]{1,0:T(8,128)}, f32[64,128]{1,0:T(8,128)S(1)}, u32[]{:S(2)}) copy-start(f32[64,128]{1,0:T(8,128)S(1)} %collective-permute-done.west.west_in) | copy-start | bytes 98308
  15.9 19.9 %copy-start.3 = (f32[64,128]{1,0:T(8,128)}, f32[64,128]{1,0:T(8,128)S(1)}, u32[]{:S(2)}) copy-start(f32[64,128]{1,0:T(8,128)S(1)} %collective-permute-done.1.east.east_in) | copy-start | bytes 98308
  15.9 11.9 %copy-start.5 = (f32[8]{0:T(128)S(1)}, f32[8]{0:T(128)}, u32[]{:S(2)}) copy-start(f32[8]{0:T(128)} %mass.11) | copy-start | bytes 100
  15.9 11.9 %copy-start.6 = (f32[8]{0:T(128)S(1)}, f32[8]{0:T(128)}, u32[]{:S(2)}) copy-start(f32[8]{0:T(128)} %swim.9) | copy-start | bytes 100
  15.9 11.9 %copy-start.7 = (f32[8]{0:T(128)S(1)}, f32[8]{0:T(128)}, u32[]{:S(2)}) copy-start(f32[8]{0:T(128)} %spread.9) | copy-start | bytes 100
  15.9 15.3 %collective-permute-start.3 = (f32[100,256]{1,0:T(8,128)S(1)}, f32[100,256]{1,0:T(8,128)S(1)}, u32[]{:S(2)}, u32[]{:S(2)}) collective-permute-start(f32[100,256]{1,0:T(8,128)S(1)} %get-tuple-element.39.after), channel_id=1, source_target_pairs={{0,8},{8,16},{16,24},{1,9},{9,17},{17,25},{2,10},{10,18},{18,26},{... | collective-permute-start | bytes 307208 | tf_op jit(solution)/shard_map/ppermute | solution.py:595
  25.8 3.6 %copy-start.4 = (f32[8,8]{1,0:T(8,128)S(1)}, f32[8,8]{1,0:T(8,128)}, u32[]{:S(2)}) copy-start(f32[8,8]{1,0:T(8,128)} %selectivity.9) | copy-start | bytes 772
  25.8 3.6 %copy-start.8 = (f32[8]{0:T(128)S(1)}, f32[8]{0:T(128)}, u32[]{:S(2)}) copy-start(f32[8]{0:T(128)} %mortality.3) | copy-start | bytes 100
  25.8 9.9 %collective-permute-start.2 = (f32[100,256]{1,0:T(8,128)S(1)}, f32[100,256]{1,0:T(8,128)S(1)}, u32[]{:S(2)}, u32[]{:S(2)}) collective-permute-start(f32[100,256]{1,0:T(8,128)S(1)} %get-tuple-element.38), channel_id=1, source_target_pairs={{8,0},{16,8},{24,16},{9,1},{17,9},{25,17},{10,2},{18,10},{26,18},{... | collective-permute-start | bytes 307208 | tf_op jit(solution)/shard_map/ppermute | solution.py:596
  31.3 7.6 %copy-start = (f32[100,256]{1,0:T(8,128)}, f32[100,256]{1,0:T(8,128)S(1)}, u32[]{:S(2)}) copy-start(f32[100,256]{1,0:T(8,128)S(1)} %collective-permute-done.3.south_in) | copy-start | bytes 307204
  35.8 3.1 %copy-start.1 = (f32[100,256]{1,0:T(8,128)}, f32[100,256]{1,0:T(8,128)S(1)}, u32[]{:S(2)}) copy-start(f32[100,256]{1,0:T(8,128)S(1)} %collective-permute-done.2.north_in) | copy-start | bytes 307204
  38.8 20.7 %all-to-all-start = ((f32[8,152,128]{2,1,0:T(8,128)}), f32[8,152,128]{2,1,0:T(8,128)S(1)}, u32[]{:S(2)}, u32[]{:S(2)}) async-start(f32[8,152,128]{2,1,0:T(8,128)} %get-tuple-element.41), calls=%async_computation | async-start | bytes 1245184 | tf_op jit(solution)/shard_map/all_to_all | solution.py:611
  45.7 34.9 %collective-permute-start.4 = (f32[152,128]{1,0:T(8,128)S(1)}, f32[152,128]{1,0:T(8,128)S(1)}, u32[]{:S(2)}, u32[]{:S(2)}) collective-permute-start(f32[152,128]{1,0:T(8,128)S(1)} %get-tuple-element.52), channel_id=1, source_target_pairs={{1,0},{2,1},{3,2},{4,3},{5,4},{6,5},{7,6},{9,8},{10,9},{11,10},{12... | collective-permute-start | bytes 233480 | tf_op jit(solution)/shard_map/ppermute | solution.py:612
  71.5 8.9 %copy-start.9 = (f32[8,16]{1,0:T(8,128)S(1)}, f32[8,16]{1,0:T(8,128)}, u32[]{:S(2)}) copy-start(f32[8,16]{1,0:T(8,128)} %param.29) | copy-start | bytes 1540
  71.5 18.4 %all-to-all-start.2 = ((f32[64,1,128]{2,1,0:T(1,128)}), f32[64,1,128]{2,1,0:T(1,128)S(1)}, u32[]{:S(2)}, u32[]{:S(2)}) async-start(f32[64,1,128]{2,1,0:T(1,128)} %bitcast.5), calls=%async_computation.2 | async-start | bytes 65536 | tf_op jit(solution)/shard_map/all_to_all | solution.py:635
  91.2 23.5 %all-to-all-start.3 = ((f32[8,152,128]{2,1,0:T(8,128)}), f32[8,152,128]{2,1,0:T(8,128)S(1)}, u32[]{:S(2)}, u32[]{:S(2)}) async-start(f32[8,152,128]{2,1,0:T(8,128)} %get-tuple-element.55), calls=%async_computation.3 | async-start | bytes 1245184 | tf_op jit(solution)/shard_map/all_to_all | solution.py:645
